TPU v7x, 32 devices: a whole 2x2x4 slice. The times are simulated.
32 devices in a mesh: groups: 2 (over y), space: 4 (over z), freq: 2 (over x), band: 2 (over core).
Axes of the slice: x: 2, y: 2, z: 4, core: 2. Of those that a mesh axis runs over, the one named last changes fastest.
Arguments:
- snapshots: bfloat16 [16, 256, 32768], P(('freq', 'band'), None, ('groups', 'space')), parts along dimension 2, may hold values from -6 to 6
- weights: float32 [32768], P(('groups', 'space')), parts along dimension 0, may hold values from 0.25 to 2.5
- triads: int32 [64, 2], replicated, may hold values from 0 to 63, as said below
Outputs:
- bispectra: float32 [128, 512], P(('groups', 'space', 'freq', 'band')), parts along dimension 0
There are 2 independent parts, one for each index of `groups`. A program takes and returns all parts, laid end to end along the dimension named above; an argument that names none is the same for every part. Nothing has to cross between parts.
Inputs may be any that keep to these rules, and one draw needn't show every extreme that they name: `triads`: each row is a pair (k, l) with k >= l and k + l <= 63; all pairs are distinct; the pair (63, 0) is always present.
All inputs are finite; a program needn't handle non-finite values.
Results may differ from a plain program's by a relative error of at most 0.0078.
Values may be sent and summed in bfloat16 or wider, within the bound.
No kernel may reach another device: no remote copies, remote signals or barrier semaphores. Data moves between devices by JAX's collectives and lax.ppermute only.
A program may use at most 128 MiB of HBM per device.

v0:
```python
import functools
import math

import jax
import jax.numpy as jnp
from jax import lax
from jax.experimental import pallas as pl
from jax.experimental.pallas import tpu as pltpu
from jax.sharding import PartitionSpec as P


NB = 16
NF = 64
LANES = 128
PACK = 4
MIB = 1 << 20


def make_table(length):
    row = lax.broadcasted_iota(jnp.int32, (2 * NF, length), 0)
    time = lax.broadcasted_iota(jnp.int32, (2 * NF, length), 1)
    phase = (row % NF * time + row // NF * (length // 4)) % length
    turn = 2.0 * math.pi / length
    window = 0.5 - 0.5 * jnp.cos(time.astype(jnp.float32) * turn)
    gain = 1.0 / math.sqrt(3.0 * length / 8.0)
    return (window * jnp.cos(phase.astype(jnp.float32) * turn) * gain).astype(jnp.bfloat16)


def split_widths(points):
    tiles = points // LANES
    first = max(1, tiles // 4)
    rest = tiles - first - 1
    middle = [(rest + 1) // 2, rest // 2] if rest > 2 else [rest]
    return [w * LANES for w in [first] + [m for m in middle if m > 0] + [1]]


def dft_first_kernel(where_ref, table_ref, *refs):
    table = table_ref[...]
    count = len(refs) // 2
    for source, target in zip(refs[:count], refs[count:]):
        for block in range(source.shape[0]):
            target[block] = jnp.dot(
                table, source[block], preferred_element_type=jnp.float32
            ).astype(jnp.bfloat16)


def dft_first(table, snapshots, where, slots, points, width):
    blocks, length, _ = snapshots.shape
    count = len(slots)

    def column(slot):
        return lambda i, where_ref: (0, 0, where_ref[slot] * (points // width))

    whole = lambda *shape: pl.BlockSpec(shape, lambda i, *_: (0,) * len(shape))
    return pl.pallas_call(
        dft_first_kernel,
        out_shape=[jax.ShapeDtypeStruct((blocks, 2 * NF, width), jnp.bfloat16)] * count,
        grid_spec=pltpu.PrefetchScalarGridSpec(
            num_scalar_prefetch=1,
            grid=(1,),
            in_specs=[whole(2 * NF, length)]
            + [pl.BlockSpec((blocks, length, width), column(slot)) for slot in slots],
            out_specs=[whole(blocks, 2 * NF, width)] * count,
        ),
        compiler_params=pltpu.CompilerParams(vmem_limit_bytes=16 * MIB),
        name="dft_first",
    )(where, table, *([snapshots] * count))


def dft_rest_kernel(plan, points, where_ref, table_ref, snap_ref, after_ref, *outs):
    table = table_ref[...]
    for (slot, offset, width), target in zip(plan, outs):
        step = math.gcd(width, 2 * LANES)
        for piece in range(0, width, step):
            start = pl.multiple_of(where_ref[slot] * points + (offset + piece), LANES)
            target[0, :, piece : piece + step] = jnp.dot(
                table, snap_ref[0, :, pl.ds(start, step)], preferred_element_type=jnp.float32
            ).astype(jnp.bfloat16)


def dft_rest(table, snapshots, where, plan, points, after):
    blocks, length, columns = snapshots.shape
    return pl.pallas_call(
        functools.partial(dft_rest_kernel, plan, points),
        out_shape=[
            jax.ShapeDtypeStruct((blocks, 2 * NF, width), jnp.bfloat16) for _, _, width in plan
        ],
        grid_spec=pltpu.PrefetchScalarGridSpec(
            num_scalar_prefetch=1,
            grid=(blocks,),
            in_specs=[
                pl.BlockSpec((2 * NF, length), lambda i, *_: (0, 0)),
                pl.BlockSpec((1, length, columns), lambda i, *_: (i, 0, 0)),
                pl.BlockSpec(memory_space=pl.ANY),
            ],
            out_specs=[
                pl.BlockSpec((1, 2 * NF, width), lambda i, *_: (i, 0, 0)) for _, _, width in plan
            ],
        ),
        compiler_params=pltpu.CompilerParams(vmem_limit_bytes=16 * MIB),
        cost_estimate=pl.CostEstimate(
            flops=4 * NF * length * columns * blocks,
            bytes_accessed=blocks * columns * (2 * length + 4 * NF),
            transcendentals=0,
        ),
        name="dft_rest",
    )(where, table, snapshots, after)


def triad_kernel(near, offset, has_prior, scale, ids_ref, group_ref, *refs):
    spec_ref = refs[-1]
    out_ref = refs[-2]
    sources = refs[: -3 - has_prior]
    weights_ref = refs[len(sources)]
    prior_ref = refs[len(sources) + 1] if has_prior else None
    blocks, rows, width = sources[-1].shape
    tiles = width // LANES

    for position, source in enumerate(sources):
        base = offset if position < near else 0
        first = group_ref[position] * blocks
        for block in range(blocks):
            for tile in range(tiles):
                lanes = slice(base + tile * LANES, base + (tile + 1) * LANES)
                spec_ref[tile, pl.ds(first + block, rows, stride=NB), :] = source[
                    block, :, lanes
                ].astype(jnp.float32)

    lane = lax.broadcasted_iota(jnp.int32, (NB, LANES), 1)
    lower = lane % (2 * NB) < NB

    def one_pack(group, carry):
        fields = []
        thirds = []
        for member in range(PACK):
            index = (group * PACK + member) * 2
            first = ids_ref[index]
            second = ids_ref[index + 1]
            third = first + second
            field_re, field_im, third_re, third_im = [], [], [], []
            for tile in range(tiles):
                def load(freq, part):
                    start = pl.multiple_of((freq + part * NF) * NB, NB)
                    return spec_ref[tile, pl.ds(start, NB), :]

                lanes = slice(offset + tile * LANES, offset + (tile + 1) * LANES)
                weight = weights_ref[:, lanes]
                first_re, first_im = load(first, 0), load(first, 1)
                second_re, second_im = load(second, 0), load(second, 1)
                field_re.append(weight * (first_re * second_re - first_im * second_im))
                field_im.append(weight * (first_re * second_im + first_im * second_re))
                third_re.append(load(third, 0))
                third_im.append(load(third, 1))
            for parts, rows_of in (
                (field_re, fields), (field_im, fields), (third_re, thirds), (third_im, thirds)
            ):
                rows_of.append(jnp.concatenate(parts, axis=1).astype(jnp.bfloat16))
        product = lax.dot_general(
            jnp.concatenate(fields, axis=0),
            jnp.concatenate(thirds, axis=0),
            (((1,), (1,)), ((), ())),
            preferred_element_type=jnp.float32,
        )
        upper_rows = product[0:NB]
        lower_rows = product[NB : 2 * NB]
        for member in range(1, PACK):
            base = member * 2 * NB
            mine = lane >= base
            upper_rows = jnp.where(mine, product[base : base + NB], upper_rows)
            lower_rows = jnp.where(mine, product[base + NB : base + 2 * NB], lower_rows)
        from_right = pltpu.roll(lower_rows, LANES - NB, 1)
        from_left = pltpu.roll(lower_rows, NB, 1)
        total = (upper_rows + jnp.where(lower, from_right, -from_left)) * scale
        if has_prior:
            total = total + prior_ref[group]
        out_ref[group] = total
        return carry

    lax.fori_loop(0, out_ref.shape[0], one_pack, 0, unroll=4)


def triad_chunk(ids, groups, near_sources, far_sources, weights, offset, prior, scale):
    _, rows, width = far_sources[0].shape
    packs = ids.shape[0] // (2 * PACK)
    vmem = pl.BlockSpec(memory_space=pltpu.VMEM)
    smem = pl.BlockSpec(memory_space=pltpu.SMEM)
    operands = list(near_sources) + list(far_sources) + [weights]
    if prior is not None:
        operands.append(prior)
    return pl.pallas_call(
        functools.partial(
            triad_kernel, len(near_sources), offset, int(prior is not None), scale
        ),
        out_shape=jax.ShapeDtypeStruct((packs, NB, LANES), jnp.float32),
        in_specs=[smem, smem] + [vmem] * len(operands),
        out_specs=vmem,
        scratch_shapes=[pltpu.VMEM((width // LANES, rows * NB, LANES), jnp.float32)],
        compiler_params=pltpu.CompilerParams(vmem_limit_bytes=16 * MIB),
        cost_estimate=pl.CostEstimate(
            flops=packs * 2 * LANES * LANES * width,
            bytes_accessed=NB * rows * width * 2,
            transcendentals=0,
        ),
        name="triads",
    )(ids, groups, *operands)


def mode_decomposition(snapshots, weights, triads):
    length, points = snapshots.shape[1:]
    snapshots = pltpu.with_memory_space_constraint(snapshots, pltpu.HBM)
    freqs, bands = lax.axis_size("freq"), lax.axis_size("band")
    shards = freqs * bands
    own_points = points // shards
    widths = split_widths(own_points)
    offsets = [sum(widths[:i]) for i in range(len(widths))]
    scale = 1.0 / math.sqrt(points * lax.axis_size("space"))
    my_freq, my_band = lax.axis_index("freq"), lax.axis_index("band")
    step = jnp.arange(shards, dtype=jnp.int32)
    step_freq, step_band = step // bands, step % bands
    where = (my_freq + step_freq) % freqs * bands + (my_band + step_band) % bands
    origin = (my_freq + freqs - step_freq) % freqs * bands + (
        my_band + bands - step_band
    ) % bands
    table = make_table(length)
    ids = triads.reshape(-1)
    own_weights = lax.dynamic_slice_in_dim(
        weights, (my_freq * bands + my_band) * own_points, own_points
    ).reshape(1, own_points)

    def send(value, slot):
        if slot == 0:
            return value
        shift_freq, shift_band = divmod(slot, bands)
        pairs = [
            (f * bands + b, (f + shift_freq) % freqs * bands + (b + shift_band) % bands)
            for f in range(freqs)
            for b in range(bands)
        ]
        return lax.ppermute(value, ("freq", "band"), pairs)

    near = list(range(bands))
    far = list(range(bands, shards))
    firsts = dft_first(table, snapshots, where, far, own_points, widths[0])
    far_arrived = [[send(value, slot) for slot, value in zip(far, firsts)]]
    plan = [
        (slot, offset, width)
        for offset, width in list(zip(offsets, widths))[1:]
        for slot in far
    ] + [(slot, 0, own_points) for slot in near]
    rest = dft_rest(table, snapshots, where, plan, own_points, firsts[0])
    for chunk in range(1, len(widths)):
        base = (chunk - 1) * len(far)
        far_arrived.append(
            [send(value, slot) for slot, value in zip(far, rest[base : base + len(far)])]
        )
    near_arrived = [send(value, slot) for slot, value in zip(near, rest[-len(near) :])]

    total = None
    for chunk, offset in enumerate(offsets):
        total = triad_chunk(
            ids, origin, near_arrived, far_arrived[chunk], own_weights, offset, total, scale
        )

    axes = ("space", "freq", "band")
    devices = lax.axis_size("space") * shards
    packs = total.shape[0]
    pieces = lax.all_to_all(total, axes, split_axis=0, concat_axis=0, tiled=True)
    mine = pieces.reshape(devices, packs // devices, NB, LANES).sum(axis=0)
    mine = mine.reshape(packs // devices, NB, PACK, 2, NB).transpose(0, 2, 3, 1, 4)
    return mine.reshape(packs // devices * PACK, 2 * NB * NB)


def solution(mesh):
    return jax.shard_map(
        mode_decomposition,
        mesh=mesh,
        in_specs=(P(("freq", "band"), None, ("groups", "space")), P(("groups", "space")), P()),
        out_specs=P(("groups", "space", "freq", "band"), None),
        check_vma=False,
    )
```

profile of v0, /device:TPU:0, one launch (start us, length us, event | category | flops | bytes accessed | tf_op | source)
XLA Modules:
  0.0 76.0 jit_solution(14926962707347943812)
XLA Ops:
  0.1 0.6 fusion.6.table_ref
  0.7 2.1 %dft_first.1 = (bf16[4,128,256]{2,1,0:T(8,128)(2,1)S(1)}, bf16[4,128,256]{2,1,0:T(8,128)(2,1)S(1)}) custom-call(s32[4]{0:T(128)S(1)} %fusion.8.where_ref, bf16[128,256]{1,0:T(8,128)(2,1)S(1)} %fusion.6.table_ref, bf16[4,256,4096]{2,1,0:T(8,128)(2,1)} %snap_ref.1, bf16[4,256,4096]{2,1,0:T(8,128)(2,1)} %snap_ref.1), custom_call_target="tpu_custom_call" | custom-call | tf_op jit(solution)/shard_map/dft_first/pallas_call | solution.py:55
  2.8 0.0 copy-start.1
  2.8 6.6 %dft_rest.1 = (bf16[4,128,384]{2,1,0:T(8,128)(2,1)}, bf16[4,128,384]{2,1,0:T(8,128)(2,1)}, bf16[4,128,256]{2,1,0:T(8,128)(2,1)}, bf16[4,128,256]{2,1,0:T(8,128)(...) custom-call(s32[4]{0:T(128)S(1)} %fusion.8.where_ref, ...), custom_call_target="tpu_custom_call" | custom-call | flops 1073741824 | bytes 12582912 | tf_op jit(solution)/shard_map/dft_rest/pallas_call | solution.py:83
  9.4 0.0 copy-start
  9.4 0.6 copy-done
  10.0 0.5 collective-permute-start
  10.5 2.5 %collective-permute-start.5 = (bf16[4,128,384]{2,1,0:T(8,128)(2,1)}, bf16[4,128,384]{2,1,0:T(8,128)(2,1)S(1)}, u32[]{:S(2)}, u32[]{:S(2)}) collective-permute-start(bf16[4,128,384]{2,1,0:T(8,128)(2,1)} %get-tuple-element.22), channel_id=1, source_target_pairs={{0,2},{1,3},{2,0},{3,1},{4,6},{5,7},{6,4},{7,5},{8,10},{9,11},{10,... | collective-permute-start | bytes 1179656 | tf_op jit(solution)/shard_map/ppermute | solution.py:239
  13.0 0.0 collective-permute-start.7
  13.0 1.6 %collective-permute-start.8 = (bf16[4,128,256]{2,1,0:T(8,128)(2,1)S(1)}, bf16[4,128,256]{2,1,0:T(8,128)(2,1)S(1)}, u32[]{:S(2)}, u32[]{:S(2)}) collective-permute-start(bf16[4,128,256]{2,1,0:T(8,128)(2,1)S(1)} %get-tuple-element.24), channel_id=1, source_target_pairs={{0,3},{1,2},{2,1},{3,0},{4,7},{5,6},{6,5},{7,4},{8,11},{9,10},{10,... | collective-permute-start | bytes 786440 | tf_op jit(solution)/shard_map/ppermute | solution.py:239
  14.6 0.2 collective-permute-start.6
  14.8 14.0 %collective-permute-done.7.refs_2_ = bf16[4,128,256]{2,1,0:T(8,128)(2,1)S(1)} collective-permute-done((bf16[4,128,256]{2,1,0:T(8,128)(2,1)S(1)}, bf16[4,128,256]{2,1,0:T(8,128)(2,1)S(1)}, u32[]{:S(2)}, u32[]{:S(2)}) %collective-permute-start.7) | collective-permute-done | bytes 262176 | tf_op jit(solution)/shard_map/ppermute | solution.py:239
  28.8 2.0 %collective-permute-start.3 = (bf16[4,128,256]{2,1,0:T(8,128)(2,1)}, bf16[4,128,256]{2,1,0:T(8,128)(2,1)}, u32[]{:S(2)}, u32[]{:S(2)}) collective-permute-start(bf16[4,128,256]{2,1,0:T(8,128)(2,1)} %get-tuple-element.20), channel_id=1, source_target_pairs={{0,2},{1,3},{2,0},{3,1},{4,6},{5,7},{6,4},{7,5},{8,10},{9,11},{10,... | collective-permute-start | bytes 786440 | tf_op jit(solution)/shard_map/ppermute | solution.py:239
  30.8 3.2 %collective-permute-done.8.refs_3_ = bf16[4,128,256]{2,1,0:T(8,128)(2,1)S(1)} collective-permute-done((bf16[4,128,256]{2,1,0:T(8,128)(2,1)S(1)}, bf16[4,128,256]{2,1,0:T(8,128)(2,1)S(1)}, u32[]{:S(2)}, u32[]{:S(2)}) %collective-permute-start.8) | collective-permute-done | bytes 262176 | tf_op jit(solution)/shard_map/ppermute | solution.py:239
  34.0 2.1 %collective-permute-start.4 = (bf16[4,128,256]{2,1,0:T(8,128)(2,1)}, bf16[4,128,256]{2,1,0:T(8,128)(2,1)}, u32[]{:S(2)}, u32[]{:S(2)}) collective-permute-start(bf16[4,128,256]{2,1,0:T(8,128)(2,1)} %get-tuple-element.21), channel_id=1, source_target_pairs={{0,3},{1,2},{2,1},{3,0},{4,7},{5,6},{6,5},{7,4},{8,11},{9,10},{10,... | collective-permute-start | bytes 786440 | tf_op jit(solution)/shard_map/ppermute | solution.py:239
  36.2 0.0 copy-done.1
  36.2 0.7 copy.6
  36.8 0.9 %reshape.15.ids_ref = s32[128]{0:T(128)S(1)} reshape(s32[64,2]{1,0:T(8,128)} %copy.6) | data formatting | bytes 1024 | tf_op jit(solution)/shard_map/reshape | solution.py:225
  37.7 0.7 dynamic_slice.3
  38.4 0.0 collective-permute-done.5.refs_2_
  38.4 0.0 collective-permute-start.1
  38.4 0.0 collective-permute-done.refs_1_
  38.5 0.8 %collective-permute-start.2 = (bf16[4,128,128]{2,1,0:T(8,128)(2,1)S(1)}, bf16[4,128,128]{2,1,0:T(8,128)(2,1)S(1)}, u32[]{:S(2)}, u32[]{:S(2)}) collective-permute-start(bf16[4,128,128]{2,1,0:T(8,128)(2,1)S(1)} %get-tuple-element.19), channel_id=1, source_target_pairs={{0,3},{1,2},{2,1},{3,0},{4,7},{5,6},{6,5},{7,4},{8,11},{9,10},{10,... | collective-permute-start | bytes 393224 | tf_op jit(solution)/shard_map/ppermute | solution.py:239
  39.3 3.0 %triads.4.refs_5_ = f32[16,16,128]{2,1,0:T(8,128)S(1)} custom-call(s32[128]{0:T(128)S(1)} %reshape.15.ids_ref, s32[4]{0:T(128)S(1)} %fusion.7.group_ref, bf16[4,128,1024]{2,1,0:T(8,128)(2,1)S(1)} %get-tuple-element.16.refs_0_, bf16[4,128,1024]{2,1,0:T(8,128)(2,1)S(1)} %collective-permute-done.refs_1_, ...), custom_call_target="tpu_custom_call" | custom-call | flops 134217728 | bytes 1048576 | tf_op jit(solution)/shard_map/triads/pallas_call | solution.py:190
  42.3 0.2 collective-permute-done.6.refs_3_
  42.5 3.7 %triads.5.refs_5_ = f32[16,16,128]{2,1,0:T(8,128)S(1)} custom-call(s32[128]{0:T(128)S(1)} %reshape.15.ids_ref, s32[4]{0:T(128)S(1)} %fusion.7.group_ref, bf16[4,128,1024]{2,1,0:T(8,128)(2,1)S(1)} %get-tuple-element.16.refs_0_, bf16[4,128,1024]{2,1,0:T(8,128)(2,1)S(1)} %collective-permute-done.refs_1_, ...), custom_call_target="tpu_custom_call" | custom-call | flops 201326592 | bytes 1572864 | tf_op jit(solution)/shard_map/triads/pallas_call | solution.py:190
  46.2 2.3 %collective-permute-done.3.refs_2_ = bf16[4,128,256]{2,1,0:T(8,128)(2,1)} collective-permute-done((bf16[4,128,256]{2,1,0:T(8,128)(2,1)}, bf16[4,128,256]{2,1,0:T(8,128)(2,1)}, u32[]{:S(2)}, u32[]{:S(2)}) %collective-permute-start.3) | collective-permute-done | bytes 262176 | tf_op jit(solution)/shard_map/ppermute | solution.py:239
  48.6 5.2 %collective-permute-done.4.refs_3_ = bf16[4,128,256]{2,1,0:T(8,128)(2,1)} collective-permute-done((bf16[4,128,256]{2,1,0:T(8,128)(2,1)}, bf16[4,128,256]{2,1,0:T(8,128)(2,1)}, u32[]{:S(2)}, u32[]{:S(2)}) %collective-permute-start.4) | collective-permute-done | bytes 262176 | tf_op jit(solution)/shard_map/ppermute | solution.py:239
  53.8 3.5 %triads.6.refs_5_ = f32[16,16,128]{2,1,0:T(8,128)S(1)} custom-call(s32[128]{0:T(128)S(1)} %reshape.15.ids_ref, s32[4]{0:T(128)S(1)} %fusion.7.group_ref, bf16[4,128,1024]{2,1,0:T(8,128)(2,1)S(1)} %get-tuple-element.16.refs_0_, bf16[4,128,1024]{2,1,0:T(8,128)(2,1)S(1)} %collective-permute-done.refs_1_, bf16[4,128,256]{2,1,0:T(8,128)(2,1)} %collective-permute-done.3.refs_2_, ...), custom_call_target="tpu_custom_call" | custom-call | flops 134217728 | bytes 1048576 | tf_op jit(solution)/shard_map/triads/pallas_call | solution.py:190
  57.3 0.0 collective-permute-done.1.refs_2_
  57.3 2.0 %collective-permute-done.2.refs_3_ = bf16[4,128,128]{2,1,0:T(8,128)(2,1)S(1)} collective-permute-done((bf16[4,128,128]{2,1,0:T(8,128)(2,1)S(1)}, bf16[4,128,128]{2,1,0:T(8,128)(2,1)S(1)}, u32[]{:S(2)}, u32[]{:S(2)}) %collective-permute-start.2) | collective-permute-done | bytes 131104 | tf_op jit(solution)/shard_map/ppermute | solution.py:239
  59.3 2.2 %triads.7 = f32[16,16,128]{2,1,0:T(8,128)S(1)} custom-call(s32[128]{0:T(128)S(1)} %reshape.15.ids_ref, s32[4]{0:T(128)S(1)} %fusion.7.group_ref, bf16[4,128,1024]{2,1,0:T(8,128)(2,1)S(1)} %get-tuple-element.16.refs_0_, bf16[4,128,1024]{2,1,0:T(8,128)(2,1)S(1)} %collective-permute-done.refs_1_, bf16[4,128,128]{2,1,0:T(8,128)(2,1)S(1)} %collective-permute-done.1.refs_2_, ...), custom_call_target="tpu_custom_call" | custom-call | flops 67108864 | bytes 524288 | tf_op jit(solution)/shard_map/triads/pallas_call | solution.py:190
  61.6 13.6 %all_to_all.5 = f32[16,16,128]{2,1,0:T(8,128)S(1)} all-to-all(f32[16,16,128]{2,1,0:T(8,128)S(1)} %triads.7), channel_id=1, replica_groups=mesh['groups'=2,'space'=4,'freq'=2,'band'=2] {'space','freq','band'}, dimensions={0} | all-to-all | bytes 262144 | tf_op jit(solution)/shard_map/all_to_all | solution.py:267
  75.2 0.1 reshape.17
  75.3 0.7 reshape.18
  (8 shorter events, 0.1 us)
Async XLA Ops:
  2.8 33.4 %copy-start.1 = (s32[64,2]{0,1:T(2,128)S(1)}, s32[64,2]{0,1:T(2,128)}, u32[]{:S(2)}) copy-start(s32[64,2]{0,1:T(2,128)} %param.5) | copy-start | bytes 1540
  9.4 0.6 copy-start
  10.0 28.4 %collective-permute-start = (bf16[4,128,1024]{2,1,0:T(8,128)(2,1)}, bf16[4,128,1024]{2,1,0:T(8,128)(2,1)S(1)}, u32[]{:S(2)}, u32[]{:S(2)}) collective-permute-start(bf16[4,128,1024]{2,1,0:T(8,128)(2,1)} %get-tuple-element.17), channel_id=1, source_target_pairs={{0,1},{1,0},{2,3},{3,2},{4,5},{5,4},{6,7},{7,6},{8,9},{9,8},{10,11... | collective-permute-start | bytes 3145736 | tf_op jit(solution)/shard_map/ppermute | solution.py:239
  10.5 27.9 %collective-permute-start.5 = (bf16[4,128,384]{2,1,0:T(8,128)(2,1)}, bf16[4,128,384]{2,1,0:T(8,128)(2,1)S(1)}, u32[]{:S(2)}, u32[]{:S(2)}) collective-permute-start(bf16[4,128,384]{2,1,0:T(8,128)(2,1)} %get-tuple-element.22), channel_id=1, source_target_pairs={{0,2},{1,3},{2,0},{3,1},{4,6},{5,7},{6,4},{7,5},{8,10},{9,11},{10,... | collective-permute-start | bytes 1179656 | tf_op jit(solution)/shard_map/ppermute | solution.py:239
  13.0 15.8 %collective-permute-start.7 = (bf16[4,128,256]{2,1,0:T(8,128)(2,1)S(1)}, bf16[4,128,256]{2,1,0:T(8,128)(2,1)S(1)}, u32[]{:S(2)}, u32[]{:S(2)}) collective-permute-start(bf16[4,128,256]{2,1,0:T(8,128)(2,1)S(1)} %get-tuple-element.15.after_ref), channel_id=1, source_target_pairs={{0,2},{1,3},{2,0},{3,1},{4,6},{5,7},{6,4},{7,5},{8,10},{9,11},{10,... | collective-permute-start | bytes 786440 | tf_op jit(solution)/shard_map/ppermute | solution.py:239
  13.0 21.0 %collective-permute-start.8 = (bf16[4,128,256]{2,1,0:T(8,128)(2,1)S(1)}, bf16[4,128,256]{2,1,0:T(8,128)(2,1)S(1)}, u32[]{:S(2)}, u32[]{:S(2)}) collective-permute-start(bf16[4,128,256]{2,1,0:T(8,128)(2,1)S(1)} %get-tuple-element.24), channel_id=1, source_target_pairs={{0,3},{1,2},{2,1},{3,0},{4,7},{5,6},{6,5},{7,4},{8,11},{9,10},{10,... | collective-permute-start | bytes 786440 | tf_op jit(solution)/shard_map/ppermute | solution.py:239
  14.6 27.9 %collective-permute-start.6 = (bf16[4,128,384]{2,1,0:T(8,128)(2,1)}, bf16[4,128,384]{2,1,0:T(8,128)(2,1)S(1)}, u32[]{:S(2)}, u32[]{:S(2)}) collective-permute-start(bf16[4,128,384]{2,1,0:T(8,128)(2,1)} %get-tuple-element.23), channel_id=1, source_target_pairs={{0,3},{1,2},{2,1},{3,0},{4,7},{5,6},{6,5},{7,4},{8,11},{9,10},{10,... | collective-permute-start | bytes 1179656 | tf_op jit(solution)/shard_map/ppermute | solution.py:239
  28.8 19.8 %collective-permute-start.3 = (bf16[4,128,256]{2,1,0:T(8,128)(2,1)}, bf16[4,128,256]{2,1,0:T(8,128)(2,1)}, u32[]{:S(2)}, u32[]{:S(2)}) collective-permute-start(bf16[4,128,256]{2,1,0:T(8,128)(2,1)} %get-tuple-element.20), channel_id=1, source_target_pairs={{0,2},{1,3},{2,0},{3,1},{4,6},{5,7},{6,4},{7,5},{8,10},{9,11},{10,... | collective-permute-start | bytes 786440 | tf_op jit(solution)/shard_map/ppermute | solution.py:239
  34.0 19.8 %collective-permute-start.4 = (bf16[4,128,256]{2,1,0:T(8,128)(2,1)}, bf16[4,128,256]{2,1,0:T(8,128)(2,1)}, u32[]{:S(2)}, u32[]{:S(2)}) collective-permute-start(bf16[4,128,256]{2,1,0:T(8,128)(2,1)} %get-tuple-element.21), channel_id=1, source_target_pairs={{0,3},{1,2},{2,1},{3,0},{4,7},{5,6},{6,5},{7,4},{8,11},{9,10},{10,... | collective-permute-start | bytes 786440 | tf_op jit(solution)/shard_map/ppermute | solution.py:239
  38.4 18.9 %collective-permute-start.1 = (bf16[4,128,128]{2,1,0:T(8,128)(2,1)}, bf16[4,128,128]{2,1,0:T(8,128)(2,1)S(1)}, u32[]{:S(2)}, u32[]{:S(2)}) collective-permute-start(bf16[4,128,128]{2,1,0:T(8,128)(2,1)} %copy-done), channel_id=1, source_target_pairs={{0,2},{1,3},{2,0},{3,1},{4,6},{5,7},{6,4},{7,5},{8,10},{9,11},{10,... | collective-permute-start | bytes 393224 | tf_op jit(solution)/shard_map/ppermute | solution.py:239
  38.5 20.9 %collective-permute-start.2 = (bf16[4,128,128]{2,1,0:T(8,128)(2,1)S(1)}, bf16[4,128,128]{2,1,0:T(8,128)(2,1)S(1)}, u32[]{:S(2)}, u32[]{:S(2)}) collective-permute-start(bf16[4,128,128]{2,1,0:T(8,128)(2,1)S(1)} %get-tuple-element.19), channel_id=1, source_target_pairs={{0,3},{1,2},{2,1},{3,0},{4,7},{5,6},{6,5},{7,4},{8,11},{9,10},{10,... | collective-permute-start | bytes 393224 | tf_op jit(solution)/shard_map/ppermute | solution.py:239
where the time goes:
time: 76.3 us; the launch traced here: 76 us
  waiting for transfers between devices  27.1 us (36%)
  Pallas kernels  21.1 us (28%)
  blocking collectives  13.6 us (18%)
  starting transfers between devices  9.7 us (13%)
  local copies, waits for them, and re-layouts  3.77 us (5%)
    ppermute x9, waiting for transfers between devices, send(): return lax.ppermute(value, ('freq', 'band'), pairs)  27.1 us
    all_to_all x1, blocking collectives, mode_decomposition(): lax.all_to_all(total, axes, split_axis=0, concat_axis=0, tiled=True)  13.6 us
    pallas_call x4, Pallas kernels, triad_chunk(): pl.pallas_call(functools.partial(triad_kernel, len(near_sources), offset,...  12.4 us
    ppermute x9, starting transfers between devices, send(): return lax.ppermute(value, ('freq', 'band'), pairs)  9.7 us
    pallas_call x1, Pallas kernels, dft_rest(): pl.pallas_call(functools.partial(dft_rest_kernel, plan, points), out_shap...  6.56 us
    pallas_call x1, Pallas kernels, dft_first(): pl.pallas_call(dft_first_kernel, out_shape=[jax.ShapeDtypeStruct((blocks,...  2.06 us
  transfers between devices with their start and end apart: 9, of which 6 were waited for; matrix products, arithmetic and copies ran while one was open for 3% of the time, Pallas kernels for 13%

commit v1 on v0

v1 whole, which is shorter than its diff:
```python
import functools
import math

import jax
import jax.numpy as jnp
from jax import lax
from jax.experimental import pallas as pl
from jax.experimental.pallas import tpu as pltpu
from jax.sharding import PartitionSpec as P


NB = 16
NF = 64
LANES = 128
PACK = 4
MIB = 1 << 20


VMEM = pl.BlockSpec(memory_space=pltpu.VMEM)
ANY = pl.BlockSpec(memory_space=pl.ANY)


def split_widths(points):
    tiles = points // LANES
    rest = max(0, tiles - 2)
    count = -(-rest // 2)
    middle = [rest // count + (i < rest % count) for i in range(count)] if count else []
    return [w * LANES for w in ([1] if tiles > 1 else []) + middle + [1]]


def make_table(length):
    turn = 2.0 * math.pi / length
    gain = 1.0 / math.sqrt(3.0 * length / 8.0)
    time = lax.broadcasted_iota(jnp.int32, (8, length), 1)
    window = (0.5 - 0.5 * jnp.cos(time.astype(jnp.float32) * turn)) * gain
    row = lax.broadcasted_iota(jnp.int32, (2 * NF, length), 0)
    time = lax.broadcasted_iota(jnp.int32, (2 * NF, length), 1)
    phase = (row & (NF - 1)) * time + jnp.where(row < NF, 0, length // 4)
    phase = phase & (length - 1) if length & (length - 1) == 0 else phase % length
    wave = jnp.cos(phase.astype(jnp.float32) * turn)
    return (jnp.concatenate([window] * (NF // 4), axis=0) * wave).astype(jnp.bfloat16)


def shifted_part(slot, sign, freqs, bands):
    step_freq, step_band = divmod(slot, bands)
    freq = lax.axis_index("freq") + (step_freq if sign > 0 else freqs - step_freq)
    band = lax.axis_index("band") + (step_band if sign > 0 else bands - step_band)
    return lax.rem(freq, freqs) * bands + lax.rem(band, bands)


def dft_far_kernel(sizes, far, points, offset, own_table, *refs):
    count = len(far)
    snap_ref = refs[0]
    outs = refs[len(refs) - 2 - count : len(refs) - 2]
    buffer, arrived = refs[-2:]
    blocks, length, width = buffer.shape[1:]
    copies = []
    for position, slot in enumerate(far):
        start = shifted_part(slot, 1, *sizes) * points + offset
        for block in range(blocks):
            copy = pltpu.make_async_copy(
                snap_ref.at[block, :, pl.ds(pl.multiple_of(start, LANES), width)],
                buffer.at[position, block],
                arrived.at[position, block],
            )
            copy.start()
            copies.append(copy)
    if own_table:
        table_ref = refs[1]
        table_ref[...] = make_table(length)
    else:
        table_ref = refs[1]
    table = table_ref[...]
    for position in range(count):
        for block in range(blocks):
            copies[position * blocks + block].wait()
            outs[position][block] = jnp.dot(
                table, buffer[position, block], preferred_element_type=jnp.float32
            ).astype(jnp.bfloat16)


def dft_far(snapshots, table, sizes, far, points, offset, width):
    blocks, length, _ = snapshots.shape
    count = len(far)
    own_table = table is None
    out_shape = [jax.ShapeDtypeStruct((blocks, 2 * NF, width), jnp.bfloat16)] * count
    if own_table:
        out_shape = [jax.ShapeDtypeStruct((2 * NF, length), jnp.bfloat16)] + out_shape
    return pl.pallas_call(
        functools.partial(dft_far_kernel, sizes, far, points, offset, own_table),
        out_shape=out_shape,
        in_specs=[ANY] + ([] if own_table else [VMEM]),
        out_specs=[VMEM] * len(out_shape),
        scratch_shapes=[
            pltpu.VMEM((count, blocks, length, width), jnp.bfloat16),
            pltpu.SemaphoreType.DMA((count, blocks)),
        ],
        compiler_params=pltpu.CompilerParams(vmem_limit_bytes=8 * MIB),
        name="dft_far",
    )(snapshots, *([] if own_table else [table]))


def dft_rest_kernel(sizes, plan, points, table_ref, snap_ref, after_ref, *outs):
    table = table_ref[...]
    for (slot, offset, width), target in zip(plan, outs):
        step = math.gcd(width, 2 * LANES)
        part = shifted_part(slot, 1, *sizes) * points
        for piece in range(0, width, step):
            start = pl.multiple_of(part + (offset + piece), LANES)
            target[0, :, piece : piece + step] = jnp.dot(
                table, snap_ref[0, :, pl.ds(start, step)], preferred_element_type=jnp.float32
            ).astype(jnp.bfloat16)


def dft_rest(snapshots, table, sizes, plan, points, after):
    blocks, length, columns = snapshots.shape
    return pl.pallas_call(
        functools.partial(dft_rest_kernel, sizes, plan, points),
        out_shape=[
            jax.ShapeDtypeStruct((blocks, 2 * NF, width), jnp.bfloat16) for _, _, width in plan
        ],
        grid=(blocks,),
        in_specs=[
            pl.BlockSpec((2 * NF, length), lambda i: (0, 0)),
            pl.BlockSpec((1, length, columns), lambda i: (i, 0, 0)),
            ANY,
        ],
        out_specs=[pl.BlockSpec((1, 2 * NF, width), lambda i: (i, 0, 0)) for _, _, width in plan],
        compiler_params=pltpu.CompilerParams(vmem_limit_bytes=16 * MIB),
        cost_estimate=pl.CostEstimate(
            flops=4 * NF * length * columns * blocks,
            bytes_accessed=blocks * columns * (2 * length + 4 * NF),
            transcendentals=0,
        ),
        name="dft_rest",
    )(table, snapshots, after)


def interleave(spec_ref, source, slot, sizes, base):
    blocks, rows, _ = source.shape
    first = shifted_part(slot, -1, *sizes) * blocks
    for block in range(blocks):
        for tile in range(spec_ref.shape[0]):
            lanes = slice(base + tile * LANES, base + (tile + 1) * LANES)
            spec_ref[tile, pl.ds(first + block, rows, stride=NB), :] = source[
                block, :, lanes
            ].astype(jnp.float32)


def prepare_kernel(sizes, near, offset, *refs):
    for slot, source in zip(near, refs[:-1]):
        interleave(refs[-1], source, slot, sizes, offset)


def prepare(near_sources, sizes, near, offset, width):
    rows = near_sources[0].shape[1]
    return pl.pallas_call(
        functools.partial(prepare_kernel, sizes, near, offset),
        out_shape=jax.ShapeDtypeStruct((width // LANES, rows * NB, LANES), jnp.float32),
        in_specs=[VMEM] * len(near),
        out_specs=VMEM,
        compiler_params=pltpu.CompilerParams(vmem_limit_bytes=8 * MIB),
        name="prepare",
    )(*near_sources)


def triad_kernel(sizes, slots, offset, prepared, has_prior, scale, *refs):
    ids_any, weights_ref = refs[:2]
    rest = list(refs[2:])
    prior_ref = rest.pop(0) if has_prior else None
    if prepared:
        rest.pop(0)
    sources = [rest.pop(0) for _ in slots]
    out_ref, spec_ref, ids_ref, ids_arrived = rest
    ids_copy = pltpu.make_async_copy(ids_any, ids_ref, ids_arrived)
    ids_copy.start()
    tiles = spec_ref.shape[0]
    own_points = weights_ref.shape[1] // (sizes[0] * sizes[1])
    here = shifted_part(0, 1, *sizes) * own_points + offset

    for (slot, base), source in zip(slots, sources):
        interleave(spec_ref, source, slot, sizes, base)
    weights = [
        weights_ref[:, pl.ds(pl.multiple_of(here + tile * LANES, LANES), LANES)]
        for tile in range(tiles)
    ]
    ids_copy.wait()
    lane = lax.broadcasted_iota(jnp.int32, (NB, LANES), 1)

    def one_pack(group, carry):
        fields = []
        thirds = []
        for member in range(PACK):
            index = (group * PACK + member) * 2
            first = ids_ref[index]
            second = ids_ref[index + 1]
            third = first + second
            field_re, field_im, third_re, third_im, third_neg = [], [], [], [], []
            for tile in range(tiles):
                def load(freq, part):
                    start = pl.multiple_of((freq + part * NF) * NB, NB)
                    return spec_ref[tile, pl.ds(start, NB), :]

                first_re, first_im = load(first, 0), load(first, 1)
                second_re, second_im = load(second, 0), load(second, 1)
                weight = weights[tile]
                field_re.append(weight * (first_re * second_re - first_im * second_im))
                field_im.append(weight * (first_re * second_im + first_im * second_re))
                third_re.append(load(third, 0))
                third_im.append(load(third, 1))
                third_neg.append(-third_re[-1])
            for parts, rows_of in (
                (field_re + field_im, fields),
                (third_re + third_im, thirds),
                (third_im + third_neg, thirds),
            ):
                rows_of.append(jnp.concatenate(parts, axis=1).astype(jnp.bfloat16))
        product = lax.dot_general(
            jnp.concatenate(fields, axis=0),
            jnp.concatenate(thirds, axis=0),
            (((1,), (1,)), ((), ())),
            preferred_element_type=jnp.float32,
        )
        total = product[0:NB]
        for member in range(1, PACK):
            total = jnp.where(
                lane >= member * 2 * NB, product[member * NB : (member + 1) * NB], total
            )
        total = total * scale
        if has_prior:
            total = total + prior_ref[group]
        out_ref[group] = total
        return carry

    lax.fori_loop(0, out_ref.shape[0], one_pack, 0, unroll=4)


def triad_chunk(ids, weights, sources, slots, sizes, offset, width, prior, scale, prepared=None):
    rows = sources[0].shape[1]
    packs = ids.shape[0] // (2 * PACK)
    spec_shape = (width // LANES, rows * NB, LANES)
    operands = [ids, weights] + ([] if prior is None else [prior])
    aliases = {}
    out_shape = [jax.ShapeDtypeStruct((packs, NB, LANES), jnp.float32)]
    scratch = [pltpu.SMEM(ids.shape, jnp.int32), pltpu.SemaphoreType.DMA]
    if prepared is None:
        scratch = [pltpu.VMEM(spec_shape, jnp.float32)] + scratch
    else:
        aliases = {len(operands): 1}
        operands.append(prepared)
        out_shape.append(jax.ShapeDtypeStruct(spec_shape, jnp.float32))
    operands += sources
    return pl.pallas_call(
        functools.partial(
            triad_kernel, sizes, slots, offset, prepared is not None, prior is not None, scale
        ),
        out_shape=out_shape,
        in_specs=[ANY] + [VMEM] * (len(operands) - 1),
        out_specs=[VMEM] * len(out_shape),
        scratch_shapes=scratch,
        input_output_aliases=aliases,
        compiler_params=pltpu.CompilerParams(vmem_limit_bytes=8 * MIB),
        cost_estimate=pl.CostEstimate(
            flops=packs * 2 * LANES * LANES * width,
            bytes_accessed=NB * rows * width * 2,
            transcendentals=0,
        ),
        name="triads",
    )(*operands)[0]


def mode_decomposition(snapshots, weights, triads):
    points = snapshots.shape[2]
    snapshots = pltpu.with_memory_space_constraint(snapshots, pltpu.HBM)
    freqs, bands = sizes = lax.axis_size("freq"), lax.axis_size("band")
    shards = freqs * bands
    own_points = points // shards
    widths = split_widths(own_points)
    offsets = [sum(widths[:i]) for i in range(len(widths))]
    scale = 1.0 / math.sqrt(points * lax.axis_size("space"))
    ids = triads.reshape(-1)
    weights = weights.reshape(1, points)

    def send(value, slot):
        if slot == 0:
            return value
        shift_freq, shift_band = divmod(slot, bands)
        pairs = [
            (f * bands + b, (f + shift_freq) % freqs * bands + (b + shift_band) % bands)
            for f in range(freqs)
            for b in range(bands)
        ]
        return lax.ppermute(value, ("freq", "band"), pairs)

    def send_all(values, slots):
        return [send(value, slot) for slot, value in zip(slots, values)]

    near = list(range(bands))
    far = list(range(bands, shards))
    table, *outs = dft_far(snapshots, None, sizes, far, own_points, 0, widths[0])
    arrived = [send_all(outs, far)]
    outs = dft_far(snapshots, table, sizes, far, own_points, offsets[1], widths[1])
    arrived.append(send_all(outs, far))
    plan = [
        (slot, offset, width)
        for offset, width in list(zip(offsets, widths))[2:]
        for slot in far
    ] + [(slot, 0, own_points) for slot in near]
    rest = dft_rest(snapshots, table, sizes, plan, own_points, outs[0])
    for _ in range(2, len(widths)):
        arrived.append(send_all(rest[: len(far)], far))
        rest = rest[len(far) :]
    near_sources = send_all(rest, near)

    total = None
    for chunk, (offset, width) in enumerate(zip(offsets, widths)):
        slots = [(slot, 0) for slot in far]
        sources = arrived[chunk]
        prepared = None
        if chunk == len(widths) - 1:
            prepared = prepare(near_sources, sizes, near, offset, width)
        else:
            slots = [(slot, offset) for slot in near] + slots
            sources = near_sources + sources
        total = triad_chunk(
            ids, weights, sources, slots, sizes, offset, width, total, scale, prepared
        )

    axes = ("space", "freq", "band")
    devices = lax.axis_size("space") * shards
    packs = total.shape[0]
    pieces = lax.all_to_all(total, axes, split_axis=0, concat_axis=0, tiled=True)
    mine = pieces.reshape(devices, packs // devices, NB, LANES).sum(axis=0)
    mine = mine.reshape(packs // devices, NB, PACK, 2, NB).transpose(0, 2, 3, 1, 4)
    return mine.reshape(packs // devices * PACK, 2 * NB * NB)


def solution(mesh):
    return jax.shard_map(
        mode_decomposition,
        mesh=mesh,
        in_specs=(P(("freq", "band"), None, ("groups", "space")), P(("groups", "space")), P()),
        out_specs=P(("groups", "space", "freq", "band"), None),
        check_vma=False,
    )
```

time: 76.3 us -> 77.2 us (1.012)
  waiting for transfers between devices: 27.1 us -> 23.4 us
  starting transfers between devices: 9.7 us -> 11.8 us
  local copies, waits for them, and re-layouts: 3.77 us -> 5.84 us
    ppermute x9 -> x11, waiting for transfers between devices: 27.1 us -> 23.4 us  [send(): return lax.ppermute(value, ('freq', 'band'), pairs)]
    unnamed x5 -> x9, local copies, waits for them, and re-layouts: 1.35 us -> 3.59 us
    ppermute x9 -> x11, starting transfers between devices: 9.7 us -> 11.8 us  [send(): return lax.ppermute(value, ('freq', 'band'), pairs)]
    pallas_call x6 -> x9, Pallas kernels: 21.1 us -> 21.7 us  [the longest x5 11.3 us: triad_chunk(): pl.pallas_call(functools.partial(triad_kernel, sizes, slots, offset, prep...]
  transfers between devices with their start and end apart: 9 -> 11, of which waited for: 6 -> 5; matrix products, arithmetic and copies ran while one was open for 3% -> 4% of each run, Pallas kernels for 13% -> 12%
where the time goes in v1:
time: 77.2 us; the launch traced here: 76.8 us
  waiting for transfers between devices  23.4 us (30%)
  Pallas kernels  21.7 us (28%)
  blocking collectives  13.9 us (18%)
  starting transfers between devices  11.8 us (15%)
  local copies, waits for them, and re-layouts  5.84 us (8%)
    ppermute x11, waiting for transfers between devices, send(): return lax.ppermute(value, ('freq', 'band'), pairs)  23.4 us
    all_to_all x1, blocking collectives, mode_decomposition(): lax.all_to_all(total, axes, split_axis=0, concat_axis=0, tiled=True)  13.9 us
    ppermute x11, starting transfers between devices, send(): return lax.ppermute(value, ('freq', 'band'), pairs)  11.8 us
    pallas_call x5, Pallas kernels, triad_chunk(): pl.pallas_call(functools.partial(triad_kernel, sizes, slots, offset, prep...  11.3 us
    pallas_call x1, Pallas kernels, dft_rest(): pl.pallas_call(functools.partial(dft_rest_kernel, sizes, plan, points), o...  5.5 us
    pallas_call x2, Pallas kernels, dft_far(): pl.pallas_call(functools.partial(dft_far_kernel, sizes, far, points, offs...  4.72 us
    unnamed x9, local copies, waits for them, and re-layouts  3.59 us
  transfers between devices with their start and end apart: 11, of which 5 were waited for; matrix products, arithmetic and copies ran while one was open for 4% of the time, Pallas kernels for 12%

profile of v1, /device:TPU:0, one launch (start us, length us, event | category | flops | bytes accessed | tf_op | source)
XLA Modules:
  0.0 76.8 jit_solution(16318412354227896164)
XLA Ops:
  0.0 2.3 %dft_far.2 = (bf16[128,256]{1,0:T(8,128)(2,1)S(1)}, bf16[4,128,128]{2,1,0:T(8,128)(2,1)S(1)}, bf16[4,128,128]{2,1,0:T(8,128)(2,1)S(1)}) custom-call(bf16[4,256,4096]{2,1,0:T(8,128)(2,1)} %snap_ref.1), custom_call_target="tpu_custom_call" | custom-call | tf_op jit(solution)/shard_map/dft_far/pallas_call | solution.py:89
  2.3 0.0 copy-start
  2.3 2.5 %dft_far.3 = (bf16[4,128,256]{2,1,0:T(8,128)(2,1)S(1)}, bf16[4,128,256]{2,1,0:T(8,128)(2,1)S(1)}) custom-call(bf16[4,256,4096]{2,1,0:T(8,128)(2,1)} %snap_ref.1, bf16[128,256]{1,0:T(8,128)(2,1)S(1)} %get-tuple-element.19.refs_1_.table_ref), custom_call_target="tpu_custom_call" | custom-call | tf_op jit(solution)/shard_map/dft_far/pallas_call | solution.py:89
  4.7 5.5 %dft_rest.1 = (bf16[4,128,256]{2,1,0:T(8,128)(2,1)S(1)}, bf16[4,128,256]{2,1,0:T(8,128)(2,1)}, bf16[4,128,256]{2,1,0:T(8,128)(2,1)}, bf16[4,128,256]{2,1,0:T(8,1...) custom-call(bf16[128,256]{1,0:T(8,128)(2,1)S(1)} %get-tuple-element., ...), custom_call_target="tpu_custom_call" | custom-call | flops 1073741824 | bytes 12582912 | tf_op jit(solution)/shard_map/dft_rest/pallas_call | solution.py:117
  10.2 0.5 collective-permute-start
  10.8 2.6 %collective-permute-start.3 = (bf16[4,128,256]{2,1,0:T(8,128)(2,1)S(1)}, bf16[4,128,256]{2,1,0:T(8,128)(2,1)S(1)}, u32[]{:S(2)}, u32[]{:S(2)}) collective-permute-start(bf16[4,128,256]{2,1,0:T(8,128)(2,1)S(1)} %get-tuple-element.20.after_ref), channel_id=1, source_target_pairs={{0,2},{1,3},{2,0},{3,1},{4,6},{5,7},{6,4},{7,5},{8,10},{9,11},{10,... | collective-permute-start | bytes 786440 | tf_op jit(solution)/shard_map/ppermute | solution.py:293
  13.3 0.0 collective-permute-start.4
  13.4 1.7 %collective-permute-start.1 = (bf16[4,128,128]{2,1,0:T(8,128)(2,1)S(1)}, bf16[4,128,128]{2,1,0:T(8,128)(2,1)S(1)}, u32[]{:S(2)}, u32[]{:S(2)}) collective-permute-start(bf16[4,128,128]{2,1,0:T(8,128)(2,1)S(1)} %get-tuple-element.23), channel_id=1, source_target_pairs={{0,2},{1,3},{2,0},{3,1},{4,6},{5,7},{6,4},{7,5},{8,10},{9,11},{10,... | collective-permute-start | bytes 393224 | tf_op jit(solution)/shard_map/ppermute | solution.py:293
  15.1 0.0 collective-permute-start.2
  15.1 13.8 %collective-permute-done.1.refs_4_ = bf16[4,128,128]{2,1,0:T(8,128)(2,1)S(1)} collective-permute-done((bf16[4,128,128]{2,1,0:T(8,128)(2,1)S(1)}, bf16[4,128,128]{2,1,0:T(8,128)(2,1)S(1)}, u32[]{:S(2)}, u32[]{:S(2)}) %collective-permute-start.1) | collective-permute-done | bytes 131104 | tf_op jit(solution)/shard_map/ppermute | solution.py:293
  28.9 2.0 %collective-permute-start.5 = (bf16[4,128,256]{2,1,0:T(8,128)(2,1)S(1)}, bf16[4,128,256]{2,1,0:T(8,128)(2,1)S(1)}, u32[]{:S(2)}, u32[]{:S(2)}) collective-permute-start(bf16[4,128,256]{2,1,0:T(8,128)(2,1)S(1)} %get-tuple-element.26), channel_id=1, source_target_pairs={{0,2},{1,3},{2,0},{3,1},{4,6},{5,7},{6,4},{7,5},{8,10},{9,11},{10,... | collective-permute-start | bytes 786440 | tf_op jit(solution)/shard_map/ppermute | solution.py:293
  30.9 0.3 collective-permute-done.2.refs_5_
  31.3 0.0 copy-start.1
  31.3 0.6 copy-done.1
  31.9 1.9 %collective-permute-start.6 = (bf16[4,128,256]{2,1,0:T(8,128)(2,1)}, bf16[4,128,256]{2,1,0:T(8,128)(2,1)S(1)}, u32[]{:S(2)}, u32[]{:S(2)}) collective-permute-start(bf16[4,128,256]{2,1,0:T(8,128)(2,1)} %get-tuple-element.27), channel_id=1, source_target_pairs={{0,3},{1,2},{2,1},{3,0},{4,7},{5,6},{6,5},{7,4},{8,11},{9,10},{10,... | collective-permute-start | bytes 786440 | tf_op jit(solution)/shard_map/ppermute | solution.py:293
  33.8 0.0 collective-permute-done.3.refs_5_
  33.8 0.0 collective-permute-start.7
  33.8 0.0 collective-permute-done.4.refs_6_
  33.8 1.0 %collective-permute-start.8 = (bf16[4,128,256]{2,1,0:T(8,128)(2,1)}, bf16[4,128,256]{2,1,0:T(8,128)(2,1)}, u32[]{:S(2)}, u32[]{:S(2)}) collective-permute-start(bf16[4,128,256]{2,1,0:T(8,128)(2,1)} %get-tuple-element.29), channel_id=1, source_target_pairs={{0,3},{1,2},{2,1},{3,0},{4,7},{5,6},{6,5},{7,4},{8,11},{9,10},{10,... | collective-permute-start | bytes 786440 | tf_op jit(solution)/shard_map/ppermute | solution.py:293
  34.8 3.3 %collective-permute-done.5.refs_5_ = bf16[4,128,256]{2,1,0:T(8,128)(2,1)S(1)} collective-permute-done((bf16[4,128,256]{2,1,0:T(8,128)(2,1)S(1)}, bf16[4,128,256]{2,1,0:T(8,128)(2,1)S(1)}, u32[]{:S(2)}, u32[]{:S(2)}) %collective-permute-start.5) | collective-permute-done | bytes 262176 | tf_op jit(solution)/shard_map/ppermute | solution.py:293
  38.1 0.0 collective-permute-start.10
  38.1 0.0 collective-permute-done.refs_3_.refs_4_.refs_1_
  38.1 2.0 %collective-permute-start.9 = (bf16[4,128,128]{2,1,0:T(8,128)(2,1)}, bf16[4,128,128]{2,1,0:T(8,128)(2,1)}, u32[]{:S(2)}, u32[]{:S(2)}) collective-permute-start(bf16[4,128,128]{2,1,0:T(8,128)(2,1)} %get-tuple-element.30), channel_id=1, source_target_pairs={{0,2},{1,3},{2,0},{3,1},{4,6},{5,7},{6,4},{7,5},{8,10},{9,11},{10,... | collective-permute-start | bytes 393224 | tf_op jit(solution)/shard_map/ppermute | solution.py:293
  40.1 1.4 %copy.7 = s32[64,2]{1,0:T(8,128)} copy(s32[64,2]{0,1:T(2,128)} %param.5) | data formatting | bytes 1024 | tf_op args[2]
  41.5 1.4 %reshape.15.refs_0_ = s32[128]{0:T(128)} reshape(s32[64,2]{1,0:T(8,128)} %copy.7) | data formatting | bytes 1024 | tf_op jit(solution)/shard_map/reshape | solution.py:281
  42.9 0.2 prepare.1.refs_3_
  43.1 0.0 copy-done
  43.1 0.0 copy-start.2
  43.1 0.9 %copy-done.2 = bf16[4,128,128]{2,1,0:T(8,128)(2,1)S(1)} copy-done((bf16[4,128,128]{2,1,0:T(8,128)(2,1)S(1)}, bf16[4,128,128]{2,1,0:T(8,128)(2,1)}, u32[]{:S(2)}) %copy-start.2) | copy-done | bytes 131096
  44.0 0.0 copy-start.3
  44.0 0.7 copy-done.3
  44.7 1.4 %triads.5.refs_2_ = f32[16,16,128]{2,1,0:T(8,128)S(1)} custom-call(s32[128]{0:T(128)S(1)} %copy-done.3, f32[1,4096]{1,0:T(1,128)S(1)} %bitcast.4, bf16[4,128,1024]{2,1,0:T(8,128)(2,1)S(1)} %get-tuple-element.21.refs_2_.refs_3_.refs_0_, bf16[4,128,1024]{2,1,0:T(8,128)(2,1)S(1)} %collective-permute-done.refs_3_.refs_4_.refs_1_, ...), custom_call_target="tpu_custom_call" | custom-call | flops 67108864 | bytes 524288 | tf_op jit(solution)/shard_map/triads/pallas_call | solution.py:253
  46.1 2.2 %triads.6.refs_2_ = f32[16,16,128]{2,1,0:T(8,128)S(1)} custom-call(s32[128]{0:T(128)S(1)} %copy-done.3, f32[1,4096]{1,0:T(1,128)S(1)} %bitcast.5, f32[16,16,128]{2,1,0:T(8,128)S(1)} %triads.5.refs_2_, bf16[4,128,1024]{2,1,0:T(8,128)(2,1)S(1)} %get-tuple-element.21.refs_2_.refs_3_.refs_0_, ...), custom_call_target="tpu_custom_call" | custom-call | flops 134217728 | bytes 1048576 | tf_op jit(solution)/shard_map/triads/pallas_call | solution.py:253
  48.3 0.0 collective-permute-done.6.refs_6_
  48.3 2.2 %triads.7.refs_2_ = f32[16,16,128]{2,1,0:T(8,128)S(1)} custom-call(s32[128]{0:T(128)S(1)} %copy-done.3, f32[1,4096]{1,0:T(1,128)S(1)} %bitcast.6, f32[16,16,128]{2,1,0:T(8,128)S(1)} %triads.6.refs_2_, bf16[4,128,1024]{2,1,0:T(8,128)(2,1)S(1)} %get-tuple-element.21.refs_2_.refs_3_.refs_0_, ...), custom_call_target="tpu_custom_call" | custom-call | flops 134217728 | bytes 1048576 | tf_op jit(solution)/shard_map/triads/pallas_call | solution.py:253
  50.5 0.0 collective-permute-done.7.refs_5_
  50.6 4.0 %collective-permute-done.8.refs_6_ = bf16[4,128,256]{2,1,0:T(8,128)(2,1)} collective-permute-done((bf16[4,128,256]{2,1,0:T(8,128)(2,1)}, bf16[4,128,256]{2,1,0:T(8,128)(2,1)}, u32[]{:S(2)}, u32[]{:S(2)}) %collective-permute-start.8) | collective-permute-done | bytes 262176 | tf_op jit(solution)/shard_map/ppermute | solution.py:293
  54.6 3.1 %triads.8.refs_2_ = f32[16,16,128]{2,1,0:T(8,128)S(1)} custom-call(s32[128]{0:T(128)S(1)} %copy-done.3, f32[1,4096]{1,0:T(1,128)S(1)} %bitcast.7, f32[16,16,128]{2,1,0:T(8,128)S(1)} %triads.7.refs_2_, bf16[4,128,1024]{2,1,0:T(8,128)(2,1)S(1)} %get-tuple-element.21.refs_2_.refs_3_.refs_0_, ...), custom_call_target="tpu_custom_call" | custom-call | flops 134217728 | bytes 1048576 | tf_op jit(solution)/shard_map/triads/pallas_call | solution.py:253
  57.7 0.0 collective-permute-done.10.refs_5_
  57.7 1.9 %collective-permute-done.9.refs_4_ = bf16[4,128,128]{2,1,0:T(8,128)(2,1)} collective-permute-done((bf16[4,128,128]{2,1,0:T(8,128)(2,1)}, bf16[4,128,128]{2,1,0:T(8,128)(2,1)}, u32[]{:S(2)}, u32[]{:S(2)}) %collective-permute-start.9) | collective-permute-done | bytes 131104 | tf_op jit(solution)/shard_map/ppermute | solution.py:293
  59.7 2.4 %triads.9 = (f32[16,16,128]{2,1,0:T(8,128)S(1)}, f32[1,2048,128]{2,1,0:T(8,128)S(1)}) custom-call(s32[128]{0:T(128)S(1)} %copy-done.3, f32[1,4096]{1,0:T(1,128)S(1)} %bitcast.8, f32[16,16,128]{2,1,0:T(8,128)S(1)} %triads.8.refs_2_, f32[1,2048,128]{2,1,0:T(8,128)S(1)} %prepare.1.refs_3_, ...), custom_call_target="tpu_custom_call", output_to_operand_aliasing={{1}: (3, {})} | custom-call | flops 67108864 | bytes 524288 | tf_op jit(solution)/shard_map/triads/pallas_call | solution.py:253
  62.0 13.9 %all_to_all.5 = f32[16,16,128]{2,1,0:T(8,128)S(1)} all-to-all(f32[16,16,128]{2,1,0:T(8,128)S(1)} %get-tuple-element.32), channel_id=1, replica_groups=mesh['groups'=2,'space'=4,'freq'=2,'band'=2] {'space','freq','band'}, dimensions={0} | all-to-all | bytes 262144 | tf_op jit(solution)/shard_map/all_to_all | solution.py:332
  75.9 0.1 reshape.17
  76.1 0.7 reshape.18
  (2 shorter events, 0.0 us)
Async XLA Ops:
  2.3 40.8 %copy-start = (f32[4096]{0:T(1024)S(1)}, f32[4096]{0:T(1024)}, u32[]{:S(2)}) copy-start(f32[4096]{0:T(1024)} %param.4) | copy-start | bytes 49156
  10.2 27.8 %collective-permute-start = (bf16[4,128,1024]{2,1,0:T(8,128)(2,1)S(1)}, bf16[4,128,1024]{2,1,0:T(8,128)(2,1)S(1)}, u32[]{:S(2)}, u32[]{:S(2)}) collective-permute-start(bf16[4,128,1024]{2,1,0:T(8,128)(2,1)S(1)} %get-tuple-element.22), channel_id=1, source_target_pairs={{0,1},{1,0},{2,3},{3,2},{4,5},{5,4},{6,7},{7,6},{8,9},{9,8},{10,11... | collective-permute-start | bytes 3145736 | tf_op jit(solution)/shard_map/ppermute | solution.py:293
  10.8 23.1 %collective-permute-start.3 = (bf16[4,128,256]{2,1,0:T(8,128)(2,1)S(1)}, bf16[4,128,256]{2,1,0:T(8,128)(2,1)S(1)}, u32[]{:S(2)}, u32[]{:S(2)}) collective-permute-start(bf16[4,128,256]{2,1,0:T(8,128)(2,1)S(1)} %get-tuple-element.20.after_ref), channel_id=1, source_target_pairs={{0,2},{1,3},{2,0},{3,1},{4,6},{5,7},{6,4},{7,5},{8,10},{9,11},{10,... | collective-permute-start | bytes 786440 | tf_op jit(solution)/shard_map/ppermute | solution.py:293
  13.3 20.5 %collective-permute-start.4 = (bf16[4,128,256]{2,1,0:T(8,128)(2,1)S(1)}, bf16[4,128,256]{2,1,0:T(8,128)(2,1)S(1)}, u32[]{:S(2)}, u32[]{:S(2)}) collective-permute-start(bf16[4,128,256]{2,1,0:T(8,128)(2,1)S(1)} %get-tuple-element.25), channel_id=1, source_target_pairs={{0,3},{1,2},{2,1},{3,0},{4,7},{5,6},{6,5},{7,4},{8,11},{9,10},{10,... | collective-permute-start | bytes 786440 | tf_op jit(solution)/shard_map/ppermute | solution.py:293
  13.4 15.5 %collective-permute-start.1 = (bf16[4,128,128]{2,1,0:T(8,128)(2,1)S(1)}, bf16[4,128,128]{2,1,0:T(8,128)(2,1)S(1)}, u32[]{:S(2)}, u32[]{:S(2)}) collective-permute-start(bf16[4,128,128]{2,1,0:T(8,128)(2,1)S(1)} %get-tuple-element.23), channel_id=1, source_target_pairs={{0,2},{1,3},{2,0},{3,1},{4,6},{5,7},{6,4},{7,5},{8,10},{9,11},{10,... | collective-permute-start | bytes 393224 | tf_op jit(solution)/shard_map/ppermute | solution.py:293
  15.1 16.2 %collective-permute-start.2 = (bf16[4,128,128]{2,1,0:T(8,128)(2,1)S(1)}, bf16[4,128,128]{2,1,0:T(8,128)(2,1)S(1)}, u32[]{:S(2)}, u32[]{:S(2)}) collective-permute-start(bf16[4,128,128]{2,1,0:T(8,128)(2,1)S(1)} %get-tuple-element.24), channel_id=1, source_target_pairs={{0,3},{1,2},{2,1},{3,0},{4,7},{5,6},{6,5},{7,4},{8,11},{9,10},{10,... | collective-permute-start | bytes 393224 | tf_op jit(solution)/shard_map/ppermute | solution.py:293
  28.9 9.2 %collective-permute-start.5 = (bf16[4,128,256]{2,1,0:T(8,128)(2,1)S(1)}, bf16[4,128,256]{2,1,0:T(8,128)(2,1)S(1)}, u32[]{:S(2)}, u32[]{:S(2)}) collective-permute-start(bf16[4,128,256]{2,1,0:T(8,128)(2,1)S(1)} %get-tuple-element.26), channel_id=1, source_target_pairs={{0,2},{1,3},{2,0},{3,1},{4,6},{5,7},{6,4},{7,5},{8,10},{9,11},{10,... | collective-permute-start | bytes 786440 | tf_op jit(solution)/shard_map/ppermute | solution.py:293
  31.3 0.6 copy-start.1
  31.9 16.4 %collective-permute-start.6 = (bf16[4,128,256]{2,1,0:T(8,128)(2,1)}, bf16[4,128,256]{2,1,0:T(8,128)(2,1)S(1)}, u32[]{:S(2)}, u32[]{:S(2)}) collective-permute-start(bf16[4,128,256]{2,1,0:T(8,128)(2,1)} %get-tuple-element.27), channel_id=1, source_target_pairs={{0,3},{1,2},{2,1},{3,0},{4,7},{5,6},{6,5},{7,4},{8,11},{9,10},{10,... | collective-permute-start | bytes 786440 | tf_op jit(solution)/shard_map/ppermute | solution.py:293
  33.8 16.7 %collective-permute-start.7 = (bf16[4,128,256]{2,1,0:T(8,128)(2,1)}, bf16[4,128,256]{2,1,0:T(8,128)(2,1)S(1)}, u32[]{:S(2)}, u32[]{:S(2)}) collective-permute-start(bf16[4,128,256]{2,1,0:T(8,128)(2,1)} %get-tuple-element.28), channel_id=1, source_target_pairs={{0,2},{1,3},{2,0},{3,1},{4,6},{5,7},{6,4},{7,5},{8,10},{9,11},{10,... | collective-permute-start | bytes 786440 | tf_op jit(solution)/shard_map/ppermute | solution.py:293
  33.8 20.8 %collective-permute-start.8 = (bf16[4,128,256]{2,1,0:T(8,128)(2,1)}, bf16[4,128,256]{2,1,0:T(8,128)(2,1)}, u32[]{:S(2)}, u32[]{:S(2)}) collective-permute-start(bf16[4,128,256]{2,1,0:T(8,128)(2,1)} %get-tuple-element.29), channel_id=1, source_target_pairs={{0,3},{1,2},{2,1},{3,0},{4,7},{5,6},{6,5},{7,4},{8,11},{9,10},{10,... | collective-permute-start | bytes 786440 | tf_op jit(solution)/shard_map/ppermute | solution.py:293
  38.1 19.6 %collective-permute-start.10 = (bf16[4,128,128]{2,1,0:T(8,128)(2,1)}, bf16[4,128,128]{2,1,0:T(8,128)(2,1)}, u32[]{:S(2)}, u32[]{:S(2)}) collective-permute-start(bf16[4,128,128]{2,1,0:T(8,128)(2,1)} %get-tuple-element.31), channel_id=1, source_target_pairs={{0,3},{1,2},{2,1},{3,0},{4,7},{5,6},{6,5},{7,4},{8,11},{9,10},{10,... | collective-permute-start | bytes 393224 | tf_op jit(solution)/shard_map/ppermute | solution.py:293
  38.1 21.6 %collective-permute-start.9 = (bf16[4,128,128]{2,1,0:T(8,128)(2,1)}, bf16[4,128,128]{2,1,0:T(8,128)(2,1)}, u32[]{:S(2)}, u32[]{:S(2)}) collective-permute-start(bf16[4,128,128]{2,1,0:T(8,128)(2,1)} %get-tuple-element.30), channel_id=1, source_target_pairs={{0,2},{1,3},{2,0},{3,1},{4,6},{5,7},{6,4},{7,5},{8,10},{9,11},{10,... | collective-permute-start | bytes 393224 | tf_op jit(solution)/shard_map/ppermute | solution.py:293
  43.1 0.9 %copy-start.2 = (bf16[4,128,128]{2,1,0:T(8,128)(2,1)S(1)}, bf16[4,128,128]{2,1,0:T(8,128)(2,1)}, u32[]{:S(2)}) copy-start(bf16[4,128,128]{2,1,0:T(8,128)(2,1)} %copy-done.1) | copy-start | bytes 393220
  44.0 0.7 copy-start.3

commit v2 on v1

--- a/solution.py
+++ b/solution.py
@@ -22,22 +22,37 @@
 
 def split_widths(points):
     tiles = points // LANES
-    rest = max(0, tiles - 2)
-    count = -(-rest // 2)
-    middle = [rest // count + (i < rest % count) for i in range(count)] if count else []
-    return [w * LANES for w in ([1] if tiles > 1 else []) + middle + [1]]
+    first = max(1, tiles // 4)
+    rest = tiles - first - 1
+    count = max(1, -(-rest // 3))
+    middle = [rest // count + (i < rest % count) for i in range(count)]
+    return [w * LANES for w in [first] + middle + [1]]
 
 
 def make_table(length):
     turn = 2.0 * math.pi / length
     gain = 1.0 / math.sqrt(3.0 * length / 8.0)
+    quarter = length // 4
+
+    def cosine(phase):
+        moved = phase + quarter // 2
+        quadrant = lax.div(moved, quarter) & 3
+        angle = (lax.rem(moved, quarter) - quarter // 2).astype(jnp.float32) * turn
+        square = angle * angle
+        even = 1.0 + square * (
+            -1 / 2 + square * (1 / 24 + square * (-1 / 720 + square * (1 / 40320)))
+        )
+        odd = angle * (
+            1.0 + square * (-1 / 6 + square * (1 / 120 + square * (-1 / 5040 + square / 362880)))
+        )
+        value = jnp.where(quadrant & 1 == 0, even, odd)
+        return jnp.where((quadrant == 1) | (quadrant == 2), -value, value)
+
     time = lax.broadcasted_iota(jnp.int32, (8, length), 1)
-    window = (0.5 - 0.5 * jnp.cos(time.astype(jnp.float32) * turn)) * gain
+    window = (0.5 - 0.5 * cosine(time)) * gain
     row = lax.broadcasted_iota(jnp.int32, (2 * NF, length), 0)
     time = lax.broadcasted_iota(jnp.int32, (2 * NF, length), 1)
-    phase = (row & (NF - 1)) * time + jnp.where(row < NF, 0, length // 4)
-    phase = phase & (length - 1) if length & (length - 1) == 0 else phase % length
-    wave = jnp.cos(phase.astype(jnp.float32) * turn)
+    wave = cosine((row & (NF - 1)) * time + jnp.where(row < NF, 0, quarter))
     return (jnp.concatenate([window] * (NF // 4), axis=0) * wave).astype(jnp.bfloat16)
 
 
@@ -83,9 +98,9 @@
     blocks, length, _ = snapshots.shape
     count = len(far)
     own_table = table is None
-    out_shape = [jax.ShapeDtypeStruct((blocks, 2 * NF, width), jnp.bfloat16)] * count
+    out_shape = [pltpu.VMEM((blocks, 2 * NF, width), jnp.bfloat16)] * count
     if own_table:
-        out_shape = [jax.ShapeDtypeStruct((2 * NF, length), jnp.bfloat16)] + out_shape
+        out_shape = [pltpu.VMEM((2 * NF, length), jnp.bfloat16)] + out_shape
     return pl.pallas_call(
         functools.partial(dft_far_kernel, sizes, far, points, offset, own_table),
         out_shape=out_shape,
@@ -191,9 +206,8 @@
         fields = []
         thirds = []
         for member in range(PACK):
-            index = (group * PACK + member) * 2
-            first = ids_ref[index]
-            second = ids_ref[index + 1]
+            first = ids_ref[0, group * PACK + member]
+            second = ids_ref[1, group * PACK + member]
             third = first + second
             field_re, field_im, third_re, third_im, third_neg = [], [], [], [], []
             for tile in range(tiles):
@@ -237,7 +251,7 @@
 
 def triad_chunk(ids, weights, sources, slots, sizes, offset, width, prior, scale, prepared=None):
     rows = sources[0].shape[1]
-    packs = ids.shape[0] // (2 * PACK)
+    packs = ids.shape[1] // PACK
     spec_shape = (width // LANES, rows * NB, LANES)
     operands = [ids, weights] + ([] if prior is None else [prior])
     aliases = {}
@@ -249,7 +263,7 @@
         aliases = {len(operands): 1}
         operands.append(prepared)
         out_shape.append(jax.ShapeDtypeStruct(spec_shape, jnp.float32))
-    operands += sources
+    operands += [pltpu.with_memory_space_constraint(x, pltpu.VMEM) for x in sources]
     return pl.pallas_call(
         functools.partial(
             triad_kernel, sizes, slots, offset, prepared is not None, prior is not None, scale
@@ -278,7 +292,7 @@
     widths = split_widths(own_points)
     offsets = [sum(widths[:i]) for i in range(len(widths))]
     scale = 1.0 / math.sqrt(points * lax.axis_size("space"))
-    ids = triads.reshape(-1)
+    ids = triads.T
     weights = weights.reshape(1, points)
 
     def send(value, slot):

time: 77.2 us -> 75 us (0.972)
  waiting for transfers between devices: 23.4 us -> 30.5 us
  local copies, waits for them, and re-layouts: 5.84 us -> 0.85 us
  Pallas kernels: 21.7 us -> 18.7 us
    ppermute x11 -> x9, waiting for transfers between devices: 23.4 us -> 30.5 us  [send(): return lax.ppermute(value, ('freq', 'band'), pairs)]
    unnamed x9 -> x4, local copies, waits for them, and re-layouts: 3.59 us -> 0.01 us
    pallas_call x5 -> x4, Pallas kernels: 11.3 us -> 8.75 us  [triad_chunk(): pl.pallas_call(functools.partial(triad_kernel, sizes, slots, offset, prep...]
    reshape x1 -> x0, local copies, waits for them, and re-layouts: 1.41 us -> none  [mode_decomposition(): ids = triads.reshape(-1)]
    ppermute x11 -> x9, starting transfers between devices: 11.8 us -> 11.1 us  [send(): return lax.ppermute(value, ('freq', 'band'), pairs)]
  transfers between devices with their start and end apart: 11 -> 9, of which waited for: 5 -> 8; matrix products, arithmetic and copies ran while one was open for 4% -> 0% of each run, Pallas kernels for 12% -> 10%
where the time goes in v2:
time: 75 us; the launch traced here: 74.8 us
  waiting for transfers between devices  30.5 us (41%)
  Pallas kernels  18.7 us (25%)
  blocking collectives  13.6 us (18%)
  starting transfers between devices  11.1 us (15%)
  local copies, waits for them, and re-layouts  0.85 us (1%)
    ppermute x9, waiting for transfers between devices, send(): return lax.ppermute(value, ('freq', 'band'), pairs)  30.5 us
    all_to_all x1, blocking collectives, mode_decomposition(): lax.all_to_all(total, axes, split_axis=0, concat_axis=0, tiled=True)  13.6 us
    ppermute x9, starting transfers between devices, send(): return lax.ppermute(value, ('freq', 'band'), pairs)  11.1 us
    pallas_call x4, Pallas kernels, triad_chunk(): pl.pallas_call(functools.partial(triad_kernel, sizes, slots, offset, prep...  8.75 us
    pallas_call x2, Pallas kernels, dft_far(): pl.pallas_call(functools.partial(dft_far_kernel, sizes, far, points, offs...  4.98 us
    pallas_call x1, Pallas kernels, dft_rest(): pl.pallas_call(functools.partial(dft_rest_kernel, sizes, plan, points), o...  4.8 us
  transfers between devices with their start and end apart: 9, of which 8 were waited for; matrix products, arithmetic and copies ran while one was open for 0% of the time, Pallas kernels for 10%

profile of v2, /device:TPU:0, one launch (start us, length us, event | category | flops | bytes accessed | tf_op | source)
XLA Modules:
  0.0 74.8 jit_solution(29582153202064263)
XLA Ops:
  0.0 2.5 %dft_far.2 = (bf16[128,256]{1,0:T(8,128)(2,1)S(1)}, bf16[4,128,256]{2,1,0:T(8,128)(2,1)S(1)}, bf16[4,128,256]{2,1,0:T(8,128)(2,1)S(1)}) custom-call(bf16[4,256,4096]{2,1,0:T(8,128)(2,1)} %snap_ref.1), custom_call_target="tpu_custom_call" | custom-call | tf_op jit(solution)/shard_map/dft_far/pallas_call | solution.py:104
  2.5 0.0 copy-start
  2.5 0.0 copy-start.1
  2.5 2.5 %dft_far.3 = (bf16[4,128,384]{2,1,0:T(8,128)(2,1)S(1)}, bf16[4,128,384]{2,1,0:T(8,128)(2,1)S(1)}) custom-call(bf16[4,256,4096]{2,1,0:T(8,128)(2,1)} %snap_ref.1, bf16[128,256]{1,0:T(8,128)(2,1)S(1)} %get-tuple-element.17.refs_1_.table_ref), custom_call_target="tpu_custom_call" | custom-call | tf_op jit(solution)/shard_map/dft_far/pallas_call | solution.py:104
  5.0 4.8 %dft_rest.1 = (bf16[4,128,256]{2,1,0:T(8,128)(2,1)S(1)}, bf16[4,128,256]{2,1,0:T(8,128)(2,1)S(1)}, bf16[4,128,128]{2,1,0:T(8,128)(2,1)S(1)}, bf16[4,128,128]{2,1...) custom-call(bf16[128,256]{1,0:T(8,128)(2,1)S(1)} %get-tuple-element.17.refs_1_.table_ref, ...), custom_call_target="tpu_custom_call" | custom-call | flops 1073741824 | bytes 12582912 | tf_op jit(solution)/shard_map/dft_rest/pallas_call | solution.py:132
  9.8 0.6 collective-permute-start
  10.4 2.5 %collective-permute-start.1 = (bf16[4,128,256]{2,1,0:T(8,128)(2,1)S(1)}, bf16[4,128,256]{2,1,0:T(8,128)(2,1)S(1)}, u32[]{:S(2)}, u32[]{:S(2)}) collective-permute-start(bf16[4,128,256]{2,1,0:T(8,128)(2,1)S(1)} %get-tuple-element.21), channel_id=1, source_target_pairs={{0,2},{1,3},{2,0},{3,1},{4,6},{5,7},{6,4},{7,5},{8,10},{9,11},{10,... | collective-permute-start | bytes 786440 | tf_op jit(solution)/shard_map/ppermute | solution.py:307
  12.9 0.0 collective-permute-start.2
  13.0 1.7 %collective-permute-start.4 = (bf16[4,128,384]{2,1,0:T(8,128)(2,1)S(1)}, bf16[4,128,384]{2,1,0:T(8,128)(2,1)S(1)}, u32[]{:S(2)}, u32[]{:S(2)}) collective-permute-start(bf16[4,128,384]{2,1,0:T(8,128)(2,1)S(1)} %get-tuple-element.23), channel_id=1, source_target_pairs={{0,3},{1,2},{2,1},{3,0},{4,7},{5,6},{6,5},{7,4},{8,11},{9,10},{10,... | collective-permute-start | bytes 1179656 | tf_op jit(solution)/shard_map/ppermute | solution.py:307
  14.7 0.1 collective-permute-start.3
  14.7 5.3 %collective-permute-done.1.refs_4_ = bf16[4,128,256]{2,1,0:T(8,128)(2,1)S(1)} collective-permute-done((bf16[4,128,256]{2,1,0:T(8,128)(2,1)S(1)}, bf16[4,128,256]{2,1,0:T(8,128)(2,1)S(1)}, u32[]{:S(2)}, u32[]{:S(2)}) %collective-permute-start.1) | collective-permute-done | bytes 262176 | tf_op jit(solution)/shard_map/ppermute | solution.py:307
  20.1 2.0 %collective-permute-start.5 = (bf16[4,128,256]{2,1,0:T(8,128)(2,1)S(1)}, bf16[4,128,256]{2,1,0:T(8,128)(2,1)S(1)}, u32[]{:S(2)}, u32[]{:S(2)}) collective-permute-start(bf16[4,128,256]{2,1,0:T(8,128)(2,1)S(1)} %get-tuple-element.24), channel_id=1, source_target_pairs={{0,2},{1,3},{2,0},{3,1},{4,6},{5,7},{6,4},{7,5},{8,10},{9,11},{10,... | collective-permute-start | bytes 786440 | tf_op jit(solution)/shard_map/ppermute | solution.py:307
  22.1 3.1 %collective-permute-done.2.refs_5_ = bf16[4,128,256]{2,1,0:T(8,128)(2,1)S(1)} collective-permute-done((bf16[4,128,256]{2,1,0:T(8,128)(2,1)S(1)}, bf16[4,128,256]{2,1,0:T(8,128)(2,1)S(1)}, u32[]{:S(2)}, u32[]{:S(2)}) %collective-permute-start.2) | collective-permute-done | bytes 262176 | tf_op jit(solution)/shard_map/ppermute | solution.py:307
  25.2 2.2 %collective-permute-start.6 = (bf16[4,128,256]{2,1,0:T(8,128)(2,1)S(1)}, bf16[4,128,256]{2,1,0:T(8,128)(2,1)S(1)}, u32[]{:S(2)}, u32[]{:S(2)}) collective-permute-start(bf16[4,128,256]{2,1,0:T(8,128)(2,1)S(1)} %get-tuple-element.25), channel_id=1, source_target_pairs={{0,3},{1,2},{2,1},{3,0},{4,7},{5,6},{6,5},{7,4},{8,11},{9,10},{10,... | collective-permute-start | bytes 786440 | tf_op jit(solution)/shard_map/ppermute | solution.py:307
  27.4 6.2 %collective-permute-done.4.refs_6_ = bf16[4,128,384]{2,1,0:T(8,128)(2,1)S(1)} collective-permute-done((bf16[4,128,384]{2,1,0:T(8,128)(2,1)S(1)}, bf16[4,128,384]{2,1,0:T(8,128)(2,1)S(1)}, u32[]{:S(2)}, u32[]{:S(2)}) %collective-permute-start.4) | collective-permute-done | bytes 393248 | tf_op jit(solution)/shard_map/ppermute | solution.py:307
  33.7 1.4 %collective-permute-start.7 = (bf16[4,128,128]{2,1,0:T(8,128)(2,1)S(1)}, bf16[4,128,128]{2,1,0:T(8,128)(2,1)S(1)}, u32[]{:S(2)}, u32[]{:S(2)}) collective-permute-start(bf16[4,128,128]{2,1,0:T(8,128)(2,1)S(1)} %get-tuple-element.26), channel_id=1, source_target_pairs={{0,2},{1,3},{2,0},{3,1},{4,6},{5,7},{6,4},{7,5},{8,10},{9,11},{10,... | collective-permute-start | bytes 393224 | tf_op jit(solution)/shard_map/ppermute | solution.py:307
  35.1 0.0 collective-permute-done.refs_3_.refs_4_.refs_1_
  35.1 0.5 collective-permute-start.8
  35.6 0.2 prepare.1.refs_3_
  35.8 0.0 copy-done
  35.8 0.0 copy-done.1
  35.8 2.2 %triads.4.refs_2_ = f32[16,16,128]{2,1,0:T(8,128)S(1)} custom-call(s32[2,64]{1,0:T(2,128)S(1)} %bitcast.9, f32[1,4096]{1,0:T(1,128)S(1)} %bitcast.5, bf16[4,128,1024]{2,1,0:T(8,128)(2,1)S(1)} %get-tuple-element.19.refs_2_.refs_3_.refs_0_, bf16[4,128,1024]{2,1,0:T(8,128)(2,1)S(1)} %collective-permute-done.refs_3_.refs_4_.refs_1_, ...), custom_call_target="tpu_custom_call" | custom-call | flops 134217728 | bytes 1048576 | tf_op jit(solution)/shard_map/triads/pallas_call | solution.py:267
  38.0 4.6 %collective-permute-done.3.refs_5_ = bf16[4,128,384]{2,1,0:T(8,128)(2,1)S(1)} collective-permute-done((bf16[4,128,384]{2,1,0:T(8,128)(2,1)S(1)}, bf16[4,128,384]{2,1,0:T(8,128)(2,1)S(1)}, u32[]{:S(2)}, u32[]{:S(2)}) %collective-permute-start.3) | collective-permute-done | bytes 393248 | tf_op jit(solution)/shard_map/ppermute | solution.py:307
  42.6 2.9 %triads.5.refs_2_ = f32[16,16,128]{2,1,0:T(8,128)S(1)} custom-call(s32[2,64]{1,0:T(2,128)S(1)} %bitcast.10, f32[1,4096]{1,0:T(1,128)S(1)} %bitcast.6, f32[16,16,128]{2,1,0:T(8,128)S(1)} %triads.4.refs_2_, bf16[4,128,1024]{2,1,0:T(8,128)(2,1)S(1)} %get-tuple-element.19.refs_2_.refs_3_.refs_0_, ...), custom_call_target="tpu_custom_call" | custom-call | flops 201326592 | bytes 1572864 | tf_op jit(solution)/shard_map/triads/pallas_call | solution.py:267
  45.4 2.7 %collective-permute-done.5.refs_5_ = bf16[4,128,256]{2,1,0:T(8,128)(2,1)S(1)} collective-permute-done((bf16[4,128,256]{2,1,0:T(8,128)(2,1)S(1)}, bf16[4,128,256]{2,1,0:T(8,128)(2,1)S(1)}, u32[]{:S(2)}, u32[]{:S(2)}) %collective-permute-start.5) | collective-permute-done | bytes 262176 | tf_op jit(solution)/shard_map/ppermute | solution.py:307
  48.2 5.2 %collective-permute-done.6.refs_6_ = bf16[4,128,256]{2,1,0:T(8,128)(2,1)S(1)} collective-permute-done((bf16[4,128,256]{2,1,0:T(8,128)(2,1)S(1)}, bf16[4,128,256]{2,1,0:T(8,128)(2,1)S(1)}, u32[]{:S(2)}, u32[]{:S(2)}) %collective-permute-start.6) | collective-permute-done | bytes 262176 | tf_op jit(solution)/shard_map/ppermute | solution.py:307
  53.3 2.2 %triads.6.refs_2_ = f32[16,16,128]{2,1,0:T(8,128)S(1)} custom-call(s32[2,64]{1,0:T(2,128)S(1)} %bitcast.11, f32[1,4096]{1,0:T(1,128)S(1)} %bitcast.7, f32[16,16,128]{2,1,0:T(8,128)S(1)} %triads.5.refs_2_, bf16[4,128,1024]{2,1,0:T(8,128)(2,1)S(1)} %get-tuple-element.19.refs_2_.refs_3_.refs_0_, ...), custom_call_target="tpu_custom_call" | custom-call | flops 134217728 | bytes 1048576 | tf_op jit(solution)/shard_map/triads/pallas_call | solution.py:267
  55.6 1.0 %collective-permute-done.7.refs_4_ = bf16[4,128,128]{2,1,0:T(8,128)(2,1)S(1)} collective-permute-done((bf16[4,128,128]{2,1,0:T(8,128)(2,1)S(1)}, bf16[4,128,128]{2,1,0:T(8,128)(2,1)S(1)}, u32[]{:S(2)}, u32[]{:S(2)}) %collective-permute-start.7) | collective-permute-done | bytes 131104 | tf_op jit(solution)/shard_map/ppermute | solution.py:307
  56.6 2.3 %collective-permute-done.8.refs_5_ = bf16[4,128,128]{2,1,0:T(8,128)(2,1)S(1)} collective-permute-done((bf16[4,128,128]{2,1,0:T(8,128)(2,1)S(1)}, bf16[4,128,128]{2,1,0:T(8,128)(2,1)S(1)}, u32[]{:S(2)}, u32[]{:S(2)}) %collective-permute-start.8) | collective-permute-done | bytes 131104 | tf_op jit(solution)/shard_map/ppermute | solution.py:307
  58.9 1.4 %triads.7 = (f32[16,16,128]{2,1,0:T(8,128)S(1)}, f32[1,2048,128]{2,1,0:T(8,128)S(1)}) custom-call(s32[2,64]{1,0:T(2,128)S(1)} %bitcast.12, f32[1,4096]{1,0:T(1,128)S(1)} %bitcast.8, f32[16,16,128]{2,1,0:T(8,128)S(1)} %triads.6.refs_2_, f32[1,2048,128]{2,1,0:T(8,128)S(1)} %prepare.1.refs_3_, ...), custom_call_target="tpu_custom_call", output_to_operand_aliasing={{1}: (3, {})} | custom-call | flops 67108864 | bytes 524288 | tf_op jit(solution)/shard_map/triads/pallas_call | solution.py:267
  60.3 13.6 %all_to_all.5 = f32[16,16,128]{2,1,0:T(8,128)S(1)} all-to-all(f32[16,16,128]{2,1,0:T(8,128)S(1)} %get-tuple-element.28), channel_id=1, replica_groups=mesh['groups'=2,'space'=4,'freq'=2,'band'=2] {'space','freq','band'}, dimensions={0} | all-to-all | bytes 262144 | tf_op jit(solution)/shard_map/all_to_all | solution.py:346
  73.9 0.1 reshape.13
  74.1 0.7 reshape.14
  (2 shorter events, 0.0 us)
Async XLA Ops:
  2.5 33.3 %copy-start = (f32[4096]{0:T(1024)S(1)}, f32[4096]{0:T(1024)}, u32[]{:S(2)}) copy-start(f32[4096]{0:T(1024)} %param.4) | copy-start | bytes 49156
  2.5 33.3 %copy-start.1 = (s32[64,2]{0,1:T(2,128)S(1)}, s32[64,2]{0,1:T(2,128)}, u32[]{:S(2)}) copy-start(s32[64,2]{0,1:T(2,128)} %param.5) | copy-start | bytes 1540
  9.8 25.2 %collective-permute-start = (bf16[4,128,1024]{2,1,0:T(8,128)(2,1)S(1)}, bf16[4,128,1024]{2,1,0:T(8,128)(2,1)S(1)}, u32[]{:S(2)}, u32[]{:S(2)}) collective-permute-start(bf16[4,128,1024]{2,1,0:T(8,128)(2,1)S(1)} %get-tuple-element.20), channel_id=1, source_target_pairs={{0,1},{1,0},{2,3},{3,2},{4,5},{5,4},{6,7},{7,6},{8,9},{9,8},{10,11... | collective-permute-start | bytes 3145736 | tf_op jit(solution)/shard_map/ppermute | solution.py:307
  10.4 9.7 %collective-permute-start.1 = (bf16[4,128,256]{2,1,0:T(8,128)(2,1)S(1)}, bf16[4,128,256]{2,1,0:T(8,128)(2,1)S(1)}, u32[]{:S(2)}, u32[]{:S(2)}) collective-permute-start(bf16[4,128,256]{2,1,0:T(8,128)(2,1)S(1)} %get-tuple-element.21), channel_id=1, source_target_pairs={{0,2},{1,3},{2,0},{3,1},{4,6},{5,7},{6,4},{7,5},{8,10},{9,11},{10,... | collective-permute-start | bytes 786440 | tf_op jit(solution)/shard_map/ppermute | solution.py:307
  12.9 12.3 %collective-permute-start.2 = (bf16[4,128,256]{2,1,0:T(8,128)(2,1)S(1)}, bf16[4,128,256]{2,1,0:T(8,128)(2,1)S(1)}, u32[]{:S(2)}, u32[]{:S(2)}) collective-permute-start(bf16[4,128,256]{2,1,0:T(8,128)(2,1)S(1)} %get-tuple-element.22), channel_id=1, source_target_pairs={{0,3},{1,2},{2,1},{3,0},{4,7},{5,6},{6,5},{7,4},{8,11},{9,10},{10,... | collective-permute-start | bytes 786440 | tf_op jit(solution)/shard_map/ppermute | solution.py:307
  13.0 20.7 %collective-permute-start.4 = (bf16[4,128,384]{2,1,0:T(8,128)(2,1)S(1)}, bf16[4,128,384]{2,1,0:T(8,128)(2,1)S(1)}, u32[]{:S(2)}, u32[]{:S(2)}) collective-permute-start(bf16[4,128,384]{2,1,0:T(8,128)(2,1)S(1)} %get-tuple-element.23), channel_id=1, source_target_pairs={{0,3},{1,2},{2,1},{3,0},{4,7},{5,6},{6,5},{7,4},{8,11},{9,10},{10,... | collective-permute-start | bytes 1179656 | tf_op jit(solution)/shard_map/ppermute | solution.py:307
  14.7 27.9 %collective-permute-start.3 = (bf16[4,128,384]{2,1,0:T(8,128)(2,1)S(1)}, bf16[4,128,384]{2,1,0:T(8,128)(2,1)S(1)}, u32[]{:S(2)}, u32[]{:S(2)}) collective-permute-start(bf16[4,128,384]{2,1,0:T(8,128)(2,1)S(1)} %get-tuple-element.18.after_ref), channel_id=1, source_target_pairs={{0,2},{1,3},{2,0},{3,1},{4,6},{5,7},{6,4},{7,5},{8,10},{9,11},{10,... | collective-permute-start | bytes 1179656 | tf_op jit(solution)/shard_map/ppermute | solution.py:307
  20.1 28.1 %collective-permute-start.5 = (bf16[4,128,256]{2,1,0:T(8,128)(2,1)S(1)}, bf16[4,128,256]{2,1,0:T(8,128)(2,1)S(1)}, u32[]{:S(2)}, u32[]{:S(2)}) collective-permute-start(bf16[4,128,256]{2,1,0:T(8,128)(2,1)S(1)} %get-tuple-element.24), channel_id=1, source_target_pairs={{0,2},{1,3},{2,0},{3,1},{4,6},{5,7},{6,4},{7,5},{8,10},{9,11},{10,... | collective-permute-start | bytes 786440 | tf_op jit(solution)/shard_map/ppermute | solution.py:307
  25.2 28.1 %collective-permute-start.6 = (bf16[4,128,256]{2,1,0:T(8,128)(2,1)S(1)}, bf16[4,128,256]{2,1,0:T(8,128)(2,1)S(1)}, u32[]{:S(2)}, u32[]{:S(2)}) collective-permute-start(bf16[4,128,256]{2,1,0:T(8,128)(2,1)S(1)} %get-tuple-element.25), channel_id=1, source_target_pairs={{0,3},{1,2},{2,1},{3,0},{4,7},{5,6},{6,5},{7,4},{8,11},{9,10},{10,... | collective-permute-start | bytes 786440 | tf_op jit(solution)/shard_map/ppermute | solution.py:307
  33.7 22.9 %collective-permute-start.7 = (bf16[4,128,128]{2,1,0:T(8,128)(2,1)S(1)}, bf16[4,128,128]{2,1,0:T(8,128)(2,1)S(1)}, u32[]{:S(2)}, u32[]{:S(2)}) collective-permute-start(bf16[4,128,128]{2,1,0:T(8,128)(2,1)S(1)} %get-tuple-element.26), channel_id=1, source_target_pairs={{0,2},{1,3},{2,0},{3,1},{4,6},{5,7},{6,4},{7,5},{8,10},{9,11},{10,... | collective-permute-start | bytes 393224 | tf_op jit(solution)/shard_map/ppermute | solution.py:307
  35.1 23.8 %collective-permute-start.8 = (bf16[4,128,128]{2,1,0:T(8,128)(2,1)S(1)}, bf16[4,128,128]{2,1,0:T(8,128)(2,1)S(1)}, u32[]{:S(2)}, u32[]{:S(2)}) collective-permute-start(bf16[4,128,128]{2,1,0:T(8,128)(2,1)S(1)} %get-tuple-element.27), channel_id=1, source_target_pairs={{0,3},{1,2},{2,1},{3,0},{4,7},{5,6},{6,5},{7,4},{8,11},{9,10},{10,... | collective-permute-start | bytes 393224 | tf_op jit(solution)/shard_map/ppermute | solution.py:307

commit v3 on v2

--- a/solution.py
+++ b/solution.py
@@ -22,11 +22,10 @@
 
 def split_widths(points):
     tiles = points // LANES
-    first = max(1, tiles // 4)
-    rest = tiles - first - 1
-    count = max(1, -(-rest // 3))
+    rest = tiles - 2
+    count = -(-rest // 3)
     middle = [rest // count + (i < rest % count) for i in range(count)]
-    return [w * LANES for w in [first] + middle + [1]]
+    return [w * LANES for w in [1] + middle + [1]]
 
 
 def make_table(length):
@@ -243,7 +242,7 @@
         total = total * scale
         if has_prior:
             total = total + prior_ref[group]
-        out_ref[group] = total
+        out_ref[group] = total.astype(out_ref.dtype)
         return carry
 
     lax.fori_loop(0, out_ref.shape[0], one_pack, 0, unroll=4)
@@ -255,7 +254,8 @@
     spec_shape = (width // LANES, rows * NB, LANES)
     operands = [ids, weights] + ([] if prior is None else [prior])
     aliases = {}
-    out_shape = [jax.ShapeDtypeStruct((packs, NB, LANES), jnp.float32)]
+    kept = jnp.float32 if prepared is None else jnp.bfloat16
+    out_shape = [jax.ShapeDtypeStruct((packs, NB, LANES), kept)]
     scratch = [pltpu.SMEM(ids.shape, jnp.int32), pltpu.SemaphoreType.DMA]
     if prepared is None:
         scratch = [pltpu.VMEM(spec_shape, jnp.float32)] + scratch
@@ -283,6 +283,37 @@
     )(*operands)[0]
 
 
+def finish_kernel(part_ref, out_ref):
+    packs = out_ref.shape[0] // PACK
+    sublane = lax.broadcasted_iota(jnp.int32, (8, LANES), 0)
+    lane = lax.broadcasted_iota(jnp.int32, (8, LANES), 1)
+    mine = lane // NB == sublane
+    for pack in range(packs):
+        total = part_ref[pack].astype(jnp.float32)
+        for device in range(1, part_ref.shape[0] // packs):
+            total = total + part_ref[device * packs + pack].astype(jnp.float32)
+        for half in range(2):
+            spread = pltpu.roll(total[half * 8 : half * 8 + 8], 0, 1, stride=NB, stride_axis=0)
+            for column in range(2 * PACK):
+                moved = pltpu.roll(spread, (-column * NB) % LANES, 1)
+                row = jnp.sum(jnp.where(mine, moved, 0.0), axis=0, keepdims=True)
+                triad, part = divmod(column, 2)
+                start = part * NB * NB + half * LANES
+                out_ref[pack * PACK + triad : pack * PACK + triad + 1, start : start + LANES] = row
+
+
+def finish(pieces, devices):
+    rows = pieces.shape[0] // devices * PACK
+    return pl.pallas_call(
+        finish_kernel,
+        out_shape=jax.ShapeDtypeStruct((rows, 2 * NB * NB), jnp.float32),
+        in_specs=[VMEM],
+        out_specs=VMEM,
+        compiler_params=pltpu.CompilerParams(vmem_limit_bytes=8 * MIB),
+        name="finish",
+    )(pieces)
+
+
 def mode_decomposition(snapshots, weights, triads):
     points = snapshots.shape[2]
     snapshots = pltpu.with_memory_space_constraint(snapshots, pltpu.HBM)
@@ -342,11 +373,8 @@
 
     axes = ("space", "freq", "band")
     devices = lax.axis_size("space") * shards
-    packs = total.shape[0]
     pieces = lax.all_to_all(total, axes, split_axis=0, concat_axis=0, tiled=True)
-    mine = pieces.reshape(devices, packs // devices, NB, LANES).sum(axis=0)
-    mine = mine.reshape(packs // devices, NB, PACK, 2, NB).transpose(0, 2, 3, 1, 4)
-    return mine.reshape(packs // devices * PACK, 2 * NB * NB)
+    return finish(pieces, devices)
 
 
 def solution(mesh):

time: 75 us -> 73.9 us (0.985)
  blocking collectives: 13.6 us -> 12.6 us
  local copies, waits for them, and re-layouts: 0.85 us -> 0.01 us
    all_to_all x1, blocking collectives: 13.6 us -> 12.6 us  [mode_decomposition(): lax.all_to_all(total, axes, split_axis=0, concat_axis=0, tiled=True)]
    reshape x2 -> x0, local copies, waits for them, and re-layouts: 0.82 us -> none  [the longest x1 0.69 us: mode_decomposition(): return mine.reshape(packs // devices * PACK, 2 * NB * NB)]
    pallas_call x0 -> x1, Pallas kernels: none -> 0.77 us  [finish(): pl.pallas_call(finish_kernel, out_shape=jax.ShapeDtypeStruct((rows, 2 * N...]
where the time goes in v3:
time: 73.9 us; the launch traced here: 73.7 us
  waiting for transfers between devices  30.6 us (41%)
  Pallas kernels  19.4 us (26%)
  blocking collectives  12.6 us (17%)
  starting transfers between devices  11.1 us (15%)
    ppermute x9, waiting for transfers between devices, send(): return lax.ppermute(value, ('freq', 'band'), pairs)  30.6 us
    all_to_all x1, blocking collectives, mode_decomposition(): lax.all_to_all(total, axes, split_axis=0, concat_axis=0, tiled=True)  12.6 us
    ppermute x9, starting transfers between devices, send(): return lax.ppermute(value, ('freq', 'band'), pairs)  11.1 us
    pallas_call x4, Pallas kernels, triad_chunk(): pl.pallas_call(functools.partial(triad_kernel, sizes, slots, offset, prep...  8.64 us
    pallas_call x1, Pallas kernels, dft_rest(): pl.pallas_call(functools.partial(dft_rest_kernel, sizes, plan, points), o...  5 us
    pallas_call x2, Pallas kernels, dft_far(): pl.pallas_call(functools.partial(dft_far_kernel, sizes, far, points, offs...  4.78 us
  transfers between devices with their start and end apart: 9, of which 8 were waited for; matrix products, arithmetic and copies ran while one was open for 0% of the time, Pallas kernels for 10%

profile of v3, /device:TPU:0, one launch (start us, length us, event | category | flops | bytes accessed | tf_op | source)
XLA Modules:
  0.0 73.7 jit_solution(12895434002675984334)
XLA Ops:
  0.0 2.3 %dft_far.2 = (bf16[128,256]{1,0:T(8,128)(2,1)S(1)}, bf16[4,128,128]{2,1,0:T(8,128)(2,1)S(1)}, bf16[4,128,128]{2,1,0:T(8,128)(2,1)S(1)}) custom-call(bf16[4,256,4096]{2,1,0:T(8,128)(2,1)} %snap_ref.1), custom_call_target="tpu_custom_call" | custom-call | tf_op jit(solution)/shard_map/dft_far/pallas_call | solution.py:103
  2.3 0.0 copy-start
  2.3 0.0 copy-start.1
  2.3 2.5 %dft_far.3 = (bf16[4,128,384]{2,1,0:T(8,128)(2,1)S(1)}, bf16[4,128,384]{2,1,0:T(8,128)(2,1)S(1)}) custom-call(bf16[4,256,4096]{2,1,0:T(8,128)(2,1)} %snap_ref.1, bf16[128,256]{1,0:T(8,128)(2,1)S(1)} %get-tuple-element.17.refs_1_.table_ref), custom_call_target="tpu_custom_call" | custom-call | tf_op jit(solution)/shard_map/dft_far/pallas_call | solution.py:103
  4.8 5.0 %dft_rest.1 = (bf16[4,128,384]{2,1,0:T(8,128)(2,1)S(1)}, bf16[4,128,384]{2,1,0:T(8,128)(2,1)S(1)}, bf16[4,128,128]{2,1,0:T(8,128)(2,1)S(1)}, bf16[4,128,128]{2,1...) custom-call(bf16[128,256]{1,0:T(8,128)(2,1)S(1)} %get-tuple-element.17.refs_1_.table_ref, ...), custom_call_target="tpu_custom_call" | custom-call | flops 1073741824 | bytes 12582912 | tf_op jit(solution)/shard_map/dft_rest/pallas_call | solution.py:131
  9.8 0.6 collective-permute-start
  10.4 2.6 %collective-permute-start.1 = (bf16[4,128,128]{2,1,0:T(8,128)(2,1)S(1)}, bf16[4,128,128]{2,1,0:T(8,128)(2,1)S(1)}, u32[]{:S(2)}, u32[]{:S(2)}) collective-permute-start(bf16[4,128,128]{2,1,0:T(8,128)(2,1)S(1)} %get-tuple-element.21), channel_id=1, source_target_pairs={{0,2},{1,3},{2,0},{3,1},{4,6},{5,7},{6,4},{7,5},{8,10},{9,11},{10,... | collective-permute-start | bytes 393224 | tf_op jit(solution)/shard_map/ppermute | solution.py:338
  12.9 0.0 collective-permute-start.2
  13.0 1.7 %collective-permute-start.4 = (bf16[4,128,384]{2,1,0:T(8,128)(2,1)S(1)}, bf16[4,128,384]{2,1,0:T(8,128)(2,1)S(1)}, u32[]{:S(2)}, u32[]{:S(2)}) collective-permute-start(bf16[4,128,384]{2,1,0:T(8,128)(2,1)S(1)} %get-tuple-element.23), channel_id=1, source_target_pairs={{0,3},{1,2},{2,1},{3,0},{4,7},{5,6},{6,5},{7,4},{8,11},{9,10},{10,... | collective-permute-start | bytes 1179656 | tf_op jit(solution)/shard_map/ppermute | solution.py:338
  14.7 0.1 collective-permute-start.3
  14.8 2.5 %collective-permute-done.1.refs_4_ = bf16[4,128,128]{2,1,0:T(8,128)(2,1)S(1)} collective-permute-done((bf16[4,128,128]{2,1,0:T(8,128)(2,1)S(1)}, bf16[4,128,128]{2,1,0:T(8,128)(2,1)S(1)}, u32[]{:S(2)}, u32[]{:S(2)}) %collective-permute-start.1) | collective-permute-done | bytes 131104 | tf_op jit(solution)/shard_map/ppermute | solution.py:338
  17.3 2.0 %collective-permute-start.5 = (bf16[4,128,384]{2,1,0:T(8,128)(2,1)S(1)}, bf16[4,128,384]{2,1,0:T(8,128)(2,1)S(1)}, u32[]{:S(2)}, u32[]{:S(2)}) collective-permute-start(bf16[4,128,384]{2,1,0:T(8,128)(2,1)S(1)} %get-tuple-element.24), channel_id=1, source_target_pairs={{0,2},{1,3},{2,0},{3,1},{4,6},{5,7},{6,4},{7,5},{8,10},{9,11},{10,... | collective-permute-start | bytes 1179656 | tf_op jit(solution)/shard_map/ppermute | solution.py:338
  19.3 0.3 collective-permute-done.2.refs_5_
  19.6 2.2 %collective-permute-start.6 = (bf16[4,128,384]{2,1,0:T(8,128)(2,1)S(1)}, bf16[4,128,384]{2,1,0:T(8,128)(2,1)S(1)}, u32[]{:S(2)}, u32[]{:S(2)}) collective-permute-start(bf16[4,128,384]{2,1,0:T(8,128)(2,1)S(1)} %get-tuple-element.25), channel_id=1, source_target_pairs={{0,3},{1,2},{2,1},{3,0},{4,7},{5,6},{6,5},{7,4},{8,11},{9,10},{10,... | collective-permute-start | bytes 1179656 | tf_op jit(solution)/shard_map/ppermute | solution.py:338
  21.8 6.2 %collective-permute-done.4.refs_6_ = bf16[4,128,384]{2,1,0:T(8,128)(2,1)S(1)} collective-permute-done((bf16[4,128,384]{2,1,0:T(8,128)(2,1)S(1)}, bf16[4,128,384]{2,1,0:T(8,128)(2,1)S(1)}, u32[]{:S(2)}, u32[]{:S(2)}) %collective-permute-start.4) | collective-permute-done | bytes 393248 | tf_op jit(solution)/shard_map/ppermute | solution.py:338
  28.1 1.4 %collective-permute-start.7 = (bf16[4,128,128]{2,1,0:T(8,128)(2,1)S(1)}, bf16[4,128,128]{2,1,0:T(8,128)(2,1)S(1)}, u32[]{:S(2)}, u32[]{:S(2)}) collective-permute-start(bf16[4,128,128]{2,1,0:T(8,128)(2,1)S(1)} %get-tuple-element.26), channel_id=1, source_target_pairs={{0,2},{1,3},{2,0},{3,1},{4,6},{5,7},{6,4},{7,5},{8,10},{9,11},{10,... | collective-permute-start | bytes 393224 | tf_op jit(solution)/shard_map/ppermute | solution.py:338
  29.5 0.0 collective-permute-done.refs_3_.refs_4_.refs_1_
  29.5 0.5 collective-permute-start.8
  30.0 0.2 prepare.1.refs_3_
  30.2 0.0 copy-done
  30.2 0.0 copy-done.1
  30.2 1.5 %triads.4.refs_2_ = f32[16,16,128]{2,1,0:T(8,128)S(1)} custom-call(s32[2,64]{1,0:T(2,128)S(1)} %bitcast.6, f32[1,4096]{1,0:T(1,128)S(1)} %bitcast.2, bf16[4,128,1024]{2,1,0:T(8,128)(2,1)S(1)} %get-tuple-element.19.refs_2_.refs_3_.refs_0_, bf16[4,128,1024]{2,1,0:T(8,128)(2,1)S(1)} %collective-permute-done.refs_3_.refs_4_.refs_1_, ...), custom_call_target="tpu_custom_call" | custom-call | flops 67108864 | bytes 524288 | tf_op jit(solution)/shard_map/triads/pallas_call | solution.py:267
  31.6 5.3 %collective-permute-done.3.refs_5_ = bf16[4,128,384]{2,1,0:T(8,128)(2,1)S(1)} collective-permute-done((bf16[4,128,384]{2,1,0:T(8,128)(2,1)S(1)}, bf16[4,128,384]{2,1,0:T(8,128)(2,1)S(1)}, u32[]{:S(2)}, u32[]{:S(2)}) %collective-permute-start.3) | collective-permute-done | bytes 393248 | tf_op jit(solution)/shard_map/ppermute | solution.py:338
  37.0 2.9 %triads.5.refs_2_ = f32[16,16,128]{2,1,0:T(8,128)S(1)} custom-call(s32[2,64]{1,0:T(2,128)S(1)} %bitcast.7, f32[1,4096]{1,0:T(1,128)S(1)} %bitcast.3, f32[16,16,128]{2,1,0:T(8,128)S(1)} %triads.4.refs_2_, bf16[4,128,1024]{2,1,0:T(8,128)(2,1)S(1)} %get-tuple-element.19.refs_2_.refs_3_.refs_0_, ...), custom_call_target="tpu_custom_call" | custom-call | flops 201326592 | bytes 1572864 | tf_op jit(solution)/shard_map/triads/pallas_call | solution.py:267
  39.8 5.5 %collective-permute-done.5.refs_5_ = bf16[4,128,384]{2,1,0:T(8,128)(2,1)S(1)} collective-permute-done((bf16[4,128,384]{2,1,0:T(8,128)(2,1)S(1)}, bf16[4,128,384]{2,1,0:T(8,128)(2,1)S(1)}, u32[]{:S(2)}, u32[]{:S(2)}) %collective-permute-start.5) | collective-permute-done | bytes 393248 | tf_op jit(solution)/shard_map/ppermute | solution.py:338
  45.4 8.0 %collective-permute-done.6.refs_6_ = bf16[4,128,384]{2,1,0:T(8,128)(2,1)S(1)} collective-permute-done((bf16[4,128,384]{2,1,0:T(8,128)(2,1)S(1)}, bf16[4,128,384]{2,1,0:T(8,128)(2,1)S(1)}, u32[]{:S(2)}, u32[]{:S(2)}) %collective-permute-start.6) | collective-permute-done | bytes 393248 | tf_op jit(solution)/shard_map/ppermute | solution.py:338
  53.3 2.9 %triads.6.refs_2_ = f32[16,16,128]{2,1,0:T(8,128)S(1)} custom-call(s32[2,64]{1,0:T(2,128)S(1)} %bitcast.8, f32[1,4096]{1,0:T(1,128)S(1)} %bitcast.4, f32[16,16,128]{2,1,0:T(8,128)S(1)} %triads.5.refs_2_, bf16[4,128,1024]{2,1,0:T(8,128)(2,1)S(1)} %get-tuple-element.19.refs_2_.refs_3_.refs_0_, ...), custom_call_target="tpu_custom_call" | custom-call | flops 201326592 | bytes 1572864 | tf_op jit(solution)/shard_map/triads/pallas_call | solution.py:267
  56.2 0.4 collective-permute-done.7.refs_4_
  56.6 2.3 %collective-permute-done.8.refs_5_ = bf16[4,128,128]{2,1,0:T(8,128)(2,1)S(1)} collective-permute-done((bf16[4,128,128]{2,1,0:T(8,128)(2,1)S(1)}, bf16[4,128,128]{2,1,0:T(8,128)(2,1)S(1)}, u32[]{:S(2)}, u32[]{:S(2)}) %collective-permute-start.8) | collective-permute-done | bytes 131104 | tf_op jit(solution)/shard_map/ppermute | solution.py:338
  58.9 1.4 %triads.7 = (bf16[16,16,128]{2,1,0:T(8,128)(2,1)S(1)}, f32[1,2048,128]{2,1,0:T(8,128)S(1)}) custom-call(s32[2,64]{1,0:T(2,128)S(1)} %bitcast.9, f32[1,4096]{1,0:T(1,128)S(1)} %bitcast.5, f32[16,16,128]{2,1,0:T(8,128)S(1)} %triads.6.refs_2_, f32[1,2048,128]{2,1,0:T(8,128)S(1)} %prepare.1.refs_3_, ...), custom_call_target="tpu_custom_call", output_to_operand_aliasing={{1}: (3, {})} | custom-call | flops 67108864 | bytes 524288 | tf_op jit(solution)/shard_map/triads/pallas_call | solution.py:267
  60.4 12.6 %all_to_all.5.part_ref = bf16[16,16,128]{2,1,0:T(8,128)(2,1)S(1)} all-to-all(bf16[16,16,128]{2,1,0:T(8,128)(2,1)S(1)} %get-tuple-element.28), channel_id=1, replica_groups=mesh['groups'=2,'space'=4,'freq'=2,'band'=2] {'space','freq','band'}, dimensions={0} | all-to-all | bytes 131072 | tf_op jit(solution)/shard_map/all_to_all | solution.py:376
  72.9 0.8 %finish.1 = f32[4,512]{1,0:T(4,128)} custom-call(bf16[16,16,128]{2,1,0:T(8,128)(2,1)S(1)} %all_to_all.5.part_ref), custom_call_target="tpu_custom_call" | custom-call | tf_op jit(solution)/shard_map/finish/pallas_call | solution.py:307
Async XLA Ops:
  2.3 27.9 %copy-start = (f32[4096]{0:T(1024)S(1)}, f32[4096]{0:T(1024)}, u32[]{:S(2)}) copy-start(f32[4096]{0:T(1024)} %param.4) | copy-start | bytes 49156
  2.3 27.9 %copy-start.1 = (s32[64,2]{0,1:T(2,128)S(1)}, s32[64,2]{0,1:T(2,128)}, u32[]{:S(2)}) copy-start(s32[64,2]{0,1:T(2,128)} %param.5) | copy-start | bytes 1540
  9.8 19.6 %collective-permute-start = (bf16[4,128,1024]{2,1,0:T(8,128)(2,1)S(1)}, bf16[4,128,1024]{2,1,0:T(8,128)(2,1)S(1)}, u32[]{:S(2)}, u32[]{:S(2)}) collective-permute-start(bf16[4,128,1024]{2,1,0:T(8,128)(2,1)S(1)} %get-tuple-element.20), channel_id=1, source_target_pairs={{0,1},{1,0},{2,3},{3,2},{4,5},{5,4},{6,7},{7,6},{8,9},{9,8},{10,11... | collective-permute-start | bytes 3145736 | tf_op jit(solution)/shard_map/ppermute | solution.py:338
  10.4 6.9 %collective-permute-start.1 = (bf16[4,128,128]{2,1,0:T(8,128)(2,1)S(1)}, bf16[4,128,128]{2,1,0:T(8,128)(2,1)S(1)}, u32[]{:S(2)}, u32[]{:S(2)}) collective-permute-start(bf16[4,128,128]{2,1,0:T(8,128)(2,1)S(1)} %get-tuple-element.21), channel_id=1, source_target_pairs={{0,2},{1,3},{2,0},{3,1},{4,6},{5,7},{6,4},{7,5},{8,10},{9,11},{10,... | collective-permute-start | bytes 393224 | tf_op jit(solution)/shard_map/ppermute | solution.py:338
  12.9 6.7 %collective-permute-start.2 = (bf16[4,128,128]{2,1,0:T(8,128)(2,1)S(1)}, bf16[4,128,128]{2,1,0:T(8,128)(2,1)S(1)}, u32[]{:S(2)}, u32[]{:S(2)}) collective-permute-start(bf16[4,128,128]{2,1,0:T(8,128)(2,1)S(1)} %get-tuple-element.22), channel_id=1, source_target_pairs={{0,3},{1,2},{2,1},{3,0},{4,7},{5,6},{6,5},{7,4},{8,11},{9,10},{10,... | collective-permute-start | bytes 393224 | tf_op jit(solution)/shard_map/ppermute | solution.py:338
  13.0 15.1 %collective-permute-start.4 = (bf16[4,128,384]{2,1,0:T(8,128)(2,1)S(1)}, bf16[4,128,384]{2,1,0:T(8,128)(2,1)S(1)}, u32[]{:S(2)}, u32[]{:S(2)}) collective-permute-start(bf16[4,128,384]{2,1,0:T(8,128)(2,1)S(1)} %get-tuple-element.23), channel_id=1, source_target_pairs={{0,3},{1,2},{2,1},{3,0},{4,7},{5,6},{6,5},{7,4},{8,11},{9,10},{10,... | collective-permute-start | bytes 1179656 | tf_op jit(solution)/shard_map/ppermute | solution.py:338
  14.7 22.3 %collective-permute-start.3 = (bf16[4,128,384]{2,1,0:T(8,128)(2,1)S(1)}, bf16[4,128,384]{2,1,0:T(8,128)(2,1)S(1)}, u32[]{:S(2)}, u32[]{:S(2)}) collective-permute-start(bf16[4,128,384]{2,1,0:T(8,128)(2,1)S(1)} %get-tuple-element.18.after_ref), channel_id=1, source_target_pairs={{0,2},{1,3},{2,0},{3,1},{4,6},{5,7},{6,4},{7,5},{8,10},{9,11},{10,... | collective-permute-start | bytes 1179656 | tf_op jit(solution)/shard_map/ppermute | solution.py:338
  17.3 28.1 %collective-permute-start.5 = (bf16[4,128,384]{2,1,0:T(8,128)(2,1)S(1)}, bf16[4,128,384]{2,1,0:T(8,128)(2,1)S(1)}, u32[]{:S(2)}, u32[]{:S(2)}) collective-permute-start(bf16[4,128,384]{2,1,0:T(8,128)(2,1)S(1)} %get-tuple-element.24), channel_id=1, source_target_pairs={{0,2},{1,3},{2,0},{3,1},{4,6},{5,7},{6,4},{7,5},{8,10},{9,11},{10,... | collective-permute-start | bytes 1179656 | tf_op jit(solution)/shard_map/ppermute | solution.py:338
  19.6 33.7 %collective-permute-start.6 = (bf16[4,128,384]{2,1,0:T(8,128)(2,1)S(1)}, bf16[4,128,384]{2,1,0:T(8,128)(2,1)S(1)}, u32[]{:S(2)}, u32[]{:S(2)}) collective-permute-start(bf16[4,128,384]{2,1,0:T(8,128)(2,1)S(1)} %get-tuple-element.25), channel_id=1, source_target_pairs={{0,3},{1,2},{2,1},{3,0},{4,7},{5,6},{6,5},{7,4},{8,11},{9,10},{10,... | collective-permute-start | bytes 1179656 | tf_op jit(solution)/shard_map/ppermute | solution.py:338
  28.1 28.5 %collective-permute-start.7 = (bf16[4,128,128]{2,1,0:T(8,128)(2,1)S(1)}, bf16[4,128,128]{2,1,0:T(8,128)(2,1)S(1)}, u32[]{:S(2)}, u32[]{:S(2)}) collective-permute-start(bf16[4,128,128]{2,1,0:T(8,128)(2,1)S(1)} %get-tuple-element.26), channel_id=1, source_target_pairs={{0,2},{1,3},{2,0},{3,1},{4,6},{5,7},{6,4},{7,5},{8,10},{9,11},{10,... | collective-permute-start | bytes 393224 | tf_op jit(solution)/shard_map/ppermute | solution.py:338
  29.5 29.4 %collective-permute-start.8 = (bf16[4,128,128]{2,1,0:T(8,128)(2,1)S(1)}, bf16[4,128,128]{2,1,0:T(8,128)(2,1)S(1)}, u32[]{:S(2)}, u32[]{:S(2)}) collective-permute-start(bf16[4,128,128]{2,1,0:T(8,128)(2,1)S(1)} %get-tuple-element.27), channel_id=1, source_target_pairs={{0,3},{1,2},{2,1},{3,0},{4,7},{5,6},{6,5},{7,4},{8,11},{9,10},{10,... | collective-permute-start | bytes 393224 | tf_op jit(solution)/shard_map/ppermute | solution.py:338

commit v4 on v3

--- a/solution.py
+++ b/solution.py
@@ -28,7 +28,8 @@
     return [w * LANES for w in [1] + middle + [1]]
 
 
-def make_table(length):
+def make_table(table_ref):
+    rows, length = table_ref.shape
     turn = 2.0 * math.pi / length
     gain = 1.0 / math.sqrt(3.0 * length / 8.0)
     quarter = length // 4
@@ -47,12 +48,21 @@
         value = jnp.where(quadrant & 1 == 0, even, odd)
         return jnp.where((quadrant == 1) | (quadrant == 2), -value, value)
 
-    time = lax.broadcasted_iota(jnp.int32, (8, length), 1)
+    step = 16
+    row = lax.broadcasted_iota(jnp.int32, (step, length), 0)
+    time = lax.broadcasted_iota(jnp.int32, (step, length), 1)
     window = (0.5 - 0.5 * cosine(time)) * gain
-    row = lax.broadcasted_iota(jnp.int32, (2 * NF, length), 0)
-    time = lax.broadcasted_iota(jnp.int32, (2 * NF, length), 1)
-    wave = cosine((row & (NF - 1)) * time + jnp.where(row < NF, 0, quarter))
-    return (jnp.concatenate([window] * (NF // 4), axis=0) * wave).astype(jnp.bfloat16)
+
+    def some_rows(index, carry):
+        first = pl.multiple_of(index * step, step)
+        freq = (row + first) & (NF - 1)
+        ahead = jnp.where(first < NF, 0, quarter)
+        table_ref[pl.ds(first, step), :] = (window * cosine(freq * time + ahead)).astype(
+            table_ref.dtype
+        )
+        return carry
+
+    lax.fori_loop(0, rows // step, some_rows, 0)
 
 
 def shifted_part(slot, sign, freqs, bands):
@@ -63,34 +73,32 @@
 
 
 def dft_far_kernel(sizes, far, points, offset, own_table, *refs):
-    count = len(far)
-    snap_ref = refs[0]
-    outs = refs[len(refs) - 2 - count : len(refs) - 2]
+    snap_ref, table_ref = refs[:2]
+    outs = refs[len(refs) - 2 - len(far) : len(refs) - 2]
     buffer, arrived = refs[-2:]
-    blocks, length, width = buffer.shape[1:]
+    blocks, _, width = outs[0].shape
     copies = []
     for position, slot in enumerate(far):
         start = shifted_part(slot, 1, *sizes) * points + offset
         for block in range(blocks):
+            index = position * blocks + block
             copy = pltpu.make_async_copy(
                 snap_ref.at[block, :, pl.ds(pl.multiple_of(start, LANES), width)],
-                buffer.at[position, block],
-                arrived.at[position, block],
+                buffer.at[:, index * width : (index + 1) * width],
+                arrived.at[index],
             )
             copy.start()
             copies.append(copy)
     if own_table:
-        table_ref = refs[1]
-        table_ref[...] = make_table(length)
-    else:
-        table_ref = refs[1]
-    table = table_ref[...]
-    for position in range(count):
-        for block in range(blocks):
-            copies[position * blocks + block].wait()
-            outs[position][block] = jnp.dot(
-                table, buffer[position, block], preferred_element_type=jnp.float32
-            ).astype(jnp.bfloat16)
+        make_table(table_ref)
+    for copy in copies:
+        copy.wait()
+    spectra = jnp.dot(
+        table_ref[...], buffer[...], preferred_element_type=jnp.float32
+    ).astype(jnp.bfloat16)
+    for index in range(len(copies)):
+        position, block = divmod(index, blocks)
+        outs[position][block] = spectra[:, index * width : (index + 1) * width]
 
 
 def dft_far(snapshots, table, sizes, far, points, offset, width):
@@ -106,10 +114,10 @@
         in_specs=[ANY] + ([] if own_table else [VMEM]),
         out_specs=[VMEM] * len(out_shape),
         scratch_shapes=[
-            pltpu.VMEM((count, blocks, length, width), jnp.bfloat16),
-            pltpu.SemaphoreType.DMA((count, blocks)),
+            pltpu.VMEM((length, count * blocks * width), jnp.bfloat16),
+            pltpu.SemaphoreType.DMA((count * blocks,)),
         ],
-        compiler_params=pltpu.CompilerParams(vmem_limit_bytes=8 * MIB),
+        compiler_params=pltpu.CompilerParams(vmem_limit_bytes=12 * MIB),
         name="dft_far",
     )(snapshots, *([] if own_table else [table]))
 
@@ -245,7 +253,7 @@
         out_ref[group] = total.astype(out_ref.dtype)
         return carry
 
-    lax.fori_loop(0, out_ref.shape[0], one_pack, 0, unroll=4)
+    lax.fori_loop(0, out_ref.shape[0], one_pack, 0, unroll=16 if prepared else 4)
 
 
 def triad_chunk(ids, weights, sources, slots, sizes, offset, width, prior, scale, prepared=None):

time: 73.9 us -> 72.1 us (0.976)
  Pallas kernels: 19.4 us -> 17.5 us
    pallas_call x2, Pallas kernels: 4.78 us -> 3.34 us  [dft_far(): pl.pallas_call(functools.partial(dft_far_kernel, sizes, far, points, offs...]
where the time goes in v4:
time: 72.1 us; the launch traced here: 71.8 us
  waiting for transfers between devices  30.6 us (42%)
  Pallas kernels  17.5 us (24%)
  blocking collectives  12.6 us (17%)
  starting transfers between devices  11.1 us (15%)
    ppermute x9, waiting for transfers between devices, send(): return lax.ppermute(value, ('freq', 'band'), pairs)  30.6 us
    all_to_all x1, blocking collectives, mode_decomposition(): lax.all_to_all(total, axes, split_axis=0, concat_axis=0, tiled=True)  12.6 us
    ppermute x9, starting transfers between devices, send(): return lax.ppermute(value, ('freq', 'band'), pairs)  11.1 us
    pallas_call x4, Pallas kernels, triad_chunk(): pl.pallas_call(functools.partial(triad_kernel, sizes, slots, offset, prep...  8.25 us
    pallas_call x1, Pallas kernels, dft_rest(): pl.pallas_call(functools.partial(dft_rest_kernel, sizes, plan, points), o...  4.99 us
    pallas_call x2, Pallas kernels, dft_far(): pl.pallas_call(functools.partial(dft_far_kernel, sizes, far, points, offs...  3.34 us
  transfers between devices with their start and end apart: 9, of which 8 were waited for; matrix products, arithmetic and copies ran while one was open for 0% of the time, Pallas kernels for 10%

profile of v4, /device:TPU:0, one launch (start us, length us, event | category | flops | bytes accessed | tf_op | source)
XLA Modules:
  0.0 71.8 jit_solution(12035109849869496190)
XLA Ops:
  0.0 1.4 %dft_far.2 = (bf16[128,256]{1,0:T(8,128)(2,1)S(1)}, bf16[4,128,128]{2,1,0:T(8,128)(2,1)S(1)}, bf16[4,128,128]{2,1,0:T(8,128)(2,1)S(1)}) custom-call(bf16[4,256,4096]{2,1,0:T(8,128)(2,1)} %snap_ref.1), custom_call_target="tpu_custom_call" | custom-call | tf_op jit(solution)/shard_map/dft_far/pallas_call | solution.py:111
  1.4 0.0 copy-start
  1.4 0.0 copy-start.1
  1.4 1.9 %dft_far.3 = (bf16[4,128,384]{2,1,0:T(8,128)(2,1)S(1)}, bf16[4,128,384]{2,1,0:T(8,128)(2,1)S(1)}) custom-call(bf16[4,256,4096]{2,1,0:T(8,128)(2,1)} %snap_ref.1, bf16[128,256]{1,0:T(8,128)(2,1)S(1)} %get-tuple-element.17.refs_1_.table_ref), custom_call_target="tpu_custom_call" | custom-call | tf_op jit(solution)/shard_map/dft_far/pallas_call | solution.py:111
  3.4 5.0 %dft_rest.1 = (bf16[4,128,384]{2,1,0:T(8,128)(2,1)S(1)}, bf16[4,128,384]{2,1,0:T(8,128)(2,1)S(1)}, bf16[4,128,128]{2,1,0:T(8,128)(2,1)S(1)}, bf16[4,128,128]{2,1...) custom-call(bf16[128,256]{1,0:T(8,128)(2,1)S(1)} %get-tuple-element.17.refs_1_.table_ref, ...), custom_call_target="tpu_custom_call" | custom-call | flops 1073741824 | bytes 12582912 | tf_op jit(solution)/shard_map/dft_rest/pallas_call | solution.py:139
  8.4 0.6 collective-permute-start
  8.9 2.5 %collective-permute-start.1 = (bf16[4,128,128]{2,1,0:T(8,128)(2,1)S(1)}, bf16[4,128,128]{2,1,0:T(8,128)(2,1)S(1)}, u32[]{:S(2)}, u32[]{:S(2)}) collective-permute-start(bf16[4,128,128]{2,1,0:T(8,128)(2,1)S(1)} %get-tuple-element.21), channel_id=1, source_target_pairs={{0,2},{1,3},{2,0},{3,1},{4,6},{5,7},{6,4},{7,5},{8,10},{9,11},{10,... | collective-permute-start | bytes 393224 | tf_op jit(solution)/shard_map/ppermute | solution.py:346
  11.5 0.0 collective-permute-start.2
  11.5 1.7 %collective-permute-start.4 = (bf16[4,128,384]{2,1,0:T(8,128)(2,1)S(1)}, bf16[4,128,384]{2,1,0:T(8,128)(2,1)S(1)}, u32[]{:S(2)}, u32[]{:S(2)}) collective-permute-start(bf16[4,128,384]{2,1,0:T(8,128)(2,1)S(1)} %get-tuple-element.23), channel_id=1, source_target_pairs={{0,3},{1,2},{2,1},{3,0},{4,7},{5,6},{6,5},{7,4},{8,11},{9,10},{10,... | collective-permute-start | bytes 1179656 | tf_op jit(solution)/shard_map/ppermute | solution.py:346
  13.2 0.1 collective-permute-start.3
  13.3 2.5 %collective-permute-done.1.refs_4_ = bf16[4,128,128]{2,1,0:T(8,128)(2,1)S(1)} collective-permute-done((bf16[4,128,128]{2,1,0:T(8,128)(2,1)S(1)}, bf16[4,128,128]{2,1,0:T(8,128)(2,1)S(1)}, u32[]{:S(2)}, u32[]{:S(2)}) %collective-permute-start.1) | collective-permute-done | bytes 131104 | tf_op jit(solution)/shard_map/ppermute | solution.py:346
  15.8 2.0 %collective-permute-start.5 = (bf16[4,128,384]{2,1,0:T(8,128)(2,1)S(1)}, bf16[4,128,384]{2,1,0:T(8,128)(2,1)S(1)}, u32[]{:S(2)}, u32[]{:S(2)}) collective-permute-start(bf16[4,128,384]{2,1,0:T(8,128)(2,1)S(1)} %get-tuple-element.24), channel_id=1, source_target_pairs={{0,2},{1,3},{2,0},{3,1},{4,6},{5,7},{6,4},{7,5},{8,10},{9,11},{10,... | collective-permute-start | bytes 1179656 | tf_op jit(solution)/shard_map/ppermute | solution.py:346
  17.9 0.3 collective-permute-done.2.refs_5_
  18.2 2.2 %collective-permute-start.6 = (bf16[4,128,384]{2,1,0:T(8,128)(2,1)S(1)}, bf16[4,128,384]{2,1,0:T(8,128)(2,1)S(1)}, u32[]{:S(2)}, u32[]{:S(2)}) collective-permute-start(bf16[4,128,384]{2,1,0:T(8,128)(2,1)S(1)} %get-tuple-element.25), channel_id=1, source_target_pairs={{0,3},{1,2},{2,1},{3,0},{4,7},{5,6},{6,5},{7,4},{8,11},{9,10},{10,... | collective-permute-start | bytes 1179656 | tf_op jit(solution)/shard_map/ppermute | solution.py:346
  20.4 6.2 %collective-permute-done.4.refs_6_ = bf16[4,128,384]{2,1,0:T(8,128)(2,1)S(1)} collective-permute-done((bf16[4,128,384]{2,1,0:T(8,128)(2,1)S(1)}, bf16[4,128,384]{2,1,0:T(8,128)(2,1)S(1)}, u32[]{:S(2)}, u32[]{:S(2)}) %collective-permute-start.4) | collective-permute-done | bytes 393248 | tf_op jit(solution)/shard_map/ppermute | solution.py:346
  26.6 1.4 %collective-permute-start.7 = (bf16[4,128,128]{2,1,0:T(8,128)(2,1)S(1)}, bf16[4,128,128]{2,1,0:T(8,128)(2,1)S(1)}, u32[]{:S(2)}, u32[]{:S(2)}) collective-permute-start(bf16[4,128,128]{2,1,0:T(8,128)(2,1)S(1)} %get-tuple-element.26), channel_id=1, source_target_pairs={{0,2},{1,3},{2,0},{3,1},{4,6},{5,7},{6,4},{7,5},{8,10},{9,11},{10,... | collective-permute-start | bytes 393224 | tf_op jit(solution)/shard_map/ppermute | solution.py:346
  28.0 0.0 collective-permute-done.refs_3_.refs_4_.refs_1_
  28.0 0.5 collective-permute-start.8
  28.5 0.2 prepare.1.refs_3_
  28.7 0.0 copy-done
  28.7 0.0 copy-done.1
  28.7 1.5 %triads.4.refs_2_ = f32[16,16,128]{2,1,0:T(8,128)S(1)} custom-call(s32[2,64]{1,0:T(2,128)S(1)} %bitcast.6, f32[1,4096]{1,0:T(1,128)S(1)} %bitcast.2, bf16[4,128,1024]{2,1,0:T(8,128)(2,1)S(1)} %get-tuple-element.19.refs_2_.refs_3_.refs_0_, bf16[4,128,1024]{2,1,0:T(8,128)(2,1)S(1)} %collective-permute-done.refs_3_.refs_4_.refs_1_, ...), custom_call_target="tpu_custom_call" | custom-call | flops 67108864 | bytes 524288 | tf_op jit(solution)/shard_map/triads/pallas_call | solution.py:275
  30.2 5.3 %collective-permute-done.3.refs_5_ = bf16[4,128,384]{2,1,0:T(8,128)(2,1)S(1)} collective-permute-done((bf16[4,128,384]{2,1,0:T(8,128)(2,1)S(1)}, bf16[4,128,384]{2,1,0:T(8,128)(2,1)S(1)}, u32[]{:S(2)}, u32[]{:S(2)}) %collective-permute-start.3) | collective-permute-done | bytes 393248 | tf_op jit(solution)/shard_map/ppermute | solution.py:346
  35.5 2.9 %triads.5.refs_2_ = f32[16,16,128]{2,1,0:T(8,128)S(1)} custom-call(s32[2,64]{1,0:T(2,128)S(1)} %bitcast.7, f32[1,4096]{1,0:T(1,128)S(1)} %bitcast.3, f32[16,16,128]{2,1,0:T(8,128)S(1)} %triads.4.refs_2_, bf16[4,128,1024]{2,1,0:T(8,128)(2,1)S(1)} %get-tuple-element.19.refs_2_.refs_3_.refs_0_, ...), custom_call_target="tpu_custom_call" | custom-call | flops 201326592 | bytes 1572864 | tf_op jit(solution)/shard_map/triads/pallas_call | solution.py:275
  38.4 5.5 %collective-permute-done.5.refs_5_ = bf16[4,128,384]{2,1,0:T(8,128)(2,1)S(1)} collective-permute-done((bf16[4,128,384]{2,1,0:T(8,128)(2,1)S(1)}, bf16[4,128,384]{2,1,0:T(8,128)(2,1)S(1)}, u32[]{:S(2)}, u32[]{:S(2)}) %collective-permute-start.5) | collective-permute-done | bytes 393248 | tf_op jit(solution)/shard_map/ppermute | solution.py:346
  43.9 8.0 %collective-permute-done.6.refs_6_ = bf16[4,128,384]{2,1,0:T(8,128)(2,1)S(1)} collective-permute-done((bf16[4,128,384]{2,1,0:T(8,128)(2,1)S(1)}, bf16[4,128,384]{2,1,0:T(8,128)(2,1)S(1)}, u32[]{:S(2)}, u32[]{:S(2)}) %collective-permute-start.6) | collective-permute-done | bytes 393248 | tf_op jit(solution)/shard_map/ppermute | solution.py:346
  51.9 2.9 %triads.6.refs_2_ = f32[16,16,128]{2,1,0:T(8,128)S(1)} custom-call(s32[2,64]{1,0:T(2,128)S(1)} %bitcast.8, f32[1,4096]{1,0:T(1,128)S(1)} %bitcast.4, f32[16,16,128]{2,1,0:T(8,128)S(1)} %triads.5.refs_2_, bf16[4,128,1024]{2,1,0:T(8,128)(2,1)S(1)} %get-tuple-element.19.refs_2_.refs_3_.refs_0_, ...), custom_call_target="tpu_custom_call" | custom-call | flops 201326592 | bytes 1572864 | tf_op jit(solution)/shard_map/triads/pallas_call | solution.py:275
  54.8 0.4 collective-permute-done.7.refs_4_
  55.2 2.3 %collective-permute-done.8.refs_5_ = bf16[4,128,128]{2,1,0:T(8,128)(2,1)S(1)} collective-permute-done((bf16[4,128,128]{2,1,0:T(8,128)(2,1)S(1)}, bf16[4,128,128]{2,1,0:T(8,128)(2,1)S(1)}, u32[]{:S(2)}, u32[]{:S(2)}) %collective-permute-start.8) | collective-permute-done | bytes 131104 | tf_op jit(solution)/shard_map/ppermute | solution.py:346
  57.4 1.0 %triads.7 = (bf16[16,16,128]{2,1,0:T(8,128)(2,1)S(1)}, f32[1,2048,128]{2,1,0:T(8,128)S(1)}) custom-call(s32[2,64]{1,0:T(2,128)S(1)} %bitcast.9, f32[1,4096]{1,0:T(1,128)S(1)} %bitcast.5, f32[16,16,128]{2,1,0:T(8,128)S(1)} %triads.6.refs_2_, f32[1,2048,128]{2,1,0:T(8,128)S(1)} %prepare.1.refs_3_, ...), custom_call_target="tpu_custom_call", output_to_operand_aliasing={{1}: (3, {})} | custom-call | flops 67108864 | bytes 524288 | tf_op jit(solution)/shard_map/triads/pallas_call | solution.py:275
  58.5 12.6 %all_to_all.5.part_ref = bf16[16,16,128]{2,1,0:T(8,128)(2,1)S(1)} all-to-all(bf16[16,16,128]{2,1,0:T(8,128)(2,1)S(1)} %get-tuple-element.28), channel_id=1, replica_groups=mesh['groups'=2,'space'=4,'freq'=2,'band'=2] {'space','freq','band'}, dimensions={0} | all-to-all | bytes 131072 | tf_op jit(solution)/shard_map/all_to_all | solution.py:384
  71.1 0.8 %finish.1 = f32[4,512]{1,0:T(4,128)} custom-call(bf16[16,16,128]{2,1,0:T(8,128)(2,1)S(1)} %all_to_all.5.part_ref), custom_call_target="tpu_custom_call" | custom-call | tf_op jit(solution)/shard_map/finish/pallas_call | solution.py:315
Async XLA Ops:
  1.4 27.3 %copy-start = (f32[4096]{0:T(1024)S(1)}, f32[4096]{0:T(1024)}, u32[]{:S(2)}) copy-start(f32[4096]{0:T(1024)} %param.4) | copy-start | bytes 49156
  1.4 27.3 %copy-start.1 = (s32[64,2]{0,1:T(2,128)S(1)}, s32[64,2]{0,1:T(2,128)}, u32[]{:S(2)}) copy-start(s32[64,2]{0,1:T(2,128)} %param.5) | copy-start | bytes 1540
  8.4 19.6 %collective-permute-start = (bf16[4,128,1024]{2,1,0:T(8,128)(2,1)S(1)}, bf16[4,128,1024]{2,1,0:T(8,128)(2,1)S(1)}, u32[]{:S(2)}, u32[]{:S(2)}) collective-permute-start(bf16[4,128,1024]{2,1,0:T(8,128)(2,1)S(1)} %get-tuple-element.20), channel_id=1, source_target_pairs={{0,1},{1,0},{2,3},{3,2},{4,5},{5,4},{6,7},{7,6},{8,9},{9,8},{10,11... | collective-permute-start | bytes 3145736 | tf_op jit(solution)/shard_map/ppermute | solution.py:346
  8.9 6.9 %collective-permute-start.1 = (bf16[4,128,128]{2,1,0:T(8,128)(2,1)S(1)}, bf16[4,128,128]{2,1,0:T(8,128)(2,1)S(1)}, u32[]{:S(2)}, u32[]{:S(2)}) collective-permute-start(bf16[4,128,128]{2,1,0:T(8,128)(2,1)S(1)} %get-tuple-element.21), channel_id=1, source_target_pairs={{0,2},{1,3},{2,0},{3,1},{4,6},{5,7},{6,4},{7,5},{8,10},{9,11},{10,... | collective-permute-start | bytes 393224 | tf_op jit(solution)/shard_map/ppermute | solution.py:346
  11.5 6.7 %collective-permute-start.2 = (bf16[4,128,128]{2,1,0:T(8,128)(2,1)S(1)}, bf16[4,128,128]{2,1,0:T(8,128)(2,1)S(1)}, u32[]{:S(2)}, u32[]{:S(2)}) collective-permute-start(bf16[4,128,128]{2,1,0:T(8,128)(2,1)S(1)} %get-tuple-element.22), channel_id=1, source_target_pairs={{0,3},{1,2},{2,1},{3,0},{4,7},{5,6},{6,5},{7,4},{8,11},{9,10},{10,... | collective-permute-start | bytes 393224 | tf_op jit(solution)/shard_map/ppermute | solution.py:346
  11.5 15.1 %collective-permute-start.4 = (bf16[4,128,384]{2,1,0:T(8,128)(2,1)S(1)}, bf16[4,128,384]{2,1,0:T(8,128)(2,1)S(1)}, u32[]{:S(2)}, u32[]{:S(2)}) collective-permute-start(bf16[4,128,384]{2,1,0:T(8,128)(2,1)S(1)} %get-tuple-element.23), channel_id=1, source_target_pairs={{0,3},{1,2},{2,1},{3,0},{4,7},{5,6},{6,5},{7,4},{8,11},{9,10},{10,... | collective-permute-start | bytes 1179656 | tf_op jit(solution)/shard_map/ppermute | solution.py:346
  13.2 22.3 %collective-permute-start.3 = (bf16[4,128,384]{2,1,0:T(8,128)(2,1)S(1)}, bf16[4,128,384]{2,1,0:T(8,128)(2,1)S(1)}, u32[]{:S(2)}, u32[]{:S(2)}) collective-permute-start(bf16[4,128,384]{2,1,0:T(8,128)(2,1)S(1)} %get-tuple-element.18.after_ref), channel_id=1, source_target_pairs={{0,2},{1,3},{2,0},{3,1},{4,6},{5,7},{6,4},{7,5},{8,10},{9,11},{10,... | collective-permute-start | bytes 1179656 | tf_op jit(solution)/shard_map/ppermute | solution.py:346
  15.8 28.1 %collective-permute-start.5 = (bf16[4,128,384]{2,1,0:T(8,128)(2,1)S(1)}, bf16[4,128,384]{2,1,0:T(8,128)(2,1)S(1)}, u32[]{:S(2)}, u32[]{:S(2)}) collective-permute-start(bf16[4,128,384]{2,1,0:T(8,128)(2,1)S(1)} %get-tuple-element.24), channel_id=1, source_target_pairs={{0,2},{1,3},{2,0},{3,1},{4,6},{5,7},{6,4},{7,5},{8,10},{9,11},{10,... | collective-permute-start | bytes 1179656 | tf_op jit(solution)/shard_map/ppermute | solution.py:346
  18.2 33.7 %collective-permute-start.6 = (bf16[4,128,384]{2,1,0:T(8,128)(2,1)S(1)}, bf16[4,128,384]{2,1,0:T(8,128)(2,1)S(1)}, u32[]{:S(2)}, u32[]{:S(2)}) collective-permute-start(bf16[4,128,384]{2,1,0:T(8,128)(2,1)S(1)} %get-tuple-element.25), channel_id=1, source_target_pairs={{0,3},{1,2},{2,1},{3,0},{4,7},{5,6},{6,5},{7,4},{8,11},{9,10},{10,... | collective-permute-start | bytes 1179656 | tf_op jit(solution)/shard_map/ppermute | solution.py:346
  26.6 28.5 %collective-permute-start.7 = (bf16[4,128,128]{2,1,0:T(8,128)(2,1)S(1)}, bf16[4,128,128]{2,1,0:T(8,128)(2,1)S(1)}, u32[]{:S(2)}, u32[]{:S(2)}) collective-permute-start(bf16[4,128,128]{2,1,0:T(8,128)(2,1)S(1)} %get-tuple-element.26), channel_id=1, source_target_pairs={{0,2},{1,3},{2,0},{3,1},{4,6},{5,7},{6,4},{7,5},{8,10},{9,11},{10,... | collective-permute-start | bytes 393224 | tf_op jit(solution)/shard_map/ppermute | solution.py:346
  28.0 29.4 %collective-permute-start.8 = (bf16[4,128,128]{2,1,0:T(8,128)(2,1)S(1)}, bf16[4,128,128]{2,1,0:T(8,128)(2,1)S(1)}, u32[]{:S(2)}, u32[]{:S(2)}) collective-permute-start(bf16[4,128,128]{2,1,0:T(8,128)(2,1)S(1)} %get-tuple-element.27), channel_id=1, source_target_pairs={{0,3},{1,2},{2,1},{3,0},{4,7},{5,6},{6,5},{7,4},{8,11},{9,10},{10,... | collective-permute-start | bytes 393224 | tf_op jit(solution)/shard_map/ppermute | solution.py:346

commit v5 on v4

--- a/solution.py
+++ b/solution.py
@@ -17,6 +17,7 @@
 
 
 VMEM = pl.BlockSpec(memory_space=pltpu.VMEM)
+SMEM = pl.BlockSpec(memory_space=pltpu.SMEM)
 ANY = pl.BlockSpec(memory_space=pl.ANY)
 
 
@@ -170,32 +171,39 @@
 
 
 def prepare_kernel(sizes, near, offset, *refs):
-    for slot, source in zip(near, refs[:-1]):
-        interleave(refs[-1], source, slot, sizes, offset)
-
-
-def prepare(near_sources, sizes, near, offset, width):
+    ids_any, *sources = refs[:-3]
+    ids_ref, spec_ref, ids_arrived = refs[-3:]
+    ids_copy = pltpu.make_async_copy(ids_any, ids_ref, ids_arrived)
+    ids_copy.start()
+    for slot, source in zip(near, sources):
+        interleave(spec_ref, source, slot, sizes, offset)
+    ids_copy.wait()
+
+
+def prepare(ids, near_sources, sizes, near, offset, width):
     rows = near_sources[0].shape[1]
     return pl.pallas_call(
         functools.partial(prepare_kernel, sizes, near, offset),
-        out_shape=jax.ShapeDtypeStruct((width // LANES, rows * NB, LANES), jnp.float32),
-        in_specs=[VMEM] * len(near),
-        out_specs=VMEM,
+        out_shape=[
+            pltpu.SMEM(ids.shape, jnp.int32),
+            pltpu.VMEM((width // LANES, rows * NB, LANES), jnp.float32),
+        ],
+        in_specs=[ANY] + [VMEM] * len(near),
+        out_specs=[SMEM, VMEM],
+        scratch_shapes=[pltpu.SemaphoreType.DMA],
         compiler_params=pltpu.CompilerParams(vmem_limit_bytes=8 * MIB),
         name="prepare",
-    )(*near_sources)
+    )(ids, *near_sources)
 
 
 def triad_kernel(sizes, slots, offset, prepared, has_prior, scale, *refs):
-    ids_any, weights_ref = refs[:2]
+    ids_ref, weights_ref = refs[:2]
     rest = list(refs[2:])
     prior_ref = rest.pop(0) if has_prior else None
     if prepared:
         rest.pop(0)
     sources = [rest.pop(0) for _ in slots]
-    out_ref, spec_ref, ids_ref, ids_arrived = rest
-    ids_copy = pltpu.make_async_copy(ids_any, ids_ref, ids_arrived)
-    ids_copy.start()
+    out_ref, spec_ref = rest
     tiles = spec_ref.shape[0]
     own_points = weights_ref.shape[1] // (sizes[0] * sizes[1])
     here = shifted_part(0, 1, *sizes) * own_points + offset
@@ -206,7 +214,6 @@
         weights_ref[:, pl.ds(pl.multiple_of(here + tile * LANES, LANES), LANES)]
         for tile in range(tiles)
     ]
-    ids_copy.wait()
     lane = lax.broadcasted_iota(jnp.int32, (NB, LANES), 1)
 
     def one_pack(group, carry):
@@ -264,9 +271,9 @@
     aliases = {}
     kept = jnp.float32 if prepared is None else jnp.bfloat16
     out_shape = [jax.ShapeDtypeStruct((packs, NB, LANES), kept)]
-    scratch = [pltpu.SMEM(ids.shape, jnp.int32), pltpu.SemaphoreType.DMA]
+    scratch = []
     if prepared is None:
-        scratch = [pltpu.VMEM(spec_shape, jnp.float32)] + scratch
+        scratch.append(pltpu.VMEM(spec_shape, jnp.float32))
     else:
         aliases = {len(operands): 1}
         operands.append(prepared)
@@ -277,7 +284,7 @@
             triad_kernel, sizes, slots, offset, prepared is not None, prior is not None, scale
         ),
         out_shape=out_shape,
-        in_specs=[ANY] + [VMEM] * (len(operands) - 1),
+        in_specs=[SMEM] + [VMEM] * (len(operands) - 1),
         out_specs=[VMEM] * len(out_shape),
         scratch_shapes=scratch,
         input_output_aliases=aliases,
@@ -331,7 +338,6 @@
     widths = split_widths(own_points)
     offsets = [sum(widths[:i]) for i in range(len(widths))]
     scale = 1.0 / math.sqrt(points * lax.axis_size("space"))
-    ids = triads.T
     weights = weights.reshape(1, points)
 
     def send(value, slot):
@@ -365,14 +371,13 @@
         rest = rest[len(far) :]
     near_sources = send_all(rest, near)
 
+    ids, ready = prepare(triads.T, near_sources, sizes, near, offsets[-1], widths[-1])
     total = None
     for chunk, (offset, width) in enumerate(zip(offsets, widths)):
         slots = [(slot, 0) for slot in far]
         sources = arrived[chunk]
-        prepared = None
-        if chunk == len(widths) - 1:
-            prepared = prepare(near_sources, sizes, near, offset, width)
-        else:
+        prepared = ready if chunk == len(widths) - 1 else None
+        if prepared is None:
             slots = [(slot, offset) for slot in near] + slots
             sources = near_sources + sources
         total = triad_chunk(

time: 72.1 us -> 71.7 us (level)
  transfers between devices with their start and end apart: 9 -> 9, of which waited for: 8 -> 8; matrix products, arithmetic and copies ran while one was open for 0% -> 0% of each run, Pallas kernels for 10% -> 11%
where the time goes in v5:
time: 71.7 us; the launch traced here: 71.4 us
  waiting for transfers between devices  30.4 us (42%)
  Pallas kernels  17.3 us (24%)
  blocking collectives  12.6 us (18%)
  starting transfers between devices  11.1 us (15%)
    ppermute x9, waiting for transfers between devices, send(): return lax.ppermute(value, ('freq', 'band'), pairs)  30.4 us
    all_to_all x1, blocking collectives, mode_decomposition(): lax.all_to_all(total, axes, split_axis=0, concat_axis=0, tiled=True)  12.6 us
    ppermute x9, starting transfers between devices, send(): return lax.ppermute(value, ('freq', 'band'), pairs)  11.1 us
    pallas_call x4, Pallas kernels, triad_chunk(): pl.pallas_call(functools.partial(triad_kernel, sizes, slots, offset, prep...  7.63 us
    pallas_call x1, Pallas kernels, dft_rest(): pl.pallas_call(functools.partial(dft_rest_kernel, sizes, plan, points), o...  4.99 us
    pallas_call x2, Pallas kernels, dft_far(): pl.pallas_call(functools.partial(dft_far_kernel, sizes, far, points, offs...  3.34 us
  transfers between devices with their start and end apart: 9, of which 8 were waited for; matrix products, arithmetic and copies ran while one was open for 0% of the time, Pallas kernels for 11%

profile of v5, /device:TPU:0, one launch (start us, length us, event | category | flops | bytes accessed | tf_op | source)
XLA Modules:
  0.0 71.4 jit_solution(8650715999035608607)
XLA Ops:
  0.0 1.4 %dft_far.2 = (bf16[128,256]{1,0:T(8,128)(2,1)S(1)}, bf16[4,128,128]{2,1,0:T(8,128)(2,1)S(1)}, bf16[4,128,128]{2,1,0:T(8,128)(2,1)S(1)}) custom-call(bf16[4,256,4096]{2,1,0:T(8,128)(2,1)} %snap_ref.1), custom_call_target="tpu_custom_call" | custom-call | tf_op jit(solution)/shard_map/dft_far/pallas_call | solution.py:112
  1.4 0.0 copy-start.1
  1.4 0.0 copy-start
  1.4 1.9 %dft_far.3 = (bf16[4,128,384]{2,1,0:T(8,128)(2,1)S(1)}, bf16[4,128,384]{2,1,0:T(8,128)(2,1)S(1)}) custom-call(bf16[4,256,4096]{2,1,0:T(8,128)(2,1)} %snap_ref.1, bf16[128,256]{1,0:T(8,128)(2,1)S(1)} %get-tuple-element.19.refs_1_.table_ref), custom_call_target="tpu_custom_call" | custom-call | tf_op jit(solution)/shard_map/dft_far/pallas_call | solution.py:112
  3.4 5.0 %dft_rest.1 = (bf16[4,128,384]{2,1,0:T(8,128)(2,1)S(1)}, bf16[4,128,384]{2,1,0:T(8,128)(2,1)S(1)}, bf16[4,128,128]{2,1,0:T(8,128)(2,1)S(1)}, bf16[4,128,128]{2,1...) custom-call(bf16[128,256]{1,0:T(8,128)(2,1)S(1)} %get-tuple-element.19.refs_1_.table_ref, ...), custom_call_target="tpu_custom_call" | custom-call | flops 1073741824 | bytes 12582912 | tf_op jit(solution)/shard_map/dft_rest/pallas_call | solution.py:140
  8.4 0.6 collective-permute-start
  8.9 2.5 %collective-permute-start.1 = (bf16[4,128,128]{2,1,0:T(8,128)(2,1)S(1)}, bf16[4,128,128]{2,1,0:T(8,128)(2,1)S(1)}, u32[]{:S(2)}, u32[]{:S(2)}) collective-permute-start(bf16[4,128,128]{2,1,0:T(8,128)(2,1)S(1)} %get-tuple-element.24), channel_id=1, source_target_pairs={{0,2},{1,3},{2,0},{3,1},{4,6},{5,7},{6,4},{7,5},{8,10},{9,11},{10,... | collective-permute-start | bytes 393224 | tf_op jit(solution)/shard_map/ppermute | solution.py:352
  11.5 0.0 collective-permute-start.2
  11.5 1.7 %collective-permute-start.4 = (bf16[4,128,384]{2,1,0:T(8,128)(2,1)S(1)}, bf16[4,128,384]{2,1,0:T(8,128)(2,1)S(1)}, u32[]{:S(2)}, u32[]{:S(2)}) collective-permute-start(bf16[4,128,384]{2,1,0:T(8,128)(2,1)S(1)} %get-tuple-element.26), channel_id=1, source_target_pairs={{0,3},{1,2},{2,1},{3,0},{4,7},{5,6},{6,5},{7,4},{8,11},{9,10},{10,... | collective-permute-start | bytes 1179656 | tf_op jit(solution)/shard_map/ppermute | solution.py:352
  13.2 0.1 collective-permute-start.3
  13.3 2.5 %collective-permute-done.1.refs_4_ = bf16[4,128,128]{2,1,0:T(8,128)(2,1)S(1)} collective-permute-done((bf16[4,128,128]{2,1,0:T(8,128)(2,1)S(1)}, bf16[4,128,128]{2,1,0:T(8,128)(2,1)S(1)}, u32[]{:S(2)}, u32[]{:S(2)}) %collective-permute-start.1) | collective-permute-done | bytes 131104 | tf_op jit(solution)/shard_map/ppermute | solution.py:352
  15.8 2.0 %collective-permute-start.5 = (bf16[4,128,384]{2,1,0:T(8,128)(2,1)S(1)}, bf16[4,128,384]{2,1,0:T(8,128)(2,1)S(1)}, u32[]{:S(2)}, u32[]{:S(2)}) collective-permute-start(bf16[4,128,384]{2,1,0:T(8,128)(2,1)S(1)} %get-tuple-element.27), channel_id=1, source_target_pairs={{0,2},{1,3},{2,0},{3,1},{4,6},{5,7},{6,4},{7,5},{8,10},{9,11},{10,... | collective-permute-start | bytes 1179656 | tf_op jit(solution)/shard_map/ppermute | solution.py:352
  17.9 0.3 collective-permute-done.2.refs_5_
  18.2 2.2 %collective-permute-start.6 = (bf16[4,128,384]{2,1,0:T(8,128)(2,1)S(1)}, bf16[4,128,384]{2,1,0:T(8,128)(2,1)S(1)}, u32[]{:S(2)}, u32[]{:S(2)}) collective-permute-start(bf16[4,128,384]{2,1,0:T(8,128)(2,1)S(1)} %get-tuple-element.28), channel_id=1, source_target_pairs={{0,3},{1,2},{2,1},{3,0},{4,7},{5,6},{6,5},{7,4},{8,11},{9,10},{10,... | collective-permute-start | bytes 1179656 | tf_op jit(solution)/shard_map/ppermute | solution.py:352
  20.4 6.2 %collective-permute-done.4.refs_6_ = bf16[4,128,384]{2,1,0:T(8,128)(2,1)S(1)} collective-permute-done((bf16[4,128,384]{2,1,0:T(8,128)(2,1)S(1)}, bf16[4,128,384]{2,1,0:T(8,128)(2,1)S(1)}, u32[]{:S(2)}, u32[]{:S(2)}) %collective-permute-start.4) | collective-permute-done | bytes 393248 | tf_op jit(solution)/shard_map/ppermute | solution.py:352
  26.6 1.4 %collective-permute-start.7 = (bf16[4,128,128]{2,1,0:T(8,128)(2,1)S(1)}, bf16[4,128,128]{2,1,0:T(8,128)(2,1)S(1)}, u32[]{:S(2)}, u32[]{:S(2)}) collective-permute-start(bf16[4,128,128]{2,1,0:T(8,128)(2,1)S(1)} %get-tuple-element.30), channel_id=1, source_target_pairs={{0,2},{1,3},{2,0},{3,1},{4,6},{5,7},{6,4},{7,5},{8,10},{9,11},{10,... | collective-permute-start | bytes 393224 | tf_op jit(solution)/shard_map/ppermute | solution.py:352
  28.0 0.0 collective-permute-done.refs_2_.refs_3_.refs_4_
  28.0 0.5 collective-permute-start.8
  28.5 0.0 copy-done.1
  28.5 0.6 prepare.1
  29.1 0.0 copy-done
  29.1 1.2 %triads.4.refs_2_ = f32[16,16,128]{2,1,0:T(8,128)S(1)} custom-call(s32[2,64]{1,0:T(2,128)S(4)} %get-tuple-element.23.refs_0_, f32[1,4096]{1,0:T(1,128)S(1)} %bitcast.2, bf16[4,128,1024]{2,1,0:T(8,128)(2,1)S(1)} %get-tuple-element.21.refs_1_.refs_2_.refs_3_, bf16[4,128,1024]{2,1,0:T(8,128)(2,1)S(1)} %collective-permute-done.refs_2_.refs_3_.refs_4_, ...), custom_call_target="tpu_custom_call" | custom-call | flops 67108864 | bytes 524288 | tf_op jit(solution)/shard_map/triads/pallas_call | solution.py:282
  30.3 5.2 %collective-permute-done.3.refs_5_ = bf16[4,128,384]{2,1,0:T(8,128)(2,1)S(1)} collective-permute-done((bf16[4,128,384]{2,1,0:T(8,128)(2,1)S(1)}, bf16[4,128,384]{2,1,0:T(8,128)(2,1)S(1)}, u32[]{:S(2)}, u32[]{:S(2)}) %collective-permute-start.3) | collective-permute-done | bytes 393248 | tf_op jit(solution)/shard_map/ppermute | solution.py:352
  35.5 2.9 %triads.5.refs_2_ = f32[16,16,128]{2,1,0:T(8,128)S(1)} custom-call(s32[2,64]{1,0:T(2,128)S(4)} %get-tuple-element.23.refs_0_, f32[1,4096]{1,0:T(1,128)S(1)} %bitcast.3, f32[16,16,128]{2,1,0:T(8,128)S(1)} %triads.4.refs_2_, bf16[4,128,1024]{2,1,0:T(8,128)(2,1)S(1)} %get-tuple-element.21.refs_1_.refs_2_.refs_3_, ...), custom_call_target="tpu_custom_call" | custom-call | flops 201326592 | bytes 1572864 | tf_op jit(solution)/shard_map/triads/pallas_call | solution.py:282
  38.4 5.5 %collective-permute-done.5.refs_5_ = bf16[4,128,384]{2,1,0:T(8,128)(2,1)S(1)} collective-permute-done((bf16[4,128,384]{2,1,0:T(8,128)(2,1)S(1)}, bf16[4,128,384]{2,1,0:T(8,128)(2,1)S(1)}, u32[]{:S(2)}, u32[]{:S(2)}) %collective-permute-start.5) | collective-permute-done | bytes 393248 | tf_op jit(solution)/shard_map/ppermute | solution.py:352
  43.9 8.0 %collective-permute-done.6.refs_6_ = bf16[4,128,384]{2,1,0:T(8,128)(2,1)S(1)} collective-permute-done((bf16[4,128,384]{2,1,0:T(8,128)(2,1)S(1)}, bf16[4,128,384]{2,1,0:T(8,128)(2,1)S(1)}, u32[]{:S(2)}, u32[]{:S(2)}) %collective-permute-start.6) | collective-permute-done | bytes 393248 | tf_op jit(solution)/shard_map/ppermute | solution.py:352
  51.9 2.9 %triads.6.refs_2_ = f32[16,16,128]{2,1,0:T(8,128)S(1)} custom-call(s32[2,64]{1,0:T(2,128)S(4)} %get-tuple-element.23.refs_0_, f32[1,4096]{1,0:T(1,128)S(1)} %bitcast.4, f32[16,16,128]{2,1,0:T(8,128)S(1)} %triads.5.refs_2_, bf16[4,128,1024]{2,1,0:T(8,128)(2,1)S(1)} %get-tuple-element.21.refs_1_.refs_2_.refs_3_, ...), custom_call_target="tpu_custom_call" | custom-call | flops 201326592 | bytes 1572864 | tf_op jit(solution)/shard_map/triads/pallas_call | solution.py:282
  54.8 0.4 collective-permute-done.7.refs_4_
  55.2 2.3 %collective-permute-done.8.refs_5_ = bf16[4,128,128]{2,1,0:T(8,128)(2,1)S(1)} collective-permute-done((bf16[4,128,128]{2,1,0:T(8,128)(2,1)S(1)}, bf16[4,128,128]{2,1,0:T(8,128)(2,1)S(1)}, u32[]{:S(2)}, u32[]{:S(2)}) %collective-permute-start.8) | collective-permute-done | bytes 131104 | tf_op jit(solution)/shard_map/ppermute | solution.py:352
  57.4 0.6 triads.7
  58.1 12.6 %all_to_all.5.part_ref = bf16[16,16,128]{2,1,0:T(8,128)(2,1)S(1)} all-to-all(bf16[16,16,128]{2,1,0:T(8,128)(2,1)S(1)} %get-tuple-element.32), channel_id=1, replica_groups=mesh['groups'=2,'space'=4,'freq'=2,'band'=2] {'space','freq','band'}, dimensions={0} | all-to-all | bytes 131072 | tf_op jit(solution)/shard_map/all_to_all | solution.py:389
  70.7 0.8 %finish.1 = f32[4,512]{1,0:T(4,128)} custom-call(bf16[16,16,128]{2,1,0:T(8,128)(2,1)S(1)} %all_to_all.5.part_ref), custom_call_target="tpu_custom_call" | custom-call | tf_op jit(solution)/shard_map/finish/pallas_call | solution.py:322
Async XLA Ops:
  1.4 27.1 %copy-start.1 = (s32[64,2]{0,1:T(2,128)S(1)}, s32[64,2]{0,1:T(2,128)}, u32[]{:S(2)}) copy-start(s32[64,2]{0,1:T(2,128)} %param.5) | copy-start | bytes 1540
  1.4 27.7 %copy-start = (f32[4096]{0:T(1024)S(1)}, f32[4096]{0:T(1024)}, u32[]{:S(2)}) copy-start(f32[4096]{0:T(1024)} %param.4) | copy-start | bytes 49156
  8.4 19.6 %collective-permute-start = (bf16[4,128,1024]{2,1,0:T(8,128)(2,1)S(1)}, bf16[4,128,1024]{2,1,0:T(8,128)(2,1)S(1)}, u32[]{:S(2)}, u32[]{:S(2)}) collective-permute-start(bf16[4,128,1024]{2,1,0:T(8,128)(2,1)S(1)} %get-tuple-element.22), channel_id=1, source_target_pairs={{0,1},{1,0},{2,3},{3,2},{4,5},{5,4},{6,7},{7,6},{8,9},{9,8},{10,11... | collective-permute-start | bytes 3145736 | tf_op jit(solution)/shard_map/ppermute | solution.py:352
  8.9 6.9 %collective-permute-start.1 = (bf16[4,128,128]{2,1,0:T(8,128)(2,1)S(1)}, bf16[4,128,128]{2,1,0:T(8,128)(2,1)S(1)}, u32[]{:S(2)}, u32[]{:S(2)}) collective-permute-start(bf16[4,128,128]{2,1,0:T(8,128)(2,1)S(1)} %get-tuple-element.24), channel_id=1, source_target_pairs={{0,2},{1,3},{2,0},{3,1},{4,6},{5,7},{6,4},{7,5},{8,10},{9,11},{10,... | collective-permute-start | bytes 393224 | tf_op jit(solution)/shard_map/ppermute | solution.py:352
  11.5 6.7 %collective-permute-start.2 = (bf16[4,128,128]{2,1,0:T(8,128)(2,1)S(1)}, bf16[4,128,128]{2,1,0:T(8,128)(2,1)S(1)}, u32[]{:S(2)}, u32[]{:S(2)}) collective-permute-start(bf16[4,128,128]{2,1,0:T(8,128)(2,1)S(1)} %get-tuple-element.25), channel_id=1, source_target_pairs={{0,3},{1,2},{2,1},{3,0},{4,7},{5,6},{6,5},{7,4},{8,11},{9,10},{10,... | collective-permute-start | bytes 393224 | tf_op jit(solution)/shard_map/ppermute | solution.py:352
  11.5 15.1 %collective-permute-start.4 = (bf16[4,128,384]{2,1,0:T(8,128)(2,1)S(1)}, bf16[4,128,384]{2,1,0:T(8,128)(2,1)S(1)}, u32[]{:S(2)}, u32[]{:S(2)}) collective-permute-start(bf16[4,128,384]{2,1,0:T(8,128)(2,1)S(1)} %get-tuple-element.26), channel_id=1, source_target_pairs={{0,3},{1,2},{2,1},{3,0},{4,7},{5,6},{6,5},{7,4},{8,11},{9,10},{10,... | collective-permute-start | bytes 1179656 | tf_op jit(solution)/shard_map/ppermute | solution.py:352
  13.2 22.3 %collective-permute-start.3 = (bf16[4,128,384]{2,1,0:T(8,128)(2,1)S(1)}, bf16[4,128,384]{2,1,0:T(8,128)(2,1)S(1)}, u32[]{:S(2)}, u32[]{:S(2)}) collective-permute-start(bf16[4,128,384]{2,1,0:T(8,128)(2,1)S(1)} %get-tuple-element.20.after_ref), channel_id=1, source_target_pairs={{0,2},{1,3},{2,0},{3,1},{4,6},{5,7},{6,4},{7,5},{8,10},{9,11},{10,... | collective-permute-start | bytes 1179656 | tf_op jit(solution)/shard_map/ppermute | solution.py:352
  15.8 28.1 %collective-permute-start.5 = (bf16[4,128,384]{2,1,0:T(8,128)(2,1)S(1)}, bf16[4,128,384]{2,1,0:T(8,128)(2,1)S(1)}, u32[]{:S(2)}, u32[]{:S(2)}) collective-permute-start(bf16[4,128,384]{2,1,0:T(8,128)(2,1)S(1)} %get-tuple-element.27), channel_id=1, source_target_pairs={{0,2},{1,3},{2,0},{3,1},{4,6},{5,7},{6,4},{7,5},{8,10},{9,11},{10,... | collective-permute-start | bytes 1179656 | tf_op jit(solution)/shard_map/ppermute | solution.py:352
  18.2 33.7 %collective-permute-start.6 = (bf16[4,128,384]{2,1,0:T(8,128)(2,1)S(1)}, bf16[4,128,384]{2,1,0:T(8,128)(2,1)S(1)}, u32[]{:S(2)}, u32[]{:S(2)}) collective-permute-start(bf16[4,128,384]{2,1,0:T(8,128)(2,1)S(1)} %get-tuple-element.28), channel_id=1, source_target_pairs={{0,3},{1,2},{2,1},{3,0},{4,7},{5,6},{6,5},{7,4},{8,11},{9,10},{10,... | collective-permute-start | bytes 1179656 | tf_op jit(solution)/shard_map/ppermute | solution.py:352
  26.6 28.5 %collective-permute-start.7 = (bf16[4,128,128]{2,1,0:T(8,128)(2,1)S(1)}, bf16[4,128,128]{2,1,0:T(8,128)(2,1)S(1)}, u32[]{:S(2)}, u32[]{:S(2)}) collective-permute-start(bf16[4,128,128]{2,1,0:T(8,128)(2,1)S(1)} %get-tuple-element.30), channel_id=1, source_target_pairs={{0,2},{1,3},{2,0},{3,1},{4,6},{5,7},{6,4},{7,5},{8,10},{9,11},{10,... | collective-permute-start | bytes 393224 | tf_op jit(solution)/shard_map/ppermute | solution.py:352
  28.0 29.4 %collective-permute-start.8 = (bf16[4,128,128]{2,1,0:T(8,128)(2,1)S(1)}, bf16[4,128,128]{2,1,0:T(8,128)(2,1)S(1)}, u32[]{:S(2)}, u32[]{:S(2)}) collective-permute-start(bf16[4,128,128]{2,1,0:T(8,128)(2,1)S(1)} %get-tuple-element.31), channel_id=1, source_target_pairs={{0,3},{1,2},{2,1},{3,0},{4,7},{5,6},{6,5},{7,4},{8,11},{9,10},{10,... | collective-permute-start | bytes 393224 | tf_op jit(solution)/shard_map/ppermute | solution.py:352

commit v6 on v5

--- a/solution.py
+++ b/solution.py
@@ -356,8 +356,10 @@
 
     near = list(range(bands))
     far = list(range(bands, shards))
-    table, *outs = dft_far(snapshots, None, sizes, far, own_points, 0, widths[0])
-    arrived = [send_all(outs, far)]
+    table, *outs = dft_far(snapshots, None, sizes, far[:1], own_points, 0, widths[0])
+    arrived = [send_all(outs, far[:1])]
+    outs = dft_far(snapshots, table, sizes, far[1:], own_points, 0, widths[0])
+    arrived[0] += send_all(outs, far[1:])
     outs = dft_far(snapshots, table, sizes, far, own_points, offsets[1], widths[1])
     arrived.append(send_all(outs, far))
     plan = [

time: 71.7 us -> 72.6 us (1.013)
  waiting for transfers between devices: 30.4 us -> 32.8 us
  starting transfers between devices: 11.1 us -> 8.81 us
  Pallas kernels: 17.3 us -> 18.3 us
    ppermute x9, waiting for transfers between devices: 30.4 us -> 32.8 us  [send(): return lax.ppermute(value, ('freq', 'band'), pairs)]
    ppermute x9, starting transfers between devices: 11.1 us -> 8.81 us  [send(): return lax.ppermute(value, ('freq', 'band'), pairs)]
    pallas_call x2 -> x3, Pallas kernels: 3.34 us -> 4.28 us  [dft_far(): pl.pallas_call(functools.partial(dft_far_kernel, sizes, far, points, offs...]
  transfers between devices with their start and end apart: 9 -> 9, of which waited for: 8 -> 8; matrix products, arithmetic and copies ran while one was open for 0% -> 0% of each run, Pallas kernels for 11% -> 12%
where the time goes in v6:
time: 72.6 us; the launch traced here: 72.3 us
  waiting for transfers between devices  32.8 us (45%)
  Pallas kernels  18.3 us (25%)
  blocking collectives  12.4 us (17%)
  starting transfers between devices  8.81 us (12%)
    ppermute x9, waiting for transfers between devices, send(): return lax.ppermute(value, ('freq', 'band'), pairs)  32.8 us
    all_to_all x1, blocking collectives, mode_decomposition(): lax.all_to_all(total, axes, split_axis=0, concat_axis=0, tiled=True)  12.4 us
    ppermute x9, starting transfers between devices, send(): return lax.ppermute(value, ('freq', 'band'), pairs)  8.81 us
    pallas_call x4, Pallas kernels, triad_chunk(): pl.pallas_call(functools.partial(triad_kernel, sizes, slots, offset, prep...  7.63 us
    pallas_call x1, Pallas kernels, dft_rest(): pl.pallas_call(functools.partial(dft_rest_kernel, sizes, plan, points), o...  5 us
    pallas_call x3, Pallas kernels, dft_far(): pl.pallas_call(functools.partial(dft_far_kernel, sizes, far, points, offs...  4.28 us
  transfers between devices with their start and end apart: 9, of which 8 were waited for; matrix products, arithmetic and copies ran while one was open for 0% of the time, Pallas kernels for 12%

profile of v6, /device:TPU:0, one launch (start us, length us, event | category | flops | bytes accessed | tf_op | source)
XLA Modules:
  0.0 72.3 jit_solution(15034416175696112244)
XLA Ops:
  0.0 1.2 %dft_far.3 = (bf16[128,256]{1,0:T(8,128)(2,1)S(1)}, bf16[4,128,128]{2,1,0:T(8,128)(2,1)S(1)}) custom-call(bf16[4,256,4096]{2,1,0:T(8,128)(2,1)} %refs_0_.5), custom_call_target="tpu_custom_call" | custom-call | tf_op jit(solution)/shard_map/dft_far/pallas_call | solution.py:112
  1.2 1.9 %dft_far.4 = (bf16[4,128,384]{2,1,0:T(8,128)(2,1)S(1)}, bf16[4,128,384]{2,1,0:T(8,128)(2,1)S(1)}) custom-call(bf16[4,256,4096]{2,1,0:T(8,128)(2,1)} %refs_0_.5, bf16[128,256]{1,0:T(8,128)(2,1)S(1)} %get-tuple-element.18.refs_1_.table_ref), custom_call_target="tpu_custom_call" | custom-call | tf_op jit(solution)/shard_map/dft_far/pallas_call | solution.py:112
  3.1 0.0 copy-start.1
  3.1 0.0 copy-start
  3.2 5.0 %dft_rest.1 = (bf16[4,128,384]{2,1,0:T(8,128)(2,1)S(1)}, bf16[4,128,384]{2,1,0:T(8,128)(2,1)S(1)}, bf16[4,128,128]{2,1,0:T(8,128)(2,1)S(1)}, bf16[4,128,128]{2,1...) custom-call(bf16[128,256]{1,0:T(8,128)(2,1)S(1)} %get-tuple-element.18.refs_1_.table_ref, ...), custom_call_target="tpu_custom_call" | custom-call | flops 1073741824 | bytes 12582912 | tf_op jit(solution)/shard_map/dft_rest/pallas_call | solution.py:140
  8.2 0.6 collective-permute-start
  8.7 1.2 %dft_far.5 = bf16[4,128,128]{2,1,0:T(8,128)(2,1)S(1)} custom-call(bf16[4,256,4096]{2,1,0:T(8,128)(2,1)} %refs_0_.5, bf16[128,256]{1,0:T(8,128)(2,1)S(1)} %get-tuple-element.18.refs_1_.table_ref), custom_call_target="tpu_custom_call" | custom-call | tf_op jit(solution)/shard_map/dft_far/pallas_call | solution.py:112
  9.9 2.6 %collective-permute-start.2 = (bf16[4,128,128]{2,1,0:T(8,128)(2,1)S(1)}, bf16[4,128,128]{2,1,0:T(8,128)(2,1)S(1)}, u32[]{:S(2)}, u32[]{:S(2)}) collective-permute-start(bf16[4,128,128]{2,1,0:T(8,128)(2,1)S(1)} %dft_far.5), channel_id=1, source_target_pairs={{0,3},{1,2},{2,1},{3,0},{4,7},{5,6},{6,5},{7,4},{8,11},{9,10},{10,... | collective-permute-start | bytes 393224 | tf_op jit(solution)/shard_map/ppermute | solution.py:352
  12.5 0.0 collective-permute-start.1
  12.5 1.4 %collective-permute-start.4 = (bf16[4,128,384]{2,1,0:T(8,128)(2,1)S(1)}, bf16[4,128,384]{2,1,0:T(8,128)(2,1)S(1)}, u32[]{:S(2)}, u32[]{:S(2)}) collective-permute-start(bf16[4,128,384]{2,1,0:T(8,128)(2,1)S(1)} %get-tuple-element.24), channel_id=1, source_target_pairs={{0,3},{1,2},{2,1},{3,0},{4,7},{5,6},{6,5},{7,4},{8,11},{9,10},{10,... | collective-permute-start | bytes 1179656 | tf_op jit(solution)/shard_map/ppermute | solution.py:352
  13.9 0.7 collective-permute-start.3
  14.6 1.9 %collective-permute-done.2.refs_5_ = bf16[4,128,128]{2,1,0:T(8,128)(2,1)S(1)} collective-permute-done((bf16[4,128,128]{2,1,0:T(8,128)(2,1)S(1)}, bf16[4,128,128]{2,1,0:T(8,128)(2,1)S(1)}, u32[]{:S(2)}, u32[]{:S(2)}) %collective-permute-start.2) | collective-permute-done | bytes 131104 | tf_op jit(solution)/shard_map/ppermute | solution.py:352
  16.4 1.2 %collective-permute-start.5 = (bf16[4,128,384]{2,1,0:T(8,128)(2,1)S(1)}, bf16[4,128,384]{2,1,0:T(8,128)(2,1)S(1)}, u32[]{:S(2)}, u32[]{:S(2)}) collective-permute-start(bf16[4,128,384]{2,1,0:T(8,128)(2,1)S(1)} %get-tuple-element.25), channel_id=1, source_target_pairs={{0,2},{1,3},{2,0},{3,1},{4,6},{5,7},{6,4},{7,5},{8,10},{9,11},{10,... | collective-permute-start | bytes 1179656 | tf_op jit(solution)/shard_map/ppermute | solution.py:352
  17.6 2.0 %collective-permute-done.1.refs_4_ = bf16[4,128,128]{2,1,0:T(8,128)(2,1)S(1)} collective-permute-done((bf16[4,128,128]{2,1,0:T(8,128)(2,1)S(1)}, bf16[4,128,128]{2,1,0:T(8,128)(2,1)S(1)}, u32[]{:S(2)}, u32[]{:S(2)}) %collective-permute-start.1) | collective-permute-done | bytes 131104 | tf_op jit(solution)/shard_map/ppermute | solution.py:352
  19.6 0.5 collective-permute-start.6
  20.1 7.5 %collective-permute-done.4.refs_6_ = bf16[4,128,384]{2,1,0:T(8,128)(2,1)S(1)} collective-permute-done((bf16[4,128,384]{2,1,0:T(8,128)(2,1)S(1)}, bf16[4,128,384]{2,1,0:T(8,128)(2,1)S(1)}, u32[]{:S(2)}, u32[]{:S(2)}) %collective-permute-start.4) | collective-permute-done | bytes 393248 | tf_op jit(solution)/shard_map/ppermute | solution.py:352
  27.7 1.2 %collective-permute-start.7 = (bf16[4,128,128]{2,1,0:T(8,128)(2,1)S(1)}, bf16[4,128,128]{2,1,0:T(8,128)(2,1)S(1)}, u32[]{:S(2)}, u32[]{:S(2)}) collective-permute-start(bf16[4,128,128]{2,1,0:T(8,128)(2,1)S(1)} %get-tuple-element.28), channel_id=1, source_target_pairs={{0,2},{1,3},{2,0},{3,1},{4,6},{5,7},{6,4},{7,5},{8,10},{9,11},{10,... | collective-permute-start | bytes 393224 | tf_op jit(solution)/shard_map/ppermute | solution.py:352
  28.8 0.0 collective-permute-done.refs_2_.refs_3_.refs_4_
  28.8 0.8 %collective-permute-start.8 = (bf16[4,128,128]{2,1,0:T(8,128)(2,1)S(1)}, bf16[4,128,128]{2,1,0:T(8,128)(2,1)S(1)}, u32[]{:S(2)}, u32[]{:S(2)}) collective-permute-start(bf16[4,128,128]{2,1,0:T(8,128)(2,1)S(1)} %get-tuple-element.29), channel_id=1, source_target_pairs={{0,3},{1,2},{2,1},{3,0},{4,7},{5,6},{6,5},{7,4},{8,11},{9,10},{10,... | collective-permute-start | bytes 393224 | tf_op jit(solution)/shard_map/ppermute | solution.py:352
  29.6 0.0 copy-done.1
  29.6 0.6 prepare.1
  30.2 0.0 copy-done
  30.2 1.2 %triads.4.refs_2_ = f32[16,16,128]{2,1,0:T(8,128)S(1)} custom-call(s32[2,64]{1,0:T(2,128)S(4)} %get-tuple-element.22.refs_0_, f32[1,4096]{1,0:T(1,128)S(1)} %bitcast.2, bf16[4,128,1024]{2,1,0:T(8,128)(2,1)S(1)} %get-tuple-element.20.refs_1_.refs_2_.refs_3_, bf16[4,128,1024]{2,1,0:T(8,128)(2,1)S(1)} %collective-permute-done.refs_2_.refs_3_.refs_4_, ...), custom_call_target="tpu_custom_call" | custom-call | flops 67108864 | bytes 524288 | tf_op jit(solution)/shard_map/triads/pallas_call | solution.py:282
  31.4 5.1 %collective-permute-done.3.refs_5_ = bf16[4,128,384]{2,1,0:T(8,128)(2,1)S(1)} collective-permute-done((bf16[4,128,384]{2,1,0:T(8,128)(2,1)S(1)}, bf16[4,128,384]{2,1,0:T(8,128)(2,1)S(1)}, u32[]{:S(2)}, u32[]{:S(2)}) %collective-permute-start.3) | collective-permute-done | bytes 393248 | tf_op jit(solution)/shard_map/ppermute | solution.py:352
  36.5 2.9 %triads.5.refs_2_ = f32[16,16,128]{2,1,0:T(8,128)S(1)} custom-call(s32[2,64]{1,0:T(2,128)S(4)} %get-tuple-element.22.refs_0_, f32[1,4096]{1,0:T(1,128)S(1)} %bitcast.3, f32[16,16,128]{2,1,0:T(8,128)S(1)} %triads.4.refs_2_, bf16[4,128,1024]{2,1,0:T(8,128)(2,1)S(1)} %get-tuple-element.20.refs_1_.refs_2_.refs_3_, ...), custom_call_target="tpu_custom_call" | custom-call | flops 201326592 | bytes 1572864 | tf_op jit(solution)/shard_map/triads/pallas_call | solution.py:282
  39.4 5.5 %collective-permute-done.5.refs_5_ = bf16[4,128,384]{2,1,0:T(8,128)(2,1)S(1)} collective-permute-done((bf16[4,128,384]{2,1,0:T(8,128)(2,1)S(1)}, bf16[4,128,384]{2,1,0:T(8,128)(2,1)S(1)}, u32[]{:S(2)}, u32[]{:S(2)}) %collective-permute-start.5) | collective-permute-done | bytes 393248 | tf_op jit(solution)/shard_map/ppermute | solution.py:352
  44.9 8.1 %collective-permute-done.6.refs_6_ = bf16[4,128,384]{2,1,0:T(8,128)(2,1)S(1)} collective-permute-done((bf16[4,128,384]{2,1,0:T(8,128)(2,1)S(1)}, bf16[4,128,384]{2,1,0:T(8,128)(2,1)S(1)}, u32[]{:S(2)}, u32[]{:S(2)}) %collective-permute-start.6) | collective-permute-done | bytes 393248 | tf_op jit(solution)/shard_map/ppermute | solution.py:352
  52.9 2.9 %triads.6.refs_2_ = f32[16,16,128]{2,1,0:T(8,128)S(1)} custom-call(s32[2,64]{1,0:T(2,128)S(4)} %get-tuple-element.22.refs_0_, f32[1,4096]{1,0:T(1,128)S(1)} %bitcast.4, f32[16,16,128]{2,1,0:T(8,128)S(1)} %triads.5.refs_2_, bf16[4,128,1024]{2,1,0:T(8,128)(2,1)S(1)} %get-tuple-element.20.refs_1_.refs_2_.refs_3_, ...), custom_call_target="tpu_custom_call" | custom-call | flops 201326592 | bytes 1572864 | tf_op jit(solution)/shard_map/triads/pallas_call | solution.py:282
  55.8 0.3 collective-permute-done.7.refs_4_
  56.1 2.4 %collective-permute-done.8.refs_5_ = bf16[4,128,128]{2,1,0:T(8,128)(2,1)S(1)} collective-permute-done((bf16[4,128,128]{2,1,0:T(8,128)(2,1)S(1)}, bf16[4,128,128]{2,1,0:T(8,128)(2,1)S(1)}, u32[]{:S(2)}, u32[]{:S(2)}) %collective-permute-start.8) | collective-permute-done | bytes 131104 | tf_op jit(solution)/shard_map/ppermute | solution.py:352
  58.5 0.6 triads.7
  59.2 12.4 %all_to_all.5.part_ref = bf16[16,16,128]{2,1,0:T(8,128)(2,1)S(1)} all-to-all(bf16[16,16,128]{2,1,0:T(8,128)(2,1)S(1)} %get-tuple-element.30), channel_id=1, replica_groups=mesh['groups'=2,'space'=4,'freq'=2,'band'=2] {'space','freq','band'}, dimensions={0} | all-to-all | bytes 131072 | tf_op jit(solution)/shard_map/all_to_all | solution.py:391
  71.6 0.8 %finish.1 = f32[4,512]{1,0:T(4,128)} custom-call(bf16[16,16,128]{2,1,0:T(8,128)(2,1)S(1)} %all_to_all.5.part_ref), custom_call_target="tpu_custom_call" | custom-call | tf_op jit(solution)/shard_map/finish/pallas_call | solution.py:322
Async XLA Ops:
  3.1 26.4 %copy-start.1 = (s32[64,2]{0,1:T(2,128)S(1)}, s32[64,2]{0,1:T(2,128)}, u32[]{:S(2)}) copy-start(s32[64,2]{0,1:T(2,128)} %param.5) | copy-start | bytes 1540
  3.1 27.0 %copy-start = (f32[4096]{0:T(1024)S(1)}, f32[4096]{0:T(1024)}, u32[]{:S(2)}) copy-start(f32[4096]{0:T(1024)} %param.4) | copy-start | bytes 49156
  8.2 20.7 %collective-permute-start = (bf16[4,128,1024]{2,1,0:T(8,128)(2,1)S(1)}, bf16[4,128,1024]{2,1,0:T(8,128)(2,1)S(1)}, u32[]{:S(2)}, u32[]{:S(2)}) collective-permute-start(bf16[4,128,1024]{2,1,0:T(8,128)(2,1)S(1)} %get-tuple-element.21), channel_id=1, source_target_pairs={{0,1},{1,0},{2,3},{3,2},{4,5},{5,4},{6,7},{7,6},{8,9},{9,8},{10,11... | collective-permute-start | bytes 3145736 | tf_op jit(solution)/shard_map/ppermute | solution.py:352
  9.9 6.5 %collective-permute-start.2 = (bf16[4,128,128]{2,1,0:T(8,128)(2,1)S(1)}, bf16[4,128,128]{2,1,0:T(8,128)(2,1)S(1)}, u32[]{:S(2)}, u32[]{:S(2)}) collective-permute-start(bf16[4,128,128]{2,1,0:T(8,128)(2,1)S(1)} %dft_far.5), channel_id=1, source_target_pairs={{0,3},{1,2},{2,1},{3,0},{4,7},{5,6},{6,5},{7,4},{8,11},{9,10},{10,... | collective-permute-start | bytes 393224 | tf_op jit(solution)/shard_map/ppermute | solution.py:352
  12.5 7.1 %collective-permute-start.1 = (bf16[4,128,128]{2,1,0:T(8,128)(2,1)S(1)}, bf16[4,128,128]{2,1,0:T(8,128)(2,1)S(1)}, u32[]{:S(2)}, u32[]{:S(2)}) collective-permute-start(bf16[4,128,128]{2,1,0:T(8,128)(2,1)S(1)} %get-tuple-element.23), channel_id=1, source_target_pairs={{0,2},{1,3},{2,0},{3,1},{4,6},{5,7},{6,4},{7,5},{8,10},{9,11},{10,... | collective-permute-start | bytes 393224 | tf_op jit(solution)/shard_map/ppermute | solution.py:352
  12.5 15.1 %collective-permute-start.4 = (bf16[4,128,384]{2,1,0:T(8,128)(2,1)S(1)}, bf16[4,128,384]{2,1,0:T(8,128)(2,1)S(1)}, u32[]{:S(2)}, u32[]{:S(2)}) collective-permute-start(bf16[4,128,384]{2,1,0:T(8,128)(2,1)S(1)} %get-tuple-element.24), channel_id=1, source_target_pairs={{0,3},{1,2},{2,1},{3,0},{4,7},{5,6},{6,5},{7,4},{8,11},{9,10},{10,... | collective-permute-start | bytes 1179656 | tf_op jit(solution)/shard_map/ppermute | solution.py:352
  13.9 22.5 %collective-permute-start.3 = (bf16[4,128,384]{2,1,0:T(8,128)(2,1)S(1)}, bf16[4,128,384]{2,1,0:T(8,128)(2,1)S(1)}, u32[]{:S(2)}, u32[]{:S(2)}) collective-permute-start(bf16[4,128,384]{2,1,0:T(8,128)(2,1)S(1)} %get-tuple-element.19.after_ref), channel_id=1, source_target_pairs={{0,2},{1,3},{2,0},{3,1},{4,6},{5,7},{6,4},{7,5},{8,10},{9,11},{10,... | collective-permute-start | bytes 1179656 | tf_op jit(solution)/shard_map/ppermute | solution.py:352
  16.4 28.5 %collective-permute-start.5 = (bf16[4,128,384]{2,1,0:T(8,128)(2,1)S(1)}, bf16[4,128,384]{2,1,0:T(8,128)(2,1)S(1)}, u32[]{:S(2)}, u32[]{:S(2)}) collective-permute-start(bf16[4,128,384]{2,1,0:T(8,128)(2,1)S(1)} %get-tuple-element.25), channel_id=1, source_target_pairs={{0,2},{1,3},{2,0},{3,1},{4,6},{5,7},{6,4},{7,5},{8,10},{9,11},{10,... | collective-permute-start | bytes 1179656 | tf_op jit(solution)/shard_map/ppermute | solution.py:352
  19.6 33.3 %collective-permute-start.6 = (bf16[4,128,384]{2,1,0:T(8,128)(2,1)S(1)}, bf16[4,128,384]{2,1,0:T(8,128)(2,1)S(1)}, u32[]{:S(2)}, u32[]{:S(2)}) collective-permute-start(bf16[4,128,384]{2,1,0:T(8,128)(2,1)S(1)} %get-tuple-element.26), channel_id=1, source_target_pairs={{0,3},{1,2},{2,1},{3,0},{4,7},{5,6},{6,5},{7,4},{8,11},{9,10},{10,... | collective-permute-start | bytes 1179656 | tf_op jit(solution)/shard_map/ppermute | solution.py:352
  27.7 28.5 %collective-permute-start.7 = (bf16[4,128,128]{2,1,0:T(8,128)(2,1)S(1)}, bf16[4,128,128]{2,1,0:T(8,128)(2,1)S(1)}, u32[]{:S(2)}, u32[]{:S(2)}) collective-permute-start(bf16[4,128,128]{2,1,0:T(8,128)(2,1)S(1)} %get-tuple-element.28), channel_id=1, source_target_pairs={{0,2},{1,3},{2,0},{3,1},{4,6},{5,7},{6,4},{7,5},{8,10},{9,11},{10,... | collective-permute-start | bytes 393224 | tf_op jit(solution)/shard_map/ppermute | solution.py:352
  28.8 29.7 %collective-permute-start.8 = (bf16[4,128,128]{2,1,0:T(8,128)(2,1)S(1)}, bf16[4,128,128]{2,1,0:T(8,128)(2,1)S(1)}, u32[]{:S(2)}, u32[]{:S(2)}) collective-permute-start(bf16[4,128,128]{2,1,0:T(8,128)(2,1)S(1)} %get-tuple-element.29), channel_id=1, source_target_pairs={{0,3},{1,2},{2,1},{3,0},{4,7},{5,6},{6,5},{7,4},{8,11},{9,10},{10,... | collective-permute-start | bytes 393224 | tf_op jit(solution)/shard_map/ppermute | solution.py:352

commit v7 on v5

--- a/solution.py
+++ b/solution.py
@@ -214,7 +214,8 @@
         weights_ref[:, pl.ds(pl.multiple_of(here + tile * LANES, LANES), LANES)]
         for tile in range(tiles)
     ]
-    lane = lax.broadcasted_iota(jnp.int32, (NB, LANES), 1)
+    column = lax.broadcasted_iota(jnp.int32, (NB, LANES), 1) // NB
+    owner = ((2 * PACK - column) & (2 * PACK - 1)) // 2
 
     def one_pack(group, carry):
         fields = []
@@ -245,15 +246,13 @@
                 rows_of.append(jnp.concatenate(parts, axis=1).astype(jnp.bfloat16))
         product = lax.dot_general(
             jnp.concatenate(fields, axis=0),
-            jnp.concatenate(thirds, axis=0),
+            jnp.concatenate([thirds[-column] for column in range(2 * PACK)], axis=0),
             (((1,), (1,)), ((), ())),
             preferred_element_type=jnp.float32,
         )
         total = product[0:NB]
         for member in range(1, PACK):
-            total = jnp.where(
-                lane >= member * 2 * NB, product[member * NB : (member + 1) * NB], total
-            )
+            total = jnp.where(owner == member, product[member * NB : (member + 1) * NB], total)
         total = total * scale
         if has_prior:
             total = total + prior_ref[group]
@@ -300,21 +299,22 @@
 
 def finish_kernel(part_ref, out_ref):
     packs = out_ref.shape[0] // PACK
-    sublane = lax.broadcasted_iota(jnp.int32, (8, LANES), 0)
-    lane = lax.broadcasted_iota(jnp.int32, (8, LANES), 1)
-    mine = lane // NB == sublane
+    group = lax.broadcasted_iota(jnp.int32, (8, LANES), 1) // NB
     for pack in range(packs):
         total = part_ref[pack].astype(jnp.float32)
         for device in range(1, part_ref.shape[0] // packs):
             total = total + part_ref[device * packs + pack].astype(jnp.float32)
         for half in range(2):
-            spread = pltpu.roll(total[half * 8 : half * 8 + 8], 0, 1, stride=NB, stride_axis=0)
+            skewed = pltpu.roll(total[half * 8 : half * 8 + 8], 0, 1, stride=NB, stride_axis=0)
+            moved = skewed
+            for shift in range(1, 8):
+                moved = jnp.where(group == shift, pltpu.roll(skewed, 8 - shift, 0), moved)
+            rows = pltpu.roll(moved, 0, 1, stride=NB, stride_axis=0)
             for column in range(2 * PACK):
-                moved = pltpu.roll(spread, (-column * NB) % LANES, 1)
-                row = jnp.sum(jnp.where(mine, moved, 0.0), axis=0, keepdims=True)
                 triad, part = divmod(column, 2)
+                row = pack * PACK + triad
                 start = part * NB * NB + half * LANES
-                out_ref[pack * PACK + triad : pack * PACK + triad + 1, start : start + LANES] = row
+                out_ref[row : row + 1, start : start + LANES] = rows[column : column + 1]
 
 
 def finish(pieces, devices):

time: 71.7 us -> 71.7 us (level)
  transfers between devices with their start and end apart: 9 -> 9, of which waited for: 8 -> 8; matrix products, arithmetic and copies ran while one was open for 0% -> 0% of each run, Pallas kernels for 11% -> 10%
where the time goes in v7:
time: 71.7 us; the launch traced here: 71.4 us
  waiting for transfers between devices  30.5 us (43%)
  Pallas kernels  17.2 us (24%)
  blocking collectives  12.6 us (18%)
  starting transfers between devices  11.1 us (15%)
    ppermute x9, waiting for transfers between devices, send(): return lax.ppermute(value, ('freq', 'band'), pairs)  30.5 us
    all_to_all x1, blocking collectives, mode_decomposition(): lax.all_to_all(total, axes, split_axis=0, concat_axis=0, tiled=True)  12.6 us
    ppermute x9, starting transfers between devices, send(): return lax.ppermute(value, ('freq', 'band'), pairs)  11.1 us
    pallas_call x4, Pallas kernels, triad_chunk(): pl.pallas_call(functools.partial(triad_kernel, sizes, slots, offset, prep...  7.52 us
    pallas_call x1, Pallas kernels, dft_rest(): pl.pallas_call(functools.partial(dft_rest_kernel, sizes, plan, points), o...  4.99 us
    pallas_call x2, Pallas kernels, dft_far(): pl.pallas_call(functools.partial(dft_far_kernel, sizes, far, points, offs...  3.34 us
  transfers between devices with their start and end apart: 9, of which 8 were waited for; matrix products, arithmetic and copies ran while one was open for 0% of the time, Pallas kernels for 10%

profile of v7, /device:TPU:0, one launch (start us, length us, event | category | flops | bytes accessed | tf_op | source)
XLA Modules:
  0.0 71.4 jit_solution(6759090812265527570)
XLA Ops:
  0.0 1.4 %dft_far.2 = (bf16[128,256]{1,0:T(8,128)(2,1)S(1)}, bf16[4,128,128]{2,1,0:T(8,128)(2,1)S(1)}, bf16[4,128,128]{2,1,0:T(8,128)(2,1)S(1)}) custom-call(bf16[4,256,4096]{2,1,0:T(8,128)(2,1)} %snap_ref.1), custom_call_target="tpu_custom_call" | custom-call | tf_op jit(solution)/shard_map/dft_far/pallas_call | solution.py:112
  1.4 0.0 copy-start.1
  1.4 0.0 copy-start
  1.4 1.9 %dft_far.3 = (bf16[4,128,384]{2,1,0:T(8,128)(2,1)S(1)}, bf16[4,128,384]{2,1,0:T(8,128)(2,1)S(1)}) custom-call(bf16[4,256,4096]{2,1,0:T(8,128)(2,1)} %snap_ref.1, bf16[128,256]{1,0:T(8,128)(2,1)S(1)} %get-tuple-element.19.refs_1_.table_ref), custom_call_target="tpu_custom_call" | custom-call | tf_op jit(solution)/shard_map/dft_far/pallas_call | solution.py:112
  3.4 5.0 %dft_rest.1 = (bf16[4,128,384]{2,1,0:T(8,128)(2,1)S(1)}, bf16[4,128,384]{2,1,0:T(8,128)(2,1)S(1)}, bf16[4,128,128]{2,1,0:T(8,128)(2,1)S(1)}, bf16[4,128,128]{2,1...) custom-call(bf16[128,256]{1,0:T(8,128)(2,1)S(1)} %get-tuple-element.19.refs_1_.table_ref, ...), custom_call_target="tpu_custom_call" | custom-call | flops 1073741824 | bytes 12582912 | tf_op jit(solution)/shard_map/dft_rest/pallas_call | solution.py:140
  8.4 0.6 collective-permute-start
  8.9 2.5 %collective-permute-start.1 = (bf16[4,128,128]{2,1,0:T(8,128)(2,1)S(1)}, bf16[4,128,128]{2,1,0:T(8,128)(2,1)S(1)}, u32[]{:S(2)}, u32[]{:S(2)}) collective-permute-start(bf16[4,128,128]{2,1,0:T(8,128)(2,1)S(1)} %get-tuple-element.24), channel_id=1, source_target_pairs={{0,2},{1,3},{2,0},{3,1},{4,6},{5,7},{6,4},{7,5},{8,10},{9,11},{10,... | collective-permute-start | bytes 393224 | tf_op jit(solution)/shard_map/ppermute | solution.py:352
  11.5 0.0 collective-permute-start.2
  11.5 1.7 %collective-permute-start.4 = (bf16[4,128,384]{2,1,0:T(8,128)(2,1)S(1)}, bf16[4,128,384]{2,1,0:T(8,128)(2,1)S(1)}, u32[]{:S(2)}, u32[]{:S(2)}) collective-permute-start(bf16[4,128,384]{2,1,0:T(8,128)(2,1)S(1)} %get-tuple-element.26), channel_id=1, source_target_pairs={{0,3},{1,2},{2,1},{3,0},{4,7},{5,6},{6,5},{7,4},{8,11},{9,10},{10,... | collective-permute-start | bytes 1179656 | tf_op jit(solution)/shard_map/ppermute | solution.py:352
  13.2 0.1 collective-permute-start.3
  13.3 2.5 %collective-permute-done.1.refs_4_ = bf16[4,128,128]{2,1,0:T(8,128)(2,1)S(1)} collective-permute-done((bf16[4,128,128]{2,1,0:T(8,128)(2,1)S(1)}, bf16[4,128,128]{2,1,0:T(8,128)(2,1)S(1)}, u32[]{:S(2)}, u32[]{:S(2)}) %collective-permute-start.1) | collective-permute-done | bytes 131104 | tf_op jit(solution)/shard_map/ppermute | solution.py:352
  15.8 2.0 %collective-permute-start.5 = (bf16[4,128,384]{2,1,0:T(8,128)(2,1)S(1)}, bf16[4,128,384]{2,1,0:T(8,128)(2,1)S(1)}, u32[]{:S(2)}, u32[]{:S(2)}) collective-permute-start(bf16[4,128,384]{2,1,0:T(8,128)(2,1)S(1)} %get-tuple-element.27), channel_id=1, source_target_pairs={{0,2},{1,3},{2,0},{3,1},{4,6},{5,7},{6,4},{7,5},{8,10},{9,11},{10,... | collective-permute-start | bytes 1179656 | tf_op jit(solution)/shard_map/ppermute | solution.py:352
  17.9 0.3 collective-permute-done.2.refs_5_
  18.2 2.2 %collective-permute-start.6 = (bf16[4,128,384]{2,1,0:T(8,128)(2,1)S(1)}, bf16[4,128,384]{2,1,0:T(8,128)(2,1)S(1)}, u32[]{:S(2)}, u32[]{:S(2)}) collective-permute-start(bf16[4,128,384]{2,1,0:T(8,128)(2,1)S(1)} %get-tuple-element.28), channel_id=1, source_target_pairs={{0,3},{1,2},{2,1},{3,0},{4,7},{5,6},{6,5},{7,4},{8,11},{9,10},{10,... | collective-permute-start | bytes 1179656 | tf_op jit(solution)/shard_map/ppermute | solution.py:352
  20.4 6.2 %collective-permute-done.4.refs_6_ = bf16[4,128,384]{2,1,0:T(8,128)(2,1)S(1)} collective-permute-done((bf16[4,128,384]{2,1,0:T(8,128)(2,1)S(1)}, bf16[4,128,384]{2,1,0:T(8,128)(2,1)S(1)}, u32[]{:S(2)}, u32[]{:S(2)}) %collective-permute-start.4) | collective-permute-done | bytes 393248 | tf_op jit(solution)/shard_map/ppermute | solution.py:352
  26.6 1.4 %collective-permute-start.7 = (bf16[4,128,128]{2,1,0:T(8,128)(2,1)S(1)}, bf16[4,128,128]{2,1,0:T(8,128)(2,1)S(1)}, u32[]{:S(2)}, u32[]{:S(2)}) collective-permute-start(bf16[4,128,128]{2,1,0:T(8,128)(2,1)S(1)} %get-tuple-element.30), channel_id=1, source_target_pairs={{0,2},{1,3},{2,0},{3,1},{4,6},{5,7},{6,4},{7,5},{8,10},{9,11},{10,... | collective-permute-start | bytes 393224 | tf_op jit(solution)/shard_map/ppermute | solution.py:352
  28.0 0.0 collective-permute-done.refs_2_.refs_3_.refs_4_
  28.0 0.5 collective-permute-start.8
  28.5 0.0 copy-done.1
  28.5 0.6 prepare.1
  29.1 0.0 copy-done
  29.1 1.2 %triads.4.refs_2_ = f32[16,16,128]{2,1,0:T(8,128)S(1)} custom-call(s32[2,64]{1,0:T(2,128)S(4)} %get-tuple-element.23.refs_0_, f32[1,4096]{1,0:T(1,128)S(1)} %bitcast.2, bf16[4,128,1024]{2,1,0:T(8,128)(2,1)S(1)} %get-tuple-element.21.refs_1_.refs_2_.refs_3_, bf16[4,128,1024]{2,1,0:T(8,128)(2,1)S(1)} %collective-permute-done.refs_2_.refs_3_.refs_4_, ...), custom_call_target="tpu_custom_call" | custom-call | flops 67108864 | bytes 524288 | tf_op jit(solution)/shard_map/triads/pallas_call | solution.py:281
  30.3 5.2 %collective-permute-done.3.refs_5_ = bf16[4,128,384]{2,1,0:T(8,128)(2,1)S(1)} collective-permute-done((bf16[4,128,384]{2,1,0:T(8,128)(2,1)S(1)}, bf16[4,128,384]{2,1,0:T(8,128)(2,1)S(1)}, u32[]{:S(2)}, u32[]{:S(2)}) %collective-permute-start.3) | collective-permute-done | bytes 393248 | tf_op jit(solution)/shard_map/ppermute | solution.py:352
  35.5 2.8 %triads.5.refs_2_ = f32[16,16,128]{2,1,0:T(8,128)S(1)} custom-call(s32[2,64]{1,0:T(2,128)S(4)} %get-tuple-element.23.refs_0_, f32[1,4096]{1,0:T(1,128)S(1)} %bitcast.3, f32[16,16,128]{2,1,0:T(8,128)S(1)} %triads.4.refs_2_, bf16[4,128,1024]{2,1,0:T(8,128)(2,1)S(1)} %get-tuple-element.21.refs_1_.refs_2_.refs_3_, ...), custom_call_target="tpu_custom_call" | custom-call | flops 201326592 | bytes 1572864 | tf_op jit(solution)/shard_map/triads/pallas_call | solution.py:281
  38.3 5.6 %collective-permute-done.5.refs_5_ = bf16[4,128,384]{2,1,0:T(8,128)(2,1)S(1)} collective-permute-done((bf16[4,128,384]{2,1,0:T(8,128)(2,1)S(1)}, bf16[4,128,384]{2,1,0:T(8,128)(2,1)S(1)}, u32[]{:S(2)}, u32[]{:S(2)}) %collective-permute-start.5) | collective-permute-done | bytes 393248 | tf_op jit(solution)/shard_map/ppermute | solution.py:352
  43.9 8.0 %collective-permute-done.6.refs_6_ = bf16[4,128,384]{2,1,0:T(8,128)(2,1)S(1)} collective-permute-done((bf16[4,128,384]{2,1,0:T(8,128)(2,1)S(1)}, bf16[4,128,384]{2,1,0:T(8,128)(2,1)S(1)}, u32[]{:S(2)}, u32[]{:S(2)}) %collective-permute-start.6) | collective-permute-done | bytes 393248 | tf_op jit(solution)/shard_map/ppermute | solution.py:352
  51.9 2.8 %triads.6.refs_2_ = f32[16,16,128]{2,1,0:T(8,128)S(1)} custom-call(s32[2,64]{1,0:T(2,128)S(4)} %get-tuple-element.23.refs_0_, f32[1,4096]{1,0:T(1,128)S(1)} %bitcast.4, f32[16,16,128]{2,1,0:T(8,128)S(1)} %triads.5.refs_2_, bf16[4,128,1024]{2,1,0:T(8,128)(2,1)S(1)} %get-tuple-element.21.refs_1_.refs_2_.refs_3_, ...), custom_call_target="tpu_custom_call" | custom-call | flops 201326592 | bytes 1572864 | tf_op jit(solution)/shard_map/triads/pallas_call | solution.py:281
  54.7 0.4 collective-permute-done.7.refs_4_
  55.2 2.3 %collective-permute-done.8.refs_5_ = bf16[4,128,128]{2,1,0:T(8,128)(2,1)S(1)} collective-permute-done((bf16[4,128,128]{2,1,0:T(8,128)(2,1)S(1)}, bf16[4,128,128]{2,1,0:T(8,128)(2,1)S(1)}, u32[]{:S(2)}, u32[]{:S(2)}) %collective-permute-start.8) | collective-permute-done | bytes 131104 | tf_op jit(solution)/shard_map/ppermute | solution.py:352
  57.4 0.6 triads.7
  58.1 12.6 %all_to_all.5.part_ref = bf16[16,16,128]{2,1,0:T(8,128)(2,1)S(1)} all-to-all(bf16[16,16,128]{2,1,0:T(8,128)(2,1)S(1)} %get-tuple-element.32), channel_id=1, replica_groups=mesh['groups'=2,'space'=4,'freq'=2,'band'=2] {'space','freq','band'}, dimensions={0} | all-to-all | bytes 131072 | tf_op jit(solution)/shard_map/all_to_all | solution.py:389
  70.7 0.8 %finish.1 = f32[4,512]{1,0:T(4,128)} custom-call(bf16[16,16,128]{2,1,0:T(8,128)(2,1)S(1)} %all_to_all.5.part_ref), custom_call_target="tpu_custom_call" | custom-call | tf_op jit(solution)/shard_map/finish/pallas_call | solution.py:322
Async XLA Ops:
  1.4 27.1 %copy-start.1 = (s32[64,2]{0,1:T(2,128)S(1)}, s32[64,2]{0,1:T(2,128)}, u32[]{:S(2)}) copy-start(s32[64,2]{0,1:T(2,128)} %param.5) | copy-start | bytes 1540
  1.4 27.7 %copy-start = (f32[4096]{0:T(1024)S(1)}, f32[4096]{0:T(1024)}, u32[]{:S(2)}) copy-start(f32[4096]{0:T(1024)} %param.4) | copy-start | bytes 49156
  8.4 19.6 %collective-permute-start = (bf16[4,128,1024]{2,1,0:T(8,128)(2,1)S(1)}, bf16[4,128,1024]{2,1,0:T(8,128)(2,1)S(1)}, u32[]{:S(2)}, u32[]{:S(2)}) collective-permute-start(bf16[4,128,1024]{2,1,0:T(8,128)(2,1)S(1)} %get-tuple-element.22), channel_id=1, source_target_pairs={{0,1},{1,0},{2,3},{3,2},{4,5},{5,4},{6,7},{7,6},{8,9},{9,8},{10,11... | collective-permute-start | bytes 3145736 | tf_op jit(solution)/shard_map/ppermute | solution.py:352
  8.9 6.9 %collective-permute-start.1 = (bf16[4,128,128]{2,1,0:T(8,128)(2,1)S(1)}, bf16[4,128,128]{2,1,0:T(8,128)(2,1)S(1)}, u32[]{:S(2)}, u32[]{:S(2)}) collective-permute-start(bf16[4,128,128]{2,1,0:T(8,128)(2,1)S(1)} %get-tuple-element.24), channel_id=1, source_target_pairs={{0,2},{1,3},{2,0},{3,1},{4,6},{5,7},{6,4},{7,5},{8,10},{9,11},{10,... | collective-permute-start | bytes 393224 | tf_op jit(solution)/shard_map/ppermute | solution.py:352
  11.5 6.7 %collective-permute-start.2 = (bf16[4,128,128]{2,1,0:T(8,128)(2,1)S(1)}, bf16[4,128,128]{2,1,0:T(8,128)(2,1)S(1)}, u32[]{:S(2)}, u32[]{:S(2)}) collective-permute-start(bf16[4,128,128]{2,1,0:T(8,128)(2,1)S(1)} %get-tuple-element.25), channel_id=1, source_target_pairs={{0,3},{1,2},{2,1},{3,0},{4,7},{5,6},{6,5},{7,4},{8,11},{9,10},{10,... | collective-permute-start | bytes 393224 | tf_op jit(solution)/shard_map/ppermute | solution.py:352
  11.5 15.1 %collective-permute-start.4 = (bf16[4,128,384]{2,1,0:T(8,128)(2,1)S(1)}, bf16[4,128,384]{2,1,0:T(8,128)(2,1)S(1)}, u32[]{:S(2)}, u32[]{:S(2)}) collective-permute-start(bf16[4,128,384]{2,1,0:T(8,128)(2,1)S(1)} %get-tuple-element.26), channel_id=1, source_target_pairs={{0,3},{1,2},{2,1},{3,0},{4,7},{5,6},{6,5},{7,4},{8,11},{9,10},{10,... | collective-permute-start | bytes 1179656 | tf_op jit(solution)/shard_map/ppermute | solution.py:352
  13.2 22.3 %collective-permute-start.3 = (bf16[4,128,384]{2,1,0:T(8,128)(2,1)S(1)}, bf16[4,128,384]{2,1,0:T(8,128)(2,1)S(1)}, u32[]{:S(2)}, u32[]{:S(2)}) collective-permute-start(bf16[4,128,384]{2,1,0:T(8,128)(2,1)S(1)} %get-tuple-element.20.after_ref), channel_id=1, source_target_pairs={{0,2},{1,3},{2,0},{3,1},{4,6},{5,7},{6,4},{7,5},{8,10},{9,11},{10,... | collective-permute-start | bytes 1179656 | tf_op jit(solution)/shard_map/ppermute | solution.py:352
  15.8 28.1 %collective-permute-start.5 = (bf16[4,128,384]{2,1,0:T(8,128)(2,1)S(1)}, bf16[4,128,384]{2,1,0:T(8,128)(2,1)S(1)}, u32[]{:S(2)}, u32[]{:S(2)}) collective-permute-start(bf16[4,128,384]{2,1,0:T(8,128)(2,1)S(1)} %get-tuple-element.27), channel_id=1, source_target_pairs={{0,2},{1,3},{2,0},{3,1},{4,6},{5,7},{6,4},{7,5},{8,10},{9,11},{10,... | collective-permute-start | bytes 1179656 | tf_op jit(solution)/shard_map/ppermute | solution.py:352
  18.2 33.7 %collective-permute-start.6 = (bf16[4,128,384]{2,1,0:T(8,128)(2,1)S(1)}, bf16[4,128,384]{2,1,0:T(8,128)(2,1)S(1)}, u32[]{:S(2)}, u32[]{:S(2)}) collective-permute-start(bf16[4,128,384]{2,1,0:T(8,128)(2,1)S(1)} %get-tuple-element.28), channel_id=1, source_target_pairs={{0,3},{1,2},{2,1},{3,0},{4,7},{5,6},{6,5},{7,4},{8,11},{9,10},{10,... | collective-permute-start | bytes 1179656 | tf_op jit(solution)/shard_map/ppermute | solution.py:352
  26.6 28.5 %collective-permute-start.7 = (bf16[4,128,128]{2,1,0:T(8,128)(2,1)S(1)}, bf16[4,128,128]{2,1,0:T(8,128)(2,1)S(1)}, u32[]{:S(2)}, u32[]{:S(2)}) collective-permute-start(bf16[4,128,128]{2,1,0:T(8,128)(2,1)S(1)} %get-tuple-element.30), channel_id=1, source_target_pairs={{0,2},{1,3},{2,0},{3,1},{4,6},{5,7},{6,4},{7,5},{8,10},{9,11},{10,... | collective-permute-start | bytes 393224 | tf_op jit(solution)/shard_map/ppermute | solution.py:352
  28.0 29.4 %collective-permute-start.8 = (bf16[4,128,128]{2,1,0:T(8,128)(2,1)S(1)}, bf16[4,128,128]{2,1,0:T(8,128)(2,1)S(1)}, u32[]{:S(2)}, u32[]{:S(2)}) collective-permute-start(bf16[4,128,128]{2,1,0:T(8,128)(2,1)S(1)} %get-tuple-element.31), channel_id=1, source_target_pairs={{0,3},{1,2},{2,1},{3,0},{4,7},{5,6},{6,5},{7,4},{8,11},{9,10},{10,... | collective-permute-start | bytes 393224 | tf_op jit(solution)/shard_map/ppermute | solution.py:352

commit v8 on v7

--- a/solution.py
+++ b/solution.py
@@ -214,8 +214,9 @@
         weights_ref[:, pl.ds(pl.multiple_of(here + tile * LANES, LANES), LANES)]
         for tile in range(tiles)
     ]
+    numbers = [-column % (2 * PACK) for column in range(2 * PACK)]
     column = lax.broadcasted_iota(jnp.int32, (NB, LANES), 1) // NB
-    owner = ((2 * PACK - column) & (2 * PACK - 1)) // 2
+    owner = (2 * PACK - column) & (PACK - 1)
 
     def one_pack(group, carry):
         fields = []
@@ -246,7 +247,9 @@
                 rows_of.append(jnp.concatenate(parts, axis=1).astype(jnp.bfloat16))
         product = lax.dot_general(
             jnp.concatenate(fields, axis=0),
-            jnp.concatenate([thirds[-column] for column in range(2 * PACK)], axis=0),
+            jnp.concatenate(
+                [thirds[number % PACK * 2 + number // PACK] for number in numbers], axis=0
+            ),
             (((1,), (1,)), ((), ())),
             preferred_element_type=jnp.float32,
         )
@@ -310,11 +313,11 @@
             for shift in range(1, 8):
                 moved = jnp.where(group == shift, pltpu.roll(skewed, 8 - shift, 0), moved)
             rows = pltpu.roll(moved, 0, 1, stride=NB, stride_axis=0)
-            for column in range(2 * PACK):
-                triad, part = divmod(column, 2)
-                row = pack * PACK + triad
+            for part in range(2):
                 start = part * NB * NB + half * LANES
-                out_ref[row : row + 1, start : start + LANES] = rows[column : column + 1]
+                out_ref[pack * PACK : (pack + 1) * PACK, start : start + LANES] = rows[
+                    part * PACK : (part + 1) * PACK
+                ]
 
 
 def finish(pieces, devices):

time: 71.7 us -> 71.7 us (level)
  transfers between devices with their start and end apart: 9 -> 9, of which waited for: 8 -> 8; matrix products, arithmetic and copies ran while one was open for 0% -> 0% of each run, Pallas kernels for 10% -> 11%
where the time goes in v8:
time: 71.7 us; the launch traced here: 71.4 us
  waiting for transfers between devices  30.4 us (42%)
  Pallas kernels  17.3 us (24%)
  blocking collectives  12.6 us (18%)
  starting transfers between devices  11.1 us (15%)
    ppermute x9, waiting for transfers between devices, send(): return lax.ppermute(value, ('freq', 'band'), pairs)  30.4 us
    all_to_all x1, blocking collectives, mode_decomposition(): lax.all_to_all(total, axes, split_axis=0, concat_axis=0, tiled=True)  12.6 us
    ppermute x9, starting transfers between devices, send(): return lax.ppermute(value, ('freq', 'band'), pairs)  11.1 us
    pallas_call x4, Pallas kernels, triad_chunk(): pl.pallas_call(functools.partial(triad_kernel, sizes, slots, offset, prep...  7.68 us
    pallas_call x1, Pallas kernels, dft_rest(): pl.pallas_call(functools.partial(dft_rest_kernel, sizes, plan, points), o...  4.99 us
    pallas_call x2, Pallas kernels, dft_far(): pl.pallas_call(functools.partial(dft_far_kernel, sizes, far, points, offs...  3.34 us
  transfers between devices with their start and end apart: 9, of which 8 were waited for; matrix products, arithmetic and copies ran while one was open for 0% of the time, Pallas kernels for 11%

profile of v8, /device:TPU:0, one launch (start us, length us, event | category | flops | bytes accessed | tf_op | source)
XLA Modules:
  0.0 71.4 jit_solution(12665625072431172661)
XLA Ops:
  0.0 1.4 %dft_far.2 = (bf16[128,256]{1,0:T(8,128)(2,1)S(1)}, bf16[4,128,128]{2,1,0:T(8,128)(2,1)S(1)}, bf16[4,128,128]{2,1,0:T(8,128)(2,1)S(1)}) custom-call(bf16[4,256,4096]{2,1,0:T(8,128)(2,1)} %snap_ref.1), custom_call_target="tpu_custom_call" | custom-call | tf_op jit(solution)/shard_map/dft_far/pallas_call | solution.py:112
  1.4 0.0 copy-start.1
  1.4 0.0 copy-start
  1.4 1.9 %dft_far.3 = (bf16[4,128,384]{2,1,0:T(8,128)(2,1)S(1)}, bf16[4,128,384]{2,1,0:T(8,128)(2,1)S(1)}) custom-call(bf16[4,256,4096]{2,1,0:T(8,128)(2,1)} %snap_ref.1, bf16[128,256]{1,0:T(8,128)(2,1)S(1)} %get-tuple-element.19.refs_1_.table_ref), custom_call_target="tpu_custom_call" | custom-call | tf_op jit(solution)/shard_map/dft_far/pallas_call | solution.py:112
  3.4 5.0 %dft_rest.1 = (bf16[4,128,384]{2,1,0:T(8,128)(2,1)S(1)}, bf16[4,128,384]{2,1,0:T(8,128)(2,1)S(1)}, bf16[4,128,128]{2,1,0:T(8,128)(2,1)S(1)}, bf16[4,128,128]{2,1...) custom-call(bf16[128,256]{1,0:T(8,128)(2,1)S(1)} %get-tuple-element.19.refs_1_.table_ref, ...), custom_call_target="tpu_custom_call" | custom-call | flops 1073741824 | bytes 12582912 | tf_op jit(solution)/shard_map/dft_rest/pallas_call | solution.py:140
  8.4 0.6 collective-permute-start
  8.9 2.5 %collective-permute-start.1 = (bf16[4,128,128]{2,1,0:T(8,128)(2,1)S(1)}, bf16[4,128,128]{2,1,0:T(8,128)(2,1)S(1)}, u32[]{:S(2)}, u32[]{:S(2)}) collective-permute-start(bf16[4,128,128]{2,1,0:T(8,128)(2,1)S(1)} %get-tuple-element.24), channel_id=1, source_target_pairs={{0,2},{1,3},{2,0},{3,1},{4,6},{5,7},{6,4},{7,5},{8,10},{9,11},{10,... | collective-permute-start | bytes 393224 | tf_op jit(solution)/shard_map/ppermute | solution.py:355
  11.5 0.0 collective-permute-start.2
  11.5 1.7 %collective-permute-start.4 = (bf16[4,128,384]{2,1,0:T(8,128)(2,1)S(1)}, bf16[4,128,384]{2,1,0:T(8,128)(2,1)S(1)}, u32[]{:S(2)}, u32[]{:S(2)}) collective-permute-start(bf16[4,128,384]{2,1,0:T(8,128)(2,1)S(1)} %get-tuple-element.26), channel_id=1, source_target_pairs={{0,3},{1,2},{2,1},{3,0},{4,7},{5,6},{6,5},{7,4},{8,11},{9,10},{10,... | collective-permute-start | bytes 1179656 | tf_op jit(solution)/shard_map/ppermute | solution.py:355
  13.2 0.1 collective-permute-start.3
  13.3 2.5 %collective-permute-done.1.refs_4_ = bf16[4,128,128]{2,1,0:T(8,128)(2,1)S(1)} collective-permute-done((bf16[4,128,128]{2,1,0:T(8,128)(2,1)S(1)}, bf16[4,128,128]{2,1,0:T(8,128)(2,1)S(1)}, u32[]{:S(2)}, u32[]{:S(2)}) %collective-permute-start.1) | collective-permute-done | bytes 131104 | tf_op jit(solution)/shard_map/ppermute | solution.py:355
  15.8 2.0 %collective-permute-start.5 = (bf16[4,128,384]{2,1,0:T(8,128)(2,1)S(1)}, bf16[4,128,384]{2,1,0:T(8,128)(2,1)S(1)}, u32[]{:S(2)}, u32[]{:S(2)}) collective-permute-start(bf16[4,128,384]{2,1,0:T(8,128)(2,1)S(1)} %get-tuple-element.27), channel_id=1, source_target_pairs={{0,2},{1,3},{2,0},{3,1},{4,6},{5,7},{6,4},{7,5},{8,10},{9,11},{10,... | collective-permute-start | bytes 1179656 | tf_op jit(solution)/shard_map/ppermute | solution.py:355
  17.9 0.3 collective-permute-done.2.refs_5_
  18.2 2.2 %collective-permute-start.6 = (bf16[4,128,384]{2,1,0:T(8,128)(2,1)S(1)}, bf16[4,128,384]{2,1,0:T(8,128)(2,1)S(1)}, u32[]{:S(2)}, u32[]{:S(2)}) collective-permute-start(bf16[4,128,384]{2,1,0:T(8,128)(2,1)S(1)} %get-tuple-element.28), channel_id=1, source_target_pairs={{0,3},{1,2},{2,1},{3,0},{4,7},{5,6},{6,5},{7,4},{8,11},{9,10},{10,... | collective-permute-start | bytes 1179656 | tf_op jit(solution)/shard_map/ppermute | solution.py:355
  20.4 6.2 %collective-permute-done.4.refs_6_ = bf16[4,128,384]{2,1,0:T(8,128)(2,1)S(1)} collective-permute-done((bf16[4,128,384]{2,1,0:T(8,128)(2,1)S(1)}, bf16[4,128,384]{2,1,0:T(8,128)(2,1)S(1)}, u32[]{:S(2)}, u32[]{:S(2)}) %collective-permute-start.4) | collective-permute-done | bytes 393248 | tf_op jit(solution)/shard_map/ppermute | solution.py:355
  26.6 1.4 %collective-permute-start.7 = (bf16[4,128,128]{2,1,0:T(8,128)(2,1)S(1)}, bf16[4,128,128]{2,1,0:T(8,128)(2,1)S(1)}, u32[]{:S(2)}, u32[]{:S(2)}) collective-permute-start(bf16[4,128,128]{2,1,0:T(8,128)(2,1)S(1)} %get-tuple-element.30), channel_id=1, source_target_pairs={{0,2},{1,3},{2,0},{3,1},{4,6},{5,7},{6,4},{7,5},{8,10},{9,11},{10,... | collective-permute-start | bytes 393224 | tf_op jit(solution)/shard_map/ppermute | solution.py:355
  28.0 0.0 collective-permute-done.refs_2_.refs_3_.refs_4_
  28.0 0.5 collective-permute-start.8
  28.5 0.0 copy-done.1
  28.5 0.6 prepare.1
  29.1 0.0 copy-done
  29.1 1.2 %triads.4.refs_2_ = f32[16,16,128]{2,1,0:T(8,128)S(1)} custom-call(s32[2,64]{1,0:T(2,128)S(4)} %get-tuple-element.23.refs_0_, f32[1,4096]{1,0:T(1,128)S(1)} %bitcast.2, bf16[4,128,1024]{2,1,0:T(8,128)(2,1)S(1)} %get-tuple-element.21.refs_1_.refs_2_.refs_3_, bf16[4,128,1024]{2,1,0:T(8,128)(2,1)S(1)} %collective-permute-done.refs_2_.refs_3_.refs_4_, ...), custom_call_target="tpu_custom_call" | custom-call | flops 67108864 | bytes 524288 | tf_op jit(solution)/shard_map/triads/pallas_call | solution.py:284
  30.4 5.1 %collective-permute-done.3.refs_5_ = bf16[4,128,384]{2,1,0:T(8,128)(2,1)S(1)} collective-permute-done((bf16[4,128,384]{2,1,0:T(8,128)(2,1)S(1)}, bf16[4,128,384]{2,1,0:T(8,128)(2,1)S(1)}, u32[]{:S(2)}, u32[]{:S(2)}) %collective-permute-start.3) | collective-permute-done | bytes 393248 | tf_op jit(solution)/shard_map/ppermute | solution.py:355
  35.5 2.9 %triads.5.refs_2_ = f32[16,16,128]{2,1,0:T(8,128)S(1)} custom-call(s32[2,64]{1,0:T(2,128)S(4)} %get-tuple-element.23.refs_0_, f32[1,4096]{1,0:T(1,128)S(1)} %bitcast.3, f32[16,16,128]{2,1,0:T(8,128)S(1)} %triads.4.refs_2_, bf16[4,128,1024]{2,1,0:T(8,128)(2,1)S(1)} %get-tuple-element.21.refs_1_.refs_2_.refs_3_, ...), custom_call_target="tpu_custom_call" | custom-call | flops 201326592 | bytes 1572864 | tf_op jit(solution)/shard_map/triads/pallas_call | solution.py:284
  38.4 5.5 %collective-permute-done.5.refs_5_ = bf16[4,128,384]{2,1,0:T(8,128)(2,1)S(1)} collective-permute-done((bf16[4,128,384]{2,1,0:T(8,128)(2,1)S(1)}, bf16[4,128,384]{2,1,0:T(8,128)(2,1)S(1)}, u32[]{:S(2)}, u32[]{:S(2)}) %collective-permute-start.5) | collective-permute-done | bytes 393248 | tf_op jit(solution)/shard_map/ppermute | solution.py:355
  43.9 8.0 %collective-permute-done.6.refs_6_ = bf16[4,128,384]{2,1,0:T(8,128)(2,1)S(1)} collective-permute-done((bf16[4,128,384]{2,1,0:T(8,128)(2,1)S(1)}, bf16[4,128,384]{2,1,0:T(8,128)(2,1)S(1)}, u32[]{:S(2)}, u32[]{:S(2)}) %collective-permute-start.6) | collective-permute-done | bytes 393248 | tf_op jit(solution)/shard_map/ppermute | solution.py:355
  51.9 2.9 %triads.6.refs_2_ = f32[16,16,128]{2,1,0:T(8,128)S(1)} custom-call(s32[2,64]{1,0:T(2,128)S(4)} %get-tuple-element.23.refs_0_, f32[1,4096]{1,0:T(1,128)S(1)} %bitcast.4, f32[16,16,128]{2,1,0:T(8,128)S(1)} %triads.5.refs_2_, bf16[4,128,1024]{2,1,0:T(8,128)(2,1)S(1)} %get-tuple-element.21.refs_1_.refs_2_.refs_3_, ...), custom_call_target="tpu_custom_call" | custom-call | flops 201326592 | bytes 1572864 | tf_op jit(solution)/shard_map/triads/pallas_call | solution.py:284
  54.8 0.4 collective-permute-done.7.refs_4_
  55.2 2.3 %collective-permute-done.8.refs_5_ = bf16[4,128,128]{2,1,0:T(8,128)(2,1)S(1)} collective-permute-done((bf16[4,128,128]{2,1,0:T(8,128)(2,1)S(1)}, bf16[4,128,128]{2,1,0:T(8,128)(2,1)S(1)}, u32[]{:S(2)}, u32[]{:S(2)}) %collective-permute-start.8) | collective-permute-done | bytes 131104 | tf_op jit(solution)/shard_map/ppermute | solution.py:355
  57.4 0.7 triads.7
  58.1 12.6 %all_to_all.5.part_ref = bf16[16,16,128]{2,1,0:T(8,128)(2,1)S(1)} all-to-all(bf16[16,16,128]{2,1,0:T(8,128)(2,1)S(1)} %get-tuple-element.32), channel_id=1, replica_groups=mesh['groups'=2,'space'=4,'freq'=2,'band'=2] {'space','freq','band'}, dimensions={0} | all-to-all | bytes 131072 | tf_op jit(solution)/shard_map/all_to_all | solution.py:392
  70.7 0.8 %finish.1 = f32[4,512]{1,0:T(4,128)} custom-call(bf16[16,16,128]{2,1,0:T(8,128)(2,1)S(1)} %all_to_all.5.part_ref), custom_call_target="tpu_custom_call" | custom-call | tf_op jit(solution)/shard_map/finish/pallas_call | solution.py:325
Async XLA Ops:
  1.4 27.1 %copy-start.1 = (s32[64,2]{0,1:T(2,128)S(1)}, s32[64,2]{0,1:T(2,128)}, u32[]{:S(2)}) copy-start(s32[64,2]{0,1:T(2,128)} %param.5) | copy-start | bytes 1540
  1.4 27.7 %copy-start = (f32[4096]{0:T(1024)S(1)}, f32[4096]{0:T(1024)}, u32[]{:S(2)}) copy-start(f32[4096]{0:T(1024)} %param.4) | copy-start | bytes 49156
  8.4 19.6 %collective-permute-start = (bf16[4,128,1024]{2,1,0:T(8,128)(2,1)S(1)}, bf16[4,128,1024]{2,1,0:T(8,128)(2,1)S(1)}, u32[]{:S(2)}, u32[]{:S(2)}) collective-permute-start(bf16[4,128,1024]{2,1,0:T(8,128)(2,1)S(1)} %get-tuple-element.22), channel_id=1, source_target_pairs={{0,1},{1,0},{2,3},{3,2},{4,5},{5,4},{6,7},{7,6},{8,9},{9,8},{10,11... | collective-permute-start | bytes 3145736 | tf_op jit(solution)/shard_map/ppermute | solution.py:355
  8.9 6.9 %collective-permute-start.1 = (bf16[4,128,128]{2,1,0:T(8,128)(2,1)S(1)}, bf16[4,128,128]{2,1,0:T(8,128)(2,1)S(1)}, u32[]{:S(2)}, u32[]{:S(2)}) collective-permute-start(bf16[4,128,128]{2,1,0:T(8,128)(2,1)S(1)} %get-tuple-element.24), channel_id=1, source_target_pairs={{0,2},{1,3},{2,0},{3,1},{4,6},{5,7},{6,4},{7,5},{8,10},{9,11},{10,... | collective-permute-start | bytes 393224 | tf_op jit(solution)/shard_map/ppermute | solution.py:355
  11.5 6.7 %collective-permute-start.2 = (bf16[4,128,128]{2,1,0:T(8,128)(2,1)S(1)}, bf16[4,128,128]{2,1,0:T(8,128)(2,1)S(1)}, u32[]{:S(2)}, u32[]{:S(2)}) collective-permute-start(bf16[4,128,128]{2,1,0:T(8,128)(2,1)S(1)} %get-tuple-element.25), channel_id=1, source_target_pairs={{0,3},{1,2},{2,1},{3,0},{4,7},{5,6},{6,5},{7,4},{8,11},{9,10},{10,... | collective-permute-start | bytes 393224 | tf_op jit(solution)/shard_map/ppermute | solution.py:355
  11.5 15.1 %collective-permute-start.4 = (bf16[4,128,384]{2,1,0:T(8,128)(2,1)S(1)}, bf16[4,128,384]{2,1,0:T(8,128)(2,1)S(1)}, u32[]{:S(2)}, u32[]{:S(2)}) collective-permute-start(bf16[4,128,384]{2,1,0:T(8,128)(2,1)S(1)} %get-tuple-element.26), channel_id=1, source_target_pairs={{0,3},{1,2},{2,1},{3,0},{4,7},{5,6},{6,5},{7,4},{8,11},{9,10},{10,... | collective-permute-start | bytes 1179656 | tf_op jit(solution)/shard_map/ppermute | solution.py:355
  13.2 22.3 %collective-permute-start.3 = (bf16[4,128,384]{2,1,0:T(8,128)(2,1)S(1)}, bf16[4,128,384]{2,1,0:T(8,128)(2,1)S(1)}, u32[]{:S(2)}, u32[]{:S(2)}) collective-permute-start(bf16[4,128,384]{2,1,0:T(8,128)(2,1)S(1)} %get-tuple-element.20.after_ref), channel_id=1, source_target_pairs={{0,2},{1,3},{2,0},{3,1},{4,6},{5,7},{6,4},{7,5},{8,10},{9,11},{10,... | collective-permute-start | bytes 1179656 | tf_op jit(solution)/shard_map/ppermute | solution.py:355
  15.8 28.1 %collective-permute-start.5 = (bf16[4,128,384]{2,1,0:T(8,128)(2,1)S(1)}, bf16[4,128,384]{2,1,0:T(8,128)(2,1)S(1)}, u32[]{:S(2)}, u32[]{:S(2)}) collective-permute-start(bf16[4,128,384]{2,1,0:T(8,128)(2,1)S(1)} %get-tuple-element.27), channel_id=1, source_target_pairs={{0,2},{1,3},{2,0},{3,1},{4,6},{5,7},{6,4},{7,5},{8,10},{9,11},{10,... | collective-permute-start | bytes 1179656 | tf_op jit(solution)/shard_map/ppermute | solution.py:355
  18.2 33.7 %collective-permute-start.6 = (bf16[4,128,384]{2,1,0:T(8,128)(2,1)S(1)}, bf16[4,128,384]{2,1,0:T(8,128)(2,1)S(1)}, u32[]{:S(2)}, u32[]{:S(2)}) collective-permute-start(bf16[4,128,384]{2,1,0:T(8,128)(2,1)S(1)} %get-tuple-element.28), channel_id=1, source_target_pairs={{0,3},{1,2},{2,1},{3,0},{4,7},{5,6},{6,5},{7,4},{8,11},{9,10},{10,... | collective-permute-start | bytes 1179656 | tf_op jit(solution)/shard_map/ppermute | solution.py:355
  26.6 28.5 %collective-permute-start.7 = (bf16[4,128,128]{2,1,0:T(8,128)(2,1)S(1)}, bf16[4,128,128]{2,1,0:T(8,128)(2,1)S(1)}, u32[]{:S(2)}, u32[]{:S(2)}) collective-permute-start(bf16[4,128,128]{2,1,0:T(8,128)(2,1)S(1)} %get-tuple-element.30), channel_id=1, source_target_pairs={{0,2},{1,3},{2,0},{3,1},{4,6},{5,7},{6,4},{7,5},{8,10},{9,11},{10,... | collective-permute-start | bytes 393224 | tf_op jit(solution)/shard_map/ppermute | solution.py:355
  28.0 29.4 %collective-permute-start.8 = (bf16[4,128,128]{2,1,0:T(8,128)(2,1)S(1)}, bf16[4,128,128]{2,1,0:T(8,128)(2,1)S(1)}, u32[]{:S(2)}, u32[]{:S(2)}) collective-permute-start(bf16[4,128,128]{2,1,0:T(8,128)(2,1)S(1)} %get-tuple-element.31), channel_id=1, source_target_pairs={{0,3},{1,2},{2,1},{3,0},{4,7},{5,6},{6,5},{7,4},{8,11},{9,10},{10,... | collective-permute-start | bytes 393224 | tf_op jit(solution)/shard_map/ppermute | solution.py:355

commit v9 on v7

--- a/solution.py
+++ b/solution.py
@@ -24,8 +24,9 @@
 def split_widths(points):
     tiles = points // LANES
     rest = tiles - 2
-    count = -(-rest // 3)
-    middle = [rest // count + (i < rest % count) for i in range(count)]
+    late = min(rest, 2)
+    count = -(-(rest - late) // 4)
+    middle = [(rest - late) // count + (i < (rest - late) % count) for i in range(count)] + [late]
     return [w * LANES for w in [1] + middle + [1]]
 
 

time: 71.7 us -> 71.5 us (level)
  starting transfers between devices: 11.1 us -> 9.96 us
    ppermute x9, starting transfers between devices: 11.1 us -> 9.96 us  [send(): return lax.ppermute(value, ('freq', 'band'), pairs)]
  transfers between devices with their start and end apart: 9 -> 9, of which waited for: 8 -> 5; matrix products, arithmetic and copies ran while one was open for 0% -> 0% of each run, Pallas kernels for 10% -> 10%
where the time goes in v9:
time: 71.5 us; the launch traced here: 71.3 us
  waiting for transfers between devices  31.1 us (43%)
  Pallas kernels  17.1 us (24%)
  blocking collectives  13 us (18%)
  starting transfers between devices  9.96 us (14%)
    ppermute x9, waiting for transfers between devices, send(): return lax.ppermute(value, ('freq', 'band'), pairs)  31.1 us
    all_to_all x1, blocking collectives, mode_decomposition(): lax.all_to_all(total, axes, split_axis=0, concat_axis=0, tiled=True)  13 us
    ppermute x9, starting transfers between devices, send(): return lax.ppermute(value, ('freq', 'band'), pairs)  9.96 us
    pallas_call x4, Pallas kernels, triad_chunk(): pl.pallas_call(functools.partial(triad_kernel, sizes, slots, offset, prep...  7.5 us
    pallas_call x1, Pallas kernels, dft_rest(): pl.pallas_call(functools.partial(dft_rest_kernel, sizes, plan, points), o...  4.8 us
    pallas_call x2, Pallas kernels, dft_far(): pl.pallas_call(functools.partial(dft_far_kernel, sizes, far, points, offs...  3.45 us
  transfers between devices with their start and end apart: 9, of which 5 were waited for; matrix products, arithmetic and copies ran while one was open for 0% of the time, Pallas kernels for 10%

profile of v9, /device:TPU:0, one launch (start us, length us, event | category | flops | bytes accessed | tf_op | source)
XLA Modules:
  0.0 71.3 jit_solution(1312080219719725832)
XLA Ops:
  0.0 1.4 %dft_far.2 = (bf16[128,256]{1,0:T(8,128)(2,1)S(1)}, bf16[4,128,128]{2,1,0:T(8,128)(2,1)S(1)}, bf16[4,128,128]{2,1,0:T(8,128)(2,1)S(1)}) custom-call(bf16[4,256,4096]{2,1,0:T(8,128)(2,1)} %snap_ref.1), custom_call_target="tpu_custom_call" | custom-call | tf_op jit(solution)/shard_map/dft_far/pallas_call | solution.py:113
  1.4 0.0 copy-start.1
  1.4 0.0 copy-start
  1.4 2.1 %dft_far.3 = (bf16[4,128,512]{2,1,0:T(8,128)(2,1)S(1)}, bf16[4,128,512]{2,1,0:T(8,128)(2,1)S(1)}) custom-call(bf16[4,256,4096]{2,1,0:T(8,128)(2,1)} %snap_ref.1, bf16[128,256]{1,0:T(8,128)(2,1)S(1)} %get-tuple-element.19.refs_1_.table_ref), custom_call_target="tpu_custom_call" | custom-call | tf_op jit(solution)/shard_map/dft_far/pallas_call | solution.py:113
  3.5 4.8 %dft_rest.1 = (bf16[4,128,256]{2,1,0:T(8,128)(2,1)S(1)}, bf16[4,128,256]{2,1,0:T(8,128)(2,1)S(1)}, bf16[4,128,128]{2,1,0:T(8,128)(2,1)S(1)}, bf16[4,128,128]{2,1...) custom-call(bf16[128,256]{1,0:T(8,128)(2,1)S(1)} %get-tuple-element.19.refs_1_.table_ref, ...), custom_call_target="tpu_custom_call" | custom-call | flops 1073741824 | bytes 12582912 | tf_op jit(solution)/shard_map/dft_rest/pallas_call | solution.py:141
  8.3 0.6 collective-permute-start
  8.9 2.6 %collective-permute-start.4 = (bf16[4,128,512]{2,1,0:T(8,128)(2,1)S(1)}, bf16[4,128,512]{2,1,0:T(8,128)(2,1)S(1)}, u32[]{:S(2)}, u32[]{:S(2)}) collective-permute-start(bf16[4,128,512]{2,1,0:T(8,128)(2,1)S(1)} %get-tuple-element.26), channel_id=1, source_target_pairs={{0,3},{1,2},{2,1},{3,0},{4,7},{5,6},{6,5},{7,4},{8,11},{9,10},{10,... | collective-permute-start | bytes 1572872 | tf_op jit(solution)/shard_map/ppermute | solution.py:353
  11.4 0.0 collective-permute-start.3
  11.5 2.0 %collective-permute-start.1 = (bf16[4,128,128]{2,1,0:T(8,128)(2,1)S(1)}, bf16[4,128,128]{2,1,0:T(8,128)(2,1)S(1)}, u32[]{:S(2)}, u32[]{:S(2)}) collective-permute-start(bf16[4,128,128]{2,1,0:T(8,128)(2,1)S(1)} %get-tuple-element.24), channel_id=1, source_target_pairs={{0,2},{1,3},{2,0},{3,1},{4,6},{5,7},{6,4},{7,5},{8,10},{9,11},{10,... | collective-permute-start | bytes 393224 | tf_op jit(solution)/shard_map/ppermute | solution.py:353
  13.5 0.0 collective-permute-start.2
  13.5 24.8 %collective-permute-done.1.refs_4_ = bf16[4,128,128]{2,1,0:T(8,128)(2,1)S(1)} collective-permute-done((bf16[4,128,128]{2,1,0:T(8,128)(2,1)S(1)}, bf16[4,128,128]{2,1,0:T(8,128)(2,1)S(1)}, u32[]{:S(2)}, u32[]{:S(2)}) %collective-permute-start.1) | collective-permute-done | bytes 131104 | tf_op jit(solution)/shard_map/ppermute | solution.py:353
  38.2 2.1 %collective-permute-start.5 = (bf16[4,128,256]{2,1,0:T(8,128)(2,1)S(1)}, bf16[4,128,256]{2,1,0:T(8,128)(2,1)S(1)}, u32[]{:S(2)}, u32[]{:S(2)}) collective-permute-start(bf16[4,128,256]{2,1,0:T(8,128)(2,1)S(1)} %get-tuple-element.27), channel_id=1, source_target_pairs={{0,2},{1,3},{2,0},{3,1},{4,6},{5,7},{6,4},{7,5},{8,10},{9,11},{10,... | collective-permute-start | bytes 786440 | tf_op jit(solution)/shard_map/ppermute | solution.py:353
  40.3 0.3 collective-permute-done.2.refs_5_
  40.6 1.9 %collective-permute-start.6 = (bf16[4,128,256]{2,1,0:T(8,128)(2,1)S(1)}, bf16[4,128,256]{2,1,0:T(8,128)(2,1)S(1)}, u32[]{:S(2)}, u32[]{:S(2)}) collective-permute-start(bf16[4,128,256]{2,1,0:T(8,128)(2,1)S(1)} %get-tuple-element.28), channel_id=1, source_target_pairs={{0,3},{1,2},{2,1},{3,0},{4,7},{5,6},{6,5},{7,4},{8,11},{9,10},{10,... | collective-permute-start | bytes 786440 | tf_op jit(solution)/shard_map/ppermute | solution.py:353
  42.5 0.0 collective-permute-done.4.refs_6_
  42.5 0.0 collective-permute-start.7
  42.5 0.0 collective-permute-done.refs_2_.refs_3_.refs_4_
  42.5 0.8 %collective-permute-start.8 = (bf16[4,128,128]{2,1,0:T(8,128)(2,1)S(1)}, bf16[4,128,128]{2,1,0:T(8,128)(2,1)S(1)}, u32[]{:S(2)}, u32[]{:S(2)}) collective-permute-start(bf16[4,128,128]{2,1,0:T(8,128)(2,1)S(1)} %get-tuple-element.31), channel_id=1, source_target_pairs={{0,3},{1,2},{2,1},{3,0},{4,7},{5,6},{6,5},{7,4},{8,11},{9,10},{10,... | collective-permute-start | bytes 393224 | tf_op jit(solution)/shard_map/ppermute | solution.py:353
  43.3 0.0 copy-done.1
  43.3 0.6 prepare.1
  43.9 0.0 copy-done
  43.9 1.2 %triads.4.refs_2_ = f32[16,16,128]{2,1,0:T(8,128)S(1)} custom-call(s32[2,64]{1,0:T(2,128)S(4)} %get-tuple-element.23.refs_0_, f32[1,4096]{1,0:T(1,128)S(1)} %bitcast.2, bf16[4,128,1024]{2,1,0:T(8,128)(2,1)S(1)} %get-tuple-element.21.refs_1_.refs_2_.refs_3_, bf16[4,128,1024]{2,1,0:T(8,128)(2,1)S(1)} %collective-permute-done.refs_2_.refs_3_.refs_4_, ...), custom_call_target="tpu_custom_call" | custom-call | flops 67108864 | bytes 524288 | tf_op jit(solution)/shard_map/triads/pallas_call | solution.py:282
  45.2 0.0 collective-permute-done.3.refs_5_
  45.2 3.6 %triads.5.refs_2_ = f32[16,16,128]{2,1,0:T(8,128)S(1)} custom-call(s32[2,64]{1,0:T(2,128)S(4)} %get-tuple-element.23.refs_0_, f32[1,4096]{1,0:T(1,128)S(1)} %bitcast.3, f32[16,16,128]{2,1,0:T(8,128)S(1)} %triads.4.refs_2_, bf16[4,128,1024]{2,1,0:T(8,128)(2,1)S(1)} %get-tuple-element.21.refs_1_.refs_2_.refs_3_, ...), custom_call_target="tpu_custom_call" | custom-call | flops 268435456 | bytes 2097152 | tf_op jit(solution)/shard_map/triads/pallas_call | solution.py:282
  48.8 0.0 collective-permute-done.5.refs_5_
  48.8 3.8 %collective-permute-done.6.refs_6_ = bf16[4,128,256]{2,1,0:T(8,128)(2,1)S(1)} collective-permute-done((bf16[4,128,256]{2,1,0:T(8,128)(2,1)S(1)}, bf16[4,128,256]{2,1,0:T(8,128)(2,1)S(1)}, u32[]{:S(2)}, u32[]{:S(2)}) %collective-permute-start.6) | collective-permute-done | bytes 262176 | tf_op jit(solution)/shard_map/ppermute | solution.py:353
  52.6 2.1 %triads.6.refs_2_ = f32[16,16,128]{2,1,0:T(8,128)S(1)} custom-call(s32[2,64]{1,0:T(2,128)S(4)} %get-tuple-element.23.refs_0_, f32[1,4096]{1,0:T(1,128)S(1)} %bitcast.4, f32[16,16,128]{2,1,0:T(8,128)S(1)} %triads.5.refs_2_, bf16[4,128,1024]{2,1,0:T(8,128)(2,1)S(1)} %get-tuple-element.21.refs_1_.refs_2_.refs_3_, ...), custom_call_target="tpu_custom_call" | custom-call | flops 134217728 | bytes 1048576 | tf_op jit(solution)/shard_map/triads/pallas_call | solution.py:282
  54.7 1.2 %collective-permute-done.7.refs_4_ = bf16[4,128,128]{2,1,0:T(8,128)(2,1)S(1)} collective-permute-done((bf16[4,128,128]{2,1,0:T(8,128)(2,1)S(1)}, bf16[4,128,128]{2,1,0:T(8,128)(2,1)S(1)}, u32[]{:S(2)}, u32[]{:S(2)}) %collective-permute-start.7) | collective-permute-done | bytes 131104 | tf_op jit(solution)/shard_map/ppermute | solution.py:353
  55.9 1.0 %collective-permute-done.8.refs_5_ = bf16[4,128,128]{2,1,0:T(8,128)(2,1)S(1)} collective-permute-done((bf16[4,128,128]{2,1,0:T(8,128)(2,1)S(1)}, bf16[4,128,128]{2,1,0:T(8,128)(2,1)S(1)}, u32[]{:S(2)}, u32[]{:S(2)}) %collective-permute-start.8) | collective-permute-done | bytes 131104 | tf_op jit(solution)/shard_map/ppermute | solution.py:353
  56.9 0.6 triads.7
  57.5 13.0 %all_to_all.5.part_ref = bf16[16,16,128]{2,1,0:T(8,128)(2,1)S(1)} all-to-all(bf16[16,16,128]{2,1,0:T(8,128)(2,1)S(1)} %get-tuple-element.32), channel_id=1, replica_groups=mesh['groups'=2,'space'=4,'freq'=2,'band'=2] {'space','freq','band'}, dimensions={0} | all-to-all | bytes 131072 | tf_op jit(solution)/shard_map/all_to_all | solution.py:390
  70.5 0.8 %finish.1 = f32[4,512]{1,0:T(4,128)} custom-call(bf16[16,16,128]{2,1,0:T(8,128)(2,1)S(1)} %all_to_all.5.part_ref), custom_call_target="tpu_custom_call" | custom-call | tf_op jit(solution)/shard_map/finish/pallas_call | solution.py:323
Async XLA Ops:
  1.4 41.9 %copy-start.1 = (s32[64,2]{0,1:T(2,128)S(1)}, s32[64,2]{0,1:T(2,128)}, u32[]{:S(2)}) copy-start(s32[64,2]{0,1:T(2,128)} %param.5) | copy-start | bytes 1540
  1.4 42.5 %copy-start = (f32[4096]{0:T(1024)S(1)}, f32[4096]{0:T(1024)}, u32[]{:S(2)}) copy-start(f32[4096]{0:T(1024)} %param.4) | copy-start | bytes 49156
  8.3 34.2 %collective-permute-start = (bf16[4,128,1024]{2,1,0:T(8,128)(2,1)S(1)}, bf16[4,128,1024]{2,1,0:T(8,128)(2,1)S(1)}, u32[]{:S(2)}, u32[]{:S(2)}) collective-permute-start(bf16[4,128,1024]{2,1,0:T(8,128)(2,1)S(1)} %get-tuple-element.22), channel_id=1, source_target_pairs={{0,1},{1,0},{2,3},{3,2},{4,5},{5,4},{6,7},{7,6},{8,9},{9,8},{10,11... | collective-permute-start | bytes 3145736 | tf_op jit(solution)/shard_map/ppermute | solution.py:353
  8.9 33.7 %collective-permute-start.4 = (bf16[4,128,512]{2,1,0:T(8,128)(2,1)S(1)}, bf16[4,128,512]{2,1,0:T(8,128)(2,1)S(1)}, u32[]{:S(2)}, u32[]{:S(2)}) collective-permute-start(bf16[4,128,512]{2,1,0:T(8,128)(2,1)S(1)} %get-tuple-element.26), channel_id=1, source_target_pairs={{0,3},{1,2},{2,1},{3,0},{4,7},{5,6},{6,5},{7,4},{8,11},{9,10},{10,... | collective-permute-start | bytes 1572872 | tf_op jit(solution)/shard_map/ppermute | solution.py:353
  11.4 33.7 %collective-permute-start.3 = (bf16[4,128,512]{2,1,0:T(8,128)(2,1)S(1)}, bf16[4,128,512]{2,1,0:T(8,128)(2,1)S(1)}, u32[]{:S(2)}, u32[]{:S(2)}) collective-permute-start(bf16[4,128,512]{2,1,0:T(8,128)(2,1)S(1)} %get-tuple-element.20.after_ref), channel_id=1, source_target_pairs={{0,2},{1,3},{2,0},{3,1},{4,6},{5,7},{6,4},{7,5},{8,10},{9,11},{10,... | collective-permute-start | bytes 1572872 | tf_op jit(solution)/shard_map/ppermute | solution.py:353
  11.5 26.7 %collective-permute-start.1 = (bf16[4,128,128]{2,1,0:T(8,128)(2,1)S(1)}, bf16[4,128,128]{2,1,0:T(8,128)(2,1)S(1)}, u32[]{:S(2)}, u32[]{:S(2)}) collective-permute-start(bf16[4,128,128]{2,1,0:T(8,128)(2,1)S(1)} %get-tuple-element.24), channel_id=1, source_target_pairs={{0,2},{1,3},{2,0},{3,1},{4,6},{5,7},{6,4},{7,5},{8,10},{9,11},{10,... | collective-permute-start | bytes 393224 | tf_op jit(solution)/shard_map/ppermute | solution.py:353
  13.5 27.1 %collective-permute-start.2 = (bf16[4,128,128]{2,1,0:T(8,128)(2,1)S(1)}, bf16[4,128,128]{2,1,0:T(8,128)(2,1)S(1)}, u32[]{:S(2)}, u32[]{:S(2)}) collective-permute-start(bf16[4,128,128]{2,1,0:T(8,128)(2,1)S(1)} %get-tuple-element.25), channel_id=1, source_target_pairs={{0,3},{1,2},{2,1},{3,0},{4,7},{5,6},{6,5},{7,4},{8,11},{9,10},{10,... | collective-permute-start | bytes 393224 | tf_op jit(solution)/shard_map/ppermute | solution.py:353
  38.2 10.5 %collective-permute-start.5 = (bf16[4,128,256]{2,1,0:T(8,128)(2,1)S(1)}, bf16[4,128,256]{2,1,0:T(8,128)(2,1)S(1)}, u32[]{:S(2)}, u32[]{:S(2)}) collective-permute-start(bf16[4,128,256]{2,1,0:T(8,128)(2,1)S(1)} %get-tuple-element.27), channel_id=1, source_target_pairs={{0,2},{1,3},{2,0},{3,1},{4,6},{5,7},{6,4},{7,5},{8,10},{9,11},{10,... | collective-permute-start | bytes 786440 | tf_op jit(solution)/shard_map/ppermute | solution.py:353
  40.6 12.0 %collective-permute-start.6 = (bf16[4,128,256]{2,1,0:T(8,128)(2,1)S(1)}, bf16[4,128,256]{2,1,0:T(8,128)(2,1)S(1)}, u32[]{:S(2)}, u32[]{:S(2)}) collective-permute-start(bf16[4,128,256]{2,1,0:T(8,128)(2,1)S(1)} %get-tuple-element.28), channel_id=1, source_target_pairs={{0,3},{1,2},{2,1},{3,0},{4,7},{5,6},{6,5},{7,4},{8,11},{9,10},{10,... | collective-permute-start | bytes 786440 | tf_op jit(solution)/shard_map/ppermute | solution.py:353
  42.5 13.3 %collective-permute-start.7 = (bf16[4,128,128]{2,1,0:T(8,128)(2,1)S(1)}, bf16[4,128,128]{2,1,0:T(8,128)(2,1)S(1)}, u32[]{:S(2)}, u32[]{:S(2)}) collective-permute-start(bf16[4,128,128]{2,1,0:T(8,128)(2,1)S(1)} %get-tuple-element.30), channel_id=1, source_target_pairs={{0,2},{1,3},{2,0},{3,1},{4,6},{5,7},{6,4},{7,5},{8,10},{9,11},{10,... | collective-permute-start | bytes 393224 | tf_op jit(solution)/shard_map/ppermute | solution.py:353
  42.5 14.3 %collective-permute-start.8 = (bf16[4,128,128]{2,1,0:T(8,128)(2,1)S(1)}, bf16[4,128,128]{2,1,0:T(8,128)(2,1)S(1)}, u32[]{:S(2)}, u32[]{:S(2)}) collective-permute-start(bf16[4,128,128]{2,1,0:T(8,128)(2,1)S(1)} %get-tuple-element.31), channel_id=1, source_target_pairs={{0,3},{1,2},{2,1},{3,0},{4,7},{5,6},{6,5},{7,4},{8,11},{9,10},{10,... | collective-permute-start | bytes 393224 | tf_op jit(solution)/shard_map/ppermute | solution.py:353

commit v10 on v9

--- a/solution.py
+++ b/solution.py
@@ -357,8 +357,10 @@
 
     near = list(range(bands))
     far = list(range(bands, shards))
-    table, *outs = dft_far(snapshots, None, sizes, far, own_points, 0, widths[0])
-    arrived = [send_all(outs, far)]
+    table, *outs = dft_far(snapshots, None, sizes, far[:1], own_points, 0, widths[0])
+    arrived = [send_all(outs, far[:1])]
+    outs = dft_far(snapshots, table, sizes, far[1:], own_points, 0, widths[0])
+    arrived[0] += send_all(outs, far[1:])
     outs = dft_far(snapshots, table, sizes, far, own_points, offsets[1], widths[1])
     arrived.append(send_all(outs, far))
     plan = [

time: 71.5 us -> 72.1 us (level)
  Pallas kernels: 17.1 us -> 18 us
    pallas_call x2 -> x3, Pallas kernels: 3.45 us -> 4.4 us  [dft_far(): pl.pallas_call(functools.partial(dft_far_kernel, sizes, far, points, offs...]
  transfers between devices with their start and end apart: 9 -> 9, of which waited for: 5 -> 5; matrix products, arithmetic and copies ran while one was open for 0% -> 0% of each run, Pallas kernels for 10% -> 12%
where the time goes in v10:
time: 72.1 us; the launch traced here: 71.8 us
  waiting for transfers between devices  30.7 us (43%)
  Pallas kernels  18 us (25%)
  blocking collectives  13.2 us (18%)
  starting transfers between devices  9.74 us (14%)
    ppermute x9, waiting for transfers between devices, send(): return lax.ppermute(value, ('freq', 'band'), pairs)  30.7 us
    all_to_all x1, blocking collectives, mode_decomposition(): lax.all_to_all(total, axes, split_axis=0, concat_axis=0, tiled=True)  13.2 us
    ppermute x9, starting transfers between devices, send(): return lax.ppermute(value, ('freq', 'band'), pairs)  9.74 us
    pallas_call x4, Pallas kernels, triad_chunk(): pl.pallas_call(functools.partial(triad_kernel, sizes, slots, offset, prep...  7.51 us
    pallas_call x1, Pallas kernels, dft_rest(): pl.pallas_call(functools.partial(dft_rest_kernel, sizes, plan, points), o...  4.8 us
    pallas_call x3, Pallas kernels, dft_far(): pl.pallas_call(functools.partial(dft_far_kernel, sizes, far, points, offs...  4.4 us
  transfers between devices with their start and end apart: 9, of which 5 were waited for; matrix products, arithmetic and copies ran while one was open for 0% of the time, Pallas kernels for 12%

profile of v10, /device:TPU:0, one launch (start us, length us, event | category | flops | bytes accessed | tf_op | source)
XLA Modules:
  0.0 71.8 jit_solution(3583764948124926796)
XLA Ops:
  0.0 1.2 %dft_far.3 = (bf16[128,256]{1,0:T(8,128)(2,1)S(1)}, bf16[4,128,128]{2,1,0:T(8,128)(2,1)S(1)}) custom-call(bf16[4,256,4096]{2,1,0:T(8,128)(2,1)} %refs_0_.5), custom_call_target="tpu_custom_call" | custom-call | tf_op jit(solution)/shard_map/dft_far/pallas_call | solution.py:113
  1.2 2.1 %dft_far.4 = (bf16[4,128,512]{2,1,0:T(8,128)(2,1)S(1)}, bf16[4,128,512]{2,1,0:T(8,128)(2,1)S(1)}) custom-call(bf16[4,256,4096]{2,1,0:T(8,128)(2,1)} %refs_0_.5, bf16[128,256]{1,0:T(8,128)(2,1)S(1)} %get-tuple-element.18.refs_1_.table_ref), custom_call_target="tpu_custom_call" | custom-call | tf_op jit(solution)/shard_map/dft_far/pallas_call | solution.py:113
  3.3 0.0 copy-start.1
  3.3 0.0 copy-start
  3.3 4.8 %dft_rest.1 = (bf16[4,128,256]{2,1,0:T(8,128)(2,1)S(1)}, bf16[4,128,256]{2,1,0:T(8,128)(2,1)S(1)}, bf16[4,128,128]{2,1,0:T(8,128)(2,1)S(1)}, bf16[4,128,128]{2,1...) custom-call(bf16[128,256]{1,0:T(8,128)(2,1)S(1)} %get-tuple-element.18.refs_1_.table_ref, ...), custom_call_target="tpu_custom_call" | custom-call | flops 1073741824 | bytes 12582912 | tf_op jit(solution)/shard_map/dft_rest/pallas_call | solution.py:141
  8.1 0.6 collective-permute-start
  8.6 2.6 %collective-permute-start.4 = (bf16[4,128,512]{2,1,0:T(8,128)(2,1)S(1)}, bf16[4,128,512]{2,1,0:T(8,128)(2,1)S(1)}, u32[]{:S(2)}, u32[]{:S(2)}) collective-permute-start(bf16[4,128,512]{2,1,0:T(8,128)(2,1)S(1)} %get-tuple-element.24), channel_id=1, source_target_pairs={{0,3},{1,2},{2,1},{3,0},{4,7},{5,6},{6,5},{7,4},{8,11},{9,10},{10,... | collective-permute-start | bytes 1572872 | tf_op jit(solution)/shard_map/ppermute | solution.py:353
  11.2 0.0 collective-permute-start.3
  11.3 1.2 %dft_far.5 = bf16[4,128,128]{2,1,0:T(8,128)(2,1)S(1)} custom-call(bf16[4,256,4096]{2,1,0:T(8,128)(2,1)} %refs_0_.5, bf16[128,256]{1,0:T(8,128)(2,1)S(1)} %get-tuple-element.18.refs_1_.table_ref), custom_call_target="tpu_custom_call" | custom-call | tf_op jit(solution)/shard_map/dft_far/pallas_call | solution.py:113
  12.4 1.4 %collective-permute-start.2 = (bf16[4,128,128]{2,1,0:T(8,128)(2,1)S(1)}, bf16[4,128,128]{2,1,0:T(8,128)(2,1)S(1)}, u32[]{:S(2)}, u32[]{:S(2)}) collective-permute-start(bf16[4,128,128]{2,1,0:T(8,128)(2,1)S(1)} %dft_far.5), channel_id=1, source_target_pairs={{0,3},{1,2},{2,1},{3,0},{4,7},{5,6},{6,5},{7,4},{8,11},{9,10},{10,... | collective-permute-start | bytes 393224 | tf_op jit(solution)/shard_map/ppermute | solution.py:353
  13.9 0.7 collective-permute-start.1
  14.6 23.0 %collective-permute-done.2.refs_5_ = bf16[4,128,128]{2,1,0:T(8,128)(2,1)S(1)} collective-permute-done((bf16[4,128,128]{2,1,0:T(8,128)(2,1)S(1)}, bf16[4,128,128]{2,1,0:T(8,128)(2,1)S(1)}, u32[]{:S(2)}, u32[]{:S(2)}) %collective-permute-start.2) | collective-permute-done | bytes 131104 | tf_op jit(solution)/shard_map/ppermute | solution.py:353
  37.6 1.3 %collective-permute-start.5 = (bf16[4,128,256]{2,1,0:T(8,128)(2,1)S(1)}, bf16[4,128,256]{2,1,0:T(8,128)(2,1)S(1)}, u32[]{:S(2)}, u32[]{:S(2)}) collective-permute-start(bf16[4,128,256]{2,1,0:T(8,128)(2,1)S(1)} %get-tuple-element.25), channel_id=1, source_target_pairs={{0,2},{1,3},{2,0},{3,1},{4,6},{5,7},{6,4},{7,5},{8,10},{9,11},{10,... | collective-permute-start | bytes 786440 | tf_op jit(solution)/shard_map/ppermute | solution.py:353
  38.8 1.7 %collective-permute-done.1.refs_4_ = bf16[4,128,128]{2,1,0:T(8,128)(2,1)S(1)} collective-permute-done((bf16[4,128,128]{2,1,0:T(8,128)(2,1)S(1)}, bf16[4,128,128]{2,1,0:T(8,128)(2,1)S(1)}, u32[]{:S(2)}, u32[]{:S(2)}) %collective-permute-start.1) | collective-permute-done | bytes 131104 | tf_op jit(solution)/shard_map/ppermute | solution.py:353
  40.6 0.8 %collective-permute-start.6 = (bf16[4,128,256]{2,1,0:T(8,128)(2,1)S(1)}, bf16[4,128,256]{2,1,0:T(8,128)(2,1)S(1)}, u32[]{:S(2)}, u32[]{:S(2)}) collective-permute-start(bf16[4,128,256]{2,1,0:T(8,128)(2,1)S(1)} %get-tuple-element.26), channel_id=1, source_target_pairs={{0,3},{1,2},{2,1},{3,0},{4,7},{5,6},{6,5},{7,4},{8,11},{9,10},{10,... | collective-permute-start | bytes 786440 | tf_op jit(solution)/shard_map/ppermute | solution.py:353
  41.4 0.0 collective-permute-done.4.refs_6_
  41.4 0.9 %collective-permute-start.7 = (bf16[4,128,128]{2,1,0:T(8,128)(2,1)S(1)}, bf16[4,128,128]{2,1,0:T(8,128)(2,1)S(1)}, u32[]{:S(2)}, u32[]{:S(2)}) collective-permute-start(bf16[4,128,128]{2,1,0:T(8,128)(2,1)S(1)} %get-tuple-element.28), channel_id=1, source_target_pairs={{0,2},{1,3},{2,0},{3,1},{4,6},{5,7},{6,4},{7,5},{8,10},{9,11},{10,... | collective-permute-start | bytes 393224 | tf_op jit(solution)/shard_map/ppermute | solution.py:353
  42.3 0.0 collective-permute-done.refs_2_.refs_3_.refs_4_
  42.3 1.5 %collective-permute-start.8 = (bf16[4,128,128]{2,1,0:T(8,128)(2,1)S(1)}, bf16[4,128,128]{2,1,0:T(8,128)(2,1)S(1)}, u32[]{:S(2)}, u32[]{:S(2)}) collective-permute-start(bf16[4,128,128]{2,1,0:T(8,128)(2,1)S(1)} %get-tuple-element.29), channel_id=1, source_target_pairs={{0,3},{1,2},{2,1},{3,0},{4,7},{5,6},{6,5},{7,4},{8,11},{9,10},{10,... | collective-permute-start | bytes 393224 | tf_op jit(solution)/shard_map/ppermute | solution.py:353
  43.7 0.0 copy-done.1
  43.7 0.6 prepare.1
  44.3 0.0 copy-done
  44.3 1.2 %triads.4.refs_2_ = f32[16,16,128]{2,1,0:T(8,128)S(1)} custom-call(s32[2,64]{1,0:T(2,128)S(4)} %get-tuple-element.22.refs_0_, f32[1,4096]{1,0:T(1,128)S(1)} %bitcast.2, bf16[4,128,1024]{2,1,0:T(8,128)(2,1)S(1)} %get-tuple-element.20.refs_1_.refs_2_.refs_3_, bf16[4,128,1024]{2,1,0:T(8,128)(2,1)S(1)} %collective-permute-done.refs_2_.refs_3_.refs_4_, ...), custom_call_target="tpu_custom_call" | custom-call | flops 67108864 | bytes 524288 | tf_op jit(solution)/shard_map/triads/pallas_call | solution.py:282
  45.6 0.0 collective-permute-done.3.refs_5_
  45.6 3.6 %triads.5.refs_2_ = f32[16,16,128]{2,1,0:T(8,128)S(1)} custom-call(s32[2,64]{1,0:T(2,128)S(4)} %get-tuple-element.22.refs_0_, f32[1,4096]{1,0:T(1,128)S(1)} %bitcast.3, f32[16,16,128]{2,1,0:T(8,128)S(1)} %triads.4.refs_2_, bf16[4,128,1024]{2,1,0:T(8,128)(2,1)S(1)} %get-tuple-element.20.refs_1_.refs_2_.refs_3_, ...), custom_call_target="tpu_custom_call" | custom-call | flops 268435456 | bytes 2097152 | tf_op jit(solution)/shard_map/triads/pallas_call | solution.py:282
  49.2 0.0 collective-permute-done.5.refs_5_
  49.2 2.4 %collective-permute-done.6.refs_6_ = bf16[4,128,256]{2,1,0:T(8,128)(2,1)S(1)} collective-permute-done((bf16[4,128,256]{2,1,0:T(8,128)(2,1)S(1)}, bf16[4,128,256]{2,1,0:T(8,128)(2,1)S(1)}, u32[]{:S(2)}, u32[]{:S(2)}) %collective-permute-start.6) | collective-permute-done | bytes 262176 | tf_op jit(solution)/shard_map/ppermute | solution.py:353
  51.6 2.1 %triads.6.refs_2_ = f32[16,16,128]{2,1,0:T(8,128)S(1)} custom-call(s32[2,64]{1,0:T(2,128)S(4)} %get-tuple-element.22.refs_0_, f32[1,4096]{1,0:T(1,128)S(1)} %bitcast.4, f32[16,16,128]{2,1,0:T(8,128)S(1)} %triads.5.refs_2_, bf16[4,128,1024]{2,1,0:T(8,128)(2,1)S(1)} %get-tuple-element.20.refs_1_.refs_2_.refs_3_, ...), custom_call_target="tpu_custom_call" | custom-call | flops 134217728 | bytes 1048576 | tf_op jit(solution)/shard_map/triads/pallas_call | solution.py:282
  53.6 1.5 %collective-permute-done.7.refs_4_ = bf16[4,128,128]{2,1,0:T(8,128)(2,1)S(1)} collective-permute-done((bf16[4,128,128]{2,1,0:T(8,128)(2,1)S(1)}, bf16[4,128,128]{2,1,0:T(8,128)(2,1)S(1)}, u32[]{:S(2)}, u32[]{:S(2)}) %collective-permute-start.7) | collective-permute-done | bytes 131104 | tf_op jit(solution)/shard_map/ppermute | solution.py:353
  55.2 2.0 %collective-permute-done.8.refs_5_ = bf16[4,128,128]{2,1,0:T(8,128)(2,1)S(1)} collective-permute-done((bf16[4,128,128]{2,1,0:T(8,128)(2,1)S(1)}, bf16[4,128,128]{2,1,0:T(8,128)(2,1)S(1)}, u32[]{:S(2)}, u32[]{:S(2)}) %collective-permute-start.8) | collective-permute-done | bytes 131104 | tf_op jit(solution)/shard_map/ppermute | solution.py:353
  57.2 0.6 triads.7
  57.8 13.2 %all_to_all.5.part_ref = bf16[16,16,128]{2,1,0:T(8,128)(2,1)S(1)} all-to-all(bf16[16,16,128]{2,1,0:T(8,128)(2,1)S(1)} %get-tuple-element.30), channel_id=1, replica_groups=mesh['groups'=2,'space'=4,'freq'=2,'band'=2] {'space','freq','band'}, dimensions={0} | all-to-all | bytes 131072 | tf_op jit(solution)/shard_map/all_to_all | solution.py:392
  71.0 0.8 %finish.1 = f32[4,512]{1,0:T(4,128)} custom-call(bf16[16,16,128]{2,1,0:T(8,128)(2,1)S(1)} %all_to_all.5.part_ref), custom_call_target="tpu_custom_call" | custom-call | tf_op jit(solution)/shard_map/finish/pallas_call | solution.py:323
Async XLA Ops:
  3.3 40.5 %copy-start.1 = (s32[64,2]{0,1:T(2,128)S(1)}, s32[64,2]{0,1:T(2,128)}, u32[]{:S(2)}) copy-start(s32[64,2]{0,1:T(2,128)} %param.5) | copy-start | bytes 1540
  3.3 41.1 %copy-start = (f32[4096]{0:T(1024)S(1)}, f32[4096]{0:T(1024)}, u32[]{:S(2)}) copy-start(f32[4096]{0:T(1024)} %param.4) | copy-start | bytes 49156
  8.1 34.2 %collective-permute-start = (bf16[4,128,1024]{2,1,0:T(8,128)(2,1)S(1)}, bf16[4,128,1024]{2,1,0:T(8,128)(2,1)S(1)}, u32[]{:S(2)}, u32[]{:S(2)}) collective-permute-start(bf16[4,128,1024]{2,1,0:T(8,128)(2,1)S(1)} %get-tuple-element.21), channel_id=1, source_target_pairs={{0,1},{1,0},{2,3},{3,2},{4,5},{5,4},{6,7},{7,6},{8,9},{9,8},{10,11... | collective-permute-start | bytes 3145736 | tf_op jit(solution)/shard_map/ppermute | solution.py:353
  8.6 32.7 %collective-permute-start.4 = (bf16[4,128,512]{2,1,0:T(8,128)(2,1)S(1)}, bf16[4,128,512]{2,1,0:T(8,128)(2,1)S(1)}, u32[]{:S(2)}, u32[]{:S(2)}) collective-permute-start(bf16[4,128,512]{2,1,0:T(8,128)(2,1)S(1)} %get-tuple-element.24), channel_id=1, source_target_pairs={{0,3},{1,2},{2,1},{3,0},{4,7},{5,6},{6,5},{7,4},{8,11},{9,10},{10,... | collective-permute-start | bytes 1572872 | tf_op jit(solution)/shard_map/ppermute | solution.py:353
  11.2 34.3 %collective-permute-start.3 = (bf16[4,128,512]{2,1,0:T(8,128)(2,1)S(1)}, bf16[4,128,512]{2,1,0:T(8,128)(2,1)S(1)}, u32[]{:S(2)}, u32[]{:S(2)}) collective-permute-start(bf16[4,128,512]{2,1,0:T(8,128)(2,1)S(1)} %get-tuple-element.19.after_ref), channel_id=1, source_target_pairs={{0,2},{1,3},{2,0},{3,1},{4,6},{5,7},{6,4},{7,5},{8,10},{9,11},{10,... | collective-permute-start | bytes 1572872 | tf_op jit(solution)/shard_map/ppermute | solution.py:353
  12.4 25.1 %collective-permute-start.2 = (bf16[4,128,128]{2,1,0:T(8,128)(2,1)S(1)}, bf16[4,128,128]{2,1,0:T(8,128)(2,1)S(1)}, u32[]{:S(2)}, u32[]{:S(2)}) collective-permute-start(bf16[4,128,128]{2,1,0:T(8,128)(2,1)S(1)} %dft_far.5), channel_id=1, source_target_pairs={{0,3},{1,2},{2,1},{3,0},{4,7},{5,6},{6,5},{7,4},{8,11},{9,10},{10,... | collective-permute-start | bytes 393224 | tf_op jit(solution)/shard_map/ppermute | solution.py:353
  13.9 26.7 %collective-permute-start.1 = (bf16[4,128,128]{2,1,0:T(8,128)(2,1)S(1)}, bf16[4,128,128]{2,1,0:T(8,128)(2,1)S(1)}, u32[]{:S(2)}, u32[]{:S(2)}) collective-permute-start(bf16[4,128,128]{2,1,0:T(8,128)(2,1)S(1)} %get-tuple-element.23), channel_id=1, source_target_pairs={{0,2},{1,3},{2,0},{3,1},{4,6},{5,7},{6,4},{7,5},{8,10},{9,11},{10,... | collective-permute-start | bytes 393224 | tf_op jit(solution)/shard_map/ppermute | solution.py:353
  37.6 11.6 %collective-permute-start.5 = (bf16[4,128,256]{2,1,0:T(8,128)(2,1)S(1)}, bf16[4,128,256]{2,1,0:T(8,128)(2,1)S(1)}, u32[]{:S(2)}, u32[]{:S(2)}) collective-permute-start(bf16[4,128,256]{2,1,0:T(8,128)(2,1)S(1)} %get-tuple-element.25), channel_id=1, source_target_pairs={{0,2},{1,3},{2,0},{3,1},{4,6},{5,7},{6,4},{7,5},{8,10},{9,11},{10,... | collective-permute-start | bytes 786440 | tf_op jit(solution)/shard_map/ppermute | solution.py:353
  40.6 11.0 %collective-permute-start.6 = (bf16[4,128,256]{2,1,0:T(8,128)(2,1)S(1)}, bf16[4,128,256]{2,1,0:T(8,128)(2,1)S(1)}, u32[]{:S(2)}, u32[]{:S(2)}) collective-permute-start(bf16[4,128,256]{2,1,0:T(8,128)(2,1)S(1)} %get-tuple-element.26), channel_id=1, source_target_pairs={{0,3},{1,2},{2,1},{3,0},{4,7},{5,6},{6,5},{7,4},{8,11},{9,10},{10,... | collective-permute-start | bytes 786440 | tf_op jit(solution)/shard_map/ppermute | solution.py:353
  41.4 13.8 %collective-permute-start.7 = (bf16[4,128,128]{2,1,0:T(8,128)(2,1)S(1)}, bf16[4,128,128]{2,1,0:T(8,128)(2,1)S(1)}, u32[]{:S(2)}, u32[]{:S(2)}) collective-permute-start(bf16[4,128,128]{2,1,0:T(8,128)(2,1)S(1)} %get-tuple-element.28), channel_id=1, source_target_pairs={{0,2},{1,3},{2,0},{3,1},{4,6},{5,7},{6,4},{7,5},{8,10},{9,11},{10,... | collective-permute-start | bytes 393224 | tf_op jit(solution)/shard_map/ppermute | solution.py:353
  42.3 14.9 %collective-permute-start.8 = (bf16[4,128,128]{2,1,0:T(8,128)(2,1)S(1)}, bf16[4,128,128]{2,1,0:T(8,128)(2,1)S(1)}, u32[]{:S(2)}, u32[]{:S(2)}) collective-permute-start(bf16[4,128,128]{2,1,0:T(8,128)(2,1)S(1)} %get-tuple-element.29), channel_id=1, source_target_pairs={{0,3},{1,2},{2,1},{3,0},{4,7},{5,6},{6,5},{7,4},{8,11},{9,10},{10,... | collective-permute-start | bytes 393224 | tf_op jit(solution)/shard_map/ppermute | solution.py:353

commit v11 on v9

--- a/solution.py
+++ b/solution.py
@@ -195,6 +195,23 @@
         compiler_params=pltpu.CompilerParams(vmem_limit_bytes=8 * MIB),
         name="prepare",
     )(ids, *near_sources)
+
+
+def extend_kernel(sizes, slots, *refs):
+    for slot, source in zip(slots, refs[1:-1]):
+        interleave(refs[-1], source, slot, sizes, 0)
+
+
+def extend(spec, sources, sizes, slots):
+    return pl.pallas_call(
+        functools.partial(extend_kernel, sizes, slots),
+        out_shape=pltpu.VMEM(spec.shape, jnp.float32),
+        in_specs=[VMEM] * (1 + len(sources)),
+        out_specs=VMEM,
+        input_output_aliases={0: 0},
+        compiler_params=pltpu.CompilerParams(vmem_limit_bytes=8 * MIB),
+        name="extend",
+    )(spec, *sources)
 
 
 def triad_kernel(sizes, slots, offset, prepared, has_prior, scale, *refs):
@@ -377,8 +394,11 @@
     for chunk, (offset, width) in enumerate(zip(offsets, widths)):
         slots = [(slot, 0) for slot in far]
         sources = arrived[chunk]
-        prepared = ready if chunk == len(widths) - 1 else None
-        if prepared is None:
+        prepared = None
+        if chunk == len(widths) - 1:
+            prepared = extend(ready, sources[:-1], sizes, far[:-1])
+            slots, sources = slots[-1:], sources[-1:]
+        else:
             slots = [(slot, offset) for slot in near] + slots
             sources = near_sources + sources
         total = triad_chunk(

time: 71.5 us -> 72.2 us (level)
  no operation moved by 1% of the time
where the time goes in v11:
time: 72.2 us; the launch traced here: 71.9 us
  waiting for transfers between devices  31.3 us (43%)
  Pallas kernels  17.1 us (24%)
  blocking collectives  13.2 us (18%)
  starting transfers between devices  10.2 us (14%)
    ppermute x9, waiting for transfers between devices, send(): return lax.ppermute(value, ('freq', 'band'), pairs)  31.3 us
    all_to_all x1, blocking collectives, mode_decomposition(): lax.all_to_all(total, axes, split_axis=0, concat_axis=0, tiled=True)  13.2 us
    ppermute x9, starting transfers between devices, send(): return lax.ppermute(value, ('freq', 'band'), pairs)  10.2 us
    pallas_call x4, Pallas kernels, triad_chunk(): pl.pallas_call(functools.partial(triad_kernel, sizes, slots, offset, prep...  7.43 us
    pallas_call x1, Pallas kernels, dft_rest(): pl.pallas_call(functools.partial(dft_rest_kernel, sizes, plan, points), o...  4.8 us
    pallas_call x2, Pallas kernels, dft_far(): pl.pallas_call(functools.partial(dft_far_kernel, sizes, far, points, offs...  3.45 us
  transfers between devices with their start and end apart: 9, of which 5 were waited for; matrix products, arithmetic and copies ran while one was open for 0% of the time, Pallas kernels for 10%

profile of v11, /device:TPU:0, one launch (start us, length us, event | category | flops | bytes accessed | tf_op | source)
XLA Modules:
  0.0 71.9 jit_solution(7899744567447335068)
XLA Ops:
  0.0 1.4 %dft_far.2 = (bf16[128,256]{1,0:T(8,128)(2,1)S(1)}, bf16[4,128,128]{2,1,0:T(8,128)(2,1)S(1)}, bf16[4,128,128]{2,1,0:T(8,128)(2,1)S(1)}) custom-call(bf16[4,256,4096]{2,1,0:T(8,128)(2,1)} %snap_ref.1), custom_call_target="tpu_custom_call" | custom-call | tf_op jit(solution)/shard_map/dft_far/pallas_call | solution.py:113
  1.4 0.0 copy-start.1
  1.4 2.1 %dft_far.3 = (bf16[4,128,512]{2,1,0:T(8,128)(2,1)S(1)}, bf16[4,128,512]{2,1,0:T(8,128)(2,1)S(1)}) custom-call(bf16[4,256,4096]{2,1,0:T(8,128)(2,1)} %snap_ref.1, bf16[128,256]{1,0:T(8,128)(2,1)S(1)} %get-tuple-element.19.refs_1_.table_ref), custom_call_target="tpu_custom_call" | custom-call | tf_op jit(solution)/shard_map/dft_far/pallas_call | solution.py:113
  3.5 0.0 copy-start
  3.5 4.8 %dft_rest.1 = (bf16[4,128,256]{2,1,0:T(8,128)(2,1)S(1)}, bf16[4,128,256]{2,1,0:T(8,128)(2,1)S(1)}, bf16[4,128,128]{2,1,0:T(8,128)(2,1)S(1)}, bf16[4,128,128]{2,1...) custom-call(bf16[128,256]{1,0:T(8,128)(2,1)S(1)} %get-tuple-element.19.refs_1_.table_ref, ...), custom_call_target="tpu_custom_call" | custom-call | flops 1073741824 | bytes 12582912 | tf_op jit(solution)/shard_map/dft_rest/pallas_call | solution.py:141
  8.3 0.6 collective-permute-start
  8.8 2.6 %collective-permute-start.4 = (bf16[4,128,512]{2,1,0:T(8,128)(2,1)S(1)}, bf16[4,128,512]{2,1,0:T(8,128)(2,1)S(1)}, u32[]{:S(2)}, u32[]{:S(2)}) collective-permute-start(bf16[4,128,512]{2,1,0:T(8,128)(2,1)S(1)} %get-tuple-element.26), channel_id=1, source_target_pairs={{0,3},{1,2},{2,1},{3,0},{4,7},{5,6},{6,5},{7,4},{8,11},{9,10},{10,... | collective-permute-start | bytes 1572872 | tf_op jit(solution)/shard_map/ppermute | solution.py:370
  11.4 0.0 collective-permute-start.3
  11.5 2.0 %collective-permute-start.1 = (bf16[4,128,128]{2,1,0:T(8,128)(2,1)S(1)}, bf16[4,128,128]{2,1,0:T(8,128)(2,1)S(1)}, u32[]{:S(2)}, u32[]{:S(2)}) collective-permute-start(bf16[4,128,128]{2,1,0:T(8,128)(2,1)S(1)} %get-tuple-element.24), channel_id=1, source_target_pairs={{0,2},{1,3},{2,0},{3,1},{4,6},{5,7},{6,4},{7,5},{8,10},{9,11},{10,... | collective-permute-start | bytes 393224 | tf_op jit(solution)/shard_map/ppermute | solution.py:370
  13.5 0.0 collective-permute-start.2
  13.5 24.8 %collective-permute-done.1.refs_4_ = bf16[4,128,128]{2,1,0:T(8,128)(2,1)S(1)} collective-permute-done((bf16[4,128,128]{2,1,0:T(8,128)(2,1)S(1)}, bf16[4,128,128]{2,1,0:T(8,128)(2,1)S(1)}, u32[]{:S(2)}, u32[]{:S(2)}) %collective-permute-start.1) | collective-permute-done | bytes 131104 | tf_op jit(solution)/shard_map/ppermute | solution.py:370
  38.2 2.1 %collective-permute-start.7 = (bf16[4,128,128]{2,1,0:T(8,128)(2,1)S(1)}, bf16[4,128,128]{2,1,0:T(8,128)(2,1)S(1)}, u32[]{:S(2)}, u32[]{:S(2)}) collective-permute-start(bf16[4,128,128]{2,1,0:T(8,128)(2,1)S(1)} %get-tuple-element.30), channel_id=1, source_target_pairs={{0,2},{1,3},{2,0},{3,1},{4,6},{5,7},{6,4},{7,5},{8,10},{9,11},{10,... | collective-permute-start | bytes 393224 | tf_op jit(solution)/shard_map/ppermute | solution.py:370
  40.3 0.3 collective-permute-done.2.refs_5_
  40.6 1.3 %collective-permute-start.5 = (bf16[4,128,256]{2,1,0:T(8,128)(2,1)S(1)}, bf16[4,128,256]{2,1,0:T(8,128)(2,1)S(1)}, u32[]{:S(2)}, u32[]{:S(2)}) collective-permute-start(bf16[4,128,256]{2,1,0:T(8,128)(2,1)S(1)} %get-tuple-element.27), channel_id=1, source_target_pairs={{0,2},{1,3},{2,0},{3,1},{4,6},{5,7},{6,4},{7,5},{8,10},{9,11},{10,... | collective-permute-start | bytes 786440 | tf_op jit(solution)/shard_map/ppermute | solution.py:370
  41.9 1.7 %collective-permute-done.7.refs_1_ = bf16[4,128,128]{2,1,0:T(8,128)(2,1)S(1)} collective-permute-done((bf16[4,128,128]{2,1,0:T(8,128)(2,1)S(1)}, bf16[4,128,128]{2,1,0:T(8,128)(2,1)S(1)}, u32[]{:S(2)}, u32[]{:S(2)}) %collective-permute-start.7) | collective-permute-done | bytes 131104 | tf_op jit(solution)/shard_map/ppermute | solution.py:370
  43.6 0.1 collective-permute-start.6
  43.6 0.0 collective-permute-done.refs_2_.refs_3_.refs_4_
  43.6 1.7 %collective-permute-start.8 = (bf16[4,128,128]{2,1,0:T(8,128)(2,1)S(1)}, bf16[4,128,128]{2,1,0:T(8,128)(2,1)S(1)}, u32[]{:S(2)}, u32[]{:S(2)}) collective-permute-start(bf16[4,128,128]{2,1,0:T(8,128)(2,1)S(1)} %get-tuple-element.31), channel_id=1, source_target_pairs={{0,3},{1,2},{2,1},{3,0},{4,7},{5,6},{6,5},{7,4},{8,11},{9,10},{10,... | collective-permute-start | bytes 393224 | tf_op jit(solution)/shard_map/ppermute | solution.py:370
  45.3 0.0 copy-done.1
  45.3 0.6 prepare.1
  45.9 0.1 extend.1.refs_3_
  46.0 0.0 copy-done
  46.0 1.2 %triads.4.refs_2_ = f32[16,16,128]{2,1,0:T(8,128)S(1)} custom-call(s32[2,64]{1,0:T(2,128)S(4)} %get-tuple-element.23.refs_0_, f32[1,4096]{1,0:T(1,128)S(1)} %bitcast.2, bf16[4,128,1024]{2,1,0:T(8,128)(2,1)S(1)} %get-tuple-element.21.refs_1_.refs_2_.refs_3_, bf16[4,128,1024]{2,1,0:T(8,128)(2,1)S(1)} %collective-permute-done.refs_2_.refs_3_.refs_4_, ...), custom_call_target="tpu_custom_call" | custom-call | flops 67108864 | bytes 524288 | tf_op jit(solution)/shard_map/triads/pallas_call | solution.py:299
  47.2 0.0 collective-permute-done.4.refs_6_
  47.2 0.0 collective-permute-done.3.refs_5_
  47.3 3.6 %triads.5.refs_2_ = f32[16,16,128]{2,1,0:T(8,128)S(1)} custom-call(s32[2,64]{1,0:T(2,128)S(4)} %get-tuple-element.23.refs_0_, f32[1,4096]{1,0:T(1,128)S(1)} %bitcast.3, f32[16,16,128]{2,1,0:T(8,128)S(1)} %triads.4.refs_2_, bf16[4,128,1024]{2,1,0:T(8,128)(2,1)S(1)} %get-tuple-element.21.refs_1_.refs_2_.refs_3_, ...), custom_call_target="tpu_custom_call" | custom-call | flops 268435456 | bytes 2097152 | tf_op jit(solution)/shard_map/triads/pallas_call | solution.py:299
  50.9 0.0 collective-permute-done.5.refs_5_
  50.9 3.7 %collective-permute-done.6.refs_6_ = bf16[4,128,256]{2,1,0:T(8,128)(2,1)S(1)} collective-permute-done((bf16[4,128,256]{2,1,0:T(8,128)(2,1)S(1)}, bf16[4,128,256]{2,1,0:T(8,128)(2,1)S(1)}, u32[]{:S(2)}, u32[]{:S(2)}) %collective-permute-start.6) | collective-permute-done | bytes 262176 | tf_op jit(solution)/shard_map/ppermute | solution.py:370
  54.6 2.1 %triads.6.refs_2_ = f32[16,16,128]{2,1,0:T(8,128)S(1)} custom-call(s32[2,64]{1,0:T(2,128)S(4)} %get-tuple-element.23.refs_0_, f32[1,4096]{1,0:T(1,128)S(1)} %bitcast.4, f32[16,16,128]{2,1,0:T(8,128)S(1)} %triads.5.refs_2_, bf16[4,128,1024]{2,1,0:T(8,128)(2,1)S(1)} %get-tuple-element.21.refs_1_.refs_2_.refs_3_, ...), custom_call_target="tpu_custom_call" | custom-call | flops 134217728 | bytes 1048576 | tf_op jit(solution)/shard_map/triads/pallas_call | solution.py:299
  56.7 0.7 %collective-permute-done.8.refs_4_ = bf16[4,128,128]{2,1,0:T(8,128)(2,1)S(1)} collective-permute-done((bf16[4,128,128]{2,1,0:T(8,128)(2,1)S(1)}, bf16[4,128,128]{2,1,0:T(8,128)(2,1)S(1)}, u32[]{:S(2)}, u32[]{:S(2)}) %collective-permute-start.8) | collective-permute-done | bytes 131104 | tf_op jit(solution)/shard_map/ppermute | solution.py:370
  57.4 0.6 triads.7
  58.0 13.2 %all_to_all.5.part_ref = bf16[16,16,128]{2,1,0:T(8,128)(2,1)S(1)} all-to-all(bf16[16,16,128]{2,1,0:T(8,128)(2,1)S(1)} %get-tuple-element.32), channel_id=1, replica_groups=mesh['groups'=2,'space'=4,'freq'=2,'band'=2] {'space','freq','band'}, dimensions={0} | all-to-all | bytes 131072 | tf_op jit(solution)/shard_map/all_to_all | solution.py:410
  71.2 0.8 %finish.1 = f32[4,512]{1,0:T(4,128)} custom-call(bf16[16,16,128]{2,1,0:T(8,128)(2,1)S(1)} %all_to_all.5.part_ref), custom_call_target="tpu_custom_call" | custom-call | tf_op jit(solution)/shard_map/finish/pallas_call | solution.py:340
Async XLA Ops:
  1.4 43.9 %copy-start.1 = (s32[64,2]{0,1:T(2,128)S(1)}, s32[64,2]{0,1:T(2,128)}, u32[]{:S(2)}) copy-start(s32[64,2]{0,1:T(2,128)} %param.5) | copy-start | bytes 1540
  3.5 42.5 %copy-start = (f32[4096]{0:T(1024)S(1)}, f32[4096]{0:T(1024)}, u32[]{:S(2)}) copy-start(f32[4096]{0:T(1024)} %param.4) | copy-start | bytes 49156
  8.3 35.3 %collective-permute-start = (bf16[4,128,1024]{2,1,0:T(8,128)(2,1)S(1)}, bf16[4,128,1024]{2,1,0:T(8,128)(2,1)S(1)}, u32[]{:S(2)}, u32[]{:S(2)}) collective-permute-start(bf16[4,128,1024]{2,1,0:T(8,128)(2,1)S(1)} %get-tuple-element.22), channel_id=1, source_target_pairs={{0,1},{1,0},{2,3},{3,2},{4,5},{5,4},{6,7},{7,6},{8,9},{9,8},{10,11... | collective-permute-start | bytes 3145736 | tf_op jit(solution)/shard_map/ppermute | solution.py:370
  8.8 38.4 %collective-permute-start.4 = (bf16[4,128,512]{2,1,0:T(8,128)(2,1)S(1)}, bf16[4,128,512]{2,1,0:T(8,128)(2,1)S(1)}, u32[]{:S(2)}, u32[]{:S(2)}) collective-permute-start(bf16[4,128,512]{2,1,0:T(8,128)(2,1)S(1)} %get-tuple-element.26), channel_id=1, source_target_pairs={{0,3},{1,2},{2,1},{3,0},{4,7},{5,6},{6,5},{7,4},{8,11},{9,10},{10,... | collective-permute-start | bytes 1572872 | tf_op jit(solution)/shard_map/ppermute | solution.py:370
  11.4 35.8 %collective-permute-start.3 = (bf16[4,128,512]{2,1,0:T(8,128)(2,1)S(1)}, bf16[4,128,512]{2,1,0:T(8,128)(2,1)S(1)}, u32[]{:S(2)}, u32[]{:S(2)}) collective-permute-start(bf16[4,128,512]{2,1,0:T(8,128)(2,1)S(1)} %get-tuple-element.20.after_ref), channel_id=1, source_target_pairs={{0,2},{1,3},{2,0},{3,1},{4,6},{5,7},{6,4},{7,5},{8,10},{9,11},{10,... | collective-permute-start | bytes 1572872 | tf_op jit(solution)/shard_map/ppermute | solution.py:370
  11.5 26.7 %collective-permute-start.1 = (bf16[4,128,128]{2,1,0:T(8,128)(2,1)S(1)}, bf16[4,128,128]{2,1,0:T(8,128)(2,1)S(1)}, u32[]{:S(2)}, u32[]{:S(2)}) collective-permute-start(bf16[4,128,128]{2,1,0:T(8,128)(2,1)S(1)} %get-tuple-element.24), channel_id=1, source_target_pairs={{0,2},{1,3},{2,0},{3,1},{4,6},{5,7},{6,4},{7,5},{8,10},{9,11},{10,... | collective-permute-start | bytes 393224 | tf_op jit(solution)/shard_map/ppermute | solution.py:370
  13.5 27.1 %collective-permute-start.2 = (bf16[4,128,128]{2,1,0:T(8,128)(2,1)S(1)}, bf16[4,128,128]{2,1,0:T(8,128)(2,1)S(1)}, u32[]{:S(2)}, u32[]{:S(2)}) collective-permute-start(bf16[4,128,128]{2,1,0:T(8,128)(2,1)S(1)} %get-tuple-element.25), channel_id=1, source_target_pairs={{0,3},{1,2},{2,1},{3,0},{4,7},{5,6},{6,5},{7,4},{8,11},{9,10},{10,... | collective-permute-start | bytes 393224 | tf_op jit(solution)/shard_map/ppermute | solution.py:370
  38.2 5.4 %collective-permute-start.7 = (bf16[4,128,128]{2,1,0:T(8,128)(2,1)S(1)}, bf16[4,128,128]{2,1,0:T(8,128)(2,1)S(1)}, u32[]{:S(2)}, u32[]{:S(2)}) collective-permute-start(bf16[4,128,128]{2,1,0:T(8,128)(2,1)S(1)} %get-tuple-element.30), channel_id=1, source_target_pairs={{0,2},{1,3},{2,0},{3,1},{4,6},{5,7},{6,4},{7,5},{8,10},{9,11},{10,... | collective-permute-start | bytes 393224 | tf_op jit(solution)/shard_map/ppermute | solution.py:370
  40.6 10.3 %collective-permute-start.5 = (bf16[4,128,256]{2,1,0:T(8,128)(2,1)S(1)}, bf16[4,128,256]{2,1,0:T(8,128)(2,1)S(1)}, u32[]{:S(2)}, u32[]{:S(2)}) collective-permute-start(bf16[4,128,256]{2,1,0:T(8,128)(2,1)S(1)} %get-tuple-element.27), channel_id=1, source_target_pairs={{0,2},{1,3},{2,0},{3,1},{4,6},{5,7},{6,4},{7,5},{8,10},{9,11},{10,... | collective-permute-start | bytes 786440 | tf_op jit(solution)/shard_map/ppermute | solution.py:370
  43.6 11.0 %collective-permute-start.6 = (bf16[4,128,256]{2,1,0:T(8,128)(2,1)S(1)}, bf16[4,128,256]{2,1,0:T(8,128)(2,1)S(1)}, u32[]{:S(2)}, u32[]{:S(2)}) collective-permute-start(bf16[4,128,256]{2,1,0:T(8,128)(2,1)S(1)} %get-tuple-element.28), channel_id=1, source_target_pairs={{0,3},{1,2},{2,1},{3,0},{4,7},{5,6},{6,5},{7,4},{8,11},{9,10},{10,... | collective-permute-start | bytes 786440 | tf_op jit(solution)/shard_map/ppermute | solution.py:370
  43.6 13.7 %collective-permute-start.8 = (bf16[4,128,128]{2,1,0:T(8,128)(2,1)S(1)}, bf16[4,128,128]{2,1,0:T(8,128)(2,1)S(1)}, u32[]{:S(2)}, u32[]{:S(2)}) collective-permute-start(bf16[4,128,128]{2,1,0:T(8,128)(2,1)S(1)} %get-tuple-element.31), channel_id=1, source_target_pairs={{0,3},{1,2},{2,1},{3,0},{4,7},{5,6},{6,5},{7,4},{8,11},{9,10},{10,... | collective-permute-start | bytes 393224 | tf_op jit(solution)/shard_map/ppermute | solution.py:370

commit v12 on v11

--- a/solution.py
+++ b/solution.py
@@ -198,20 +198,20 @@
 
 
 def extend_kernel(sizes, slots, *refs):
-    for slot, source in zip(slots, refs[1:-1]):
+    for slot, source in zip(slots, refs[2:-1]):
         interleave(refs[-1], source, slot, sizes, 0)
 
 
-def extend(spec, sources, sizes, slots):
+def extend(spec, after, sources, sizes, slots):
     return pl.pallas_call(
         functools.partial(extend_kernel, sizes, slots),
         out_shape=pltpu.VMEM(spec.shape, jnp.float32),
-        in_specs=[VMEM] * (1 + len(sources)),
+        in_specs=[VMEM, ANY] + [VMEM] * len(sources),
         out_specs=VMEM,
         input_output_aliases={0: 0},
         compiler_params=pltpu.CompilerParams(vmem_limit_bytes=8 * MIB),
         name="extend",
-    )(spec, *sources)
+    )(spec, after, *sources)
 
 
 def triad_kernel(sizes, slots, offset, prepared, has_prior, scale, *refs):
@@ -396,7 +396,7 @@
         sources = arrived[chunk]
         prepared = None
         if chunk == len(widths) - 1:
-            prepared = extend(ready, sources[:-1], sizes, far[:-1])
+            prepared = extend(ready, total, sources[:-1], sizes, far[:-1])
             slots, sources = slots[-1:], sources[-1:]
         else:
             slots = [(slot, offset) for slot in near] + slots

time: 72.2 us -> 71.5 us (level)
  transfers between devices with their start and end apart: 9 -> 9, of which waited for: 5 -> 5; matrix products, arithmetic and copies ran while one was open for 0% -> 0% of each run, Pallas kernels for 10% -> 11%
where the time goes in v12:
time: 71.5 us; the launch traced here: 71.2 us
  waiting for transfers between devices  31 us (43%)
  Pallas kernels  17.1 us (24%)
  blocking collectives  13 us (18%)
  starting transfers between devices  9.96 us (14%)
    ppermute x9, waiting for transfers between devices, send(): return lax.ppermute(value, ('freq', 'band'), pairs)  31 us
    all_to_all x1, blocking collectives, mode_decomposition(): lax.all_to_all(total, axes, split_axis=0, concat_axis=0, tiled=True)  13 us
    ppermute x9, starting transfers between devices, send(): return lax.ppermute(value, ('freq', 'band'), pairs)  9.96 us
    pallas_call x4, Pallas kernels, triad_chunk(): pl.pallas_call(functools.partial(triad_kernel, sizes, slots, offset, prep...  7.43 us
    pallas_call x1, Pallas kernels, dft_rest(): pl.pallas_call(functools.partial(dft_rest_kernel, sizes, plan, points), o...  4.8 us
    pallas_call x2, Pallas kernels, dft_far(): pl.pallas_call(functools.partial(dft_far_kernel, sizes, far, points, offs...  3.45 us
  transfers between devices with their start and end apart: 9, of which 5 were waited for; matrix products, arithmetic and copies ran while one was open for 0% of the time, Pallas kernels for 11%

profile of v12, /device:TPU:0, one launch (start us, length us, event | category | flops | bytes accessed | tf_op | source)
XLA Modules:
  0.0 71.2 jit_solution(10734261841796740097)
XLA Ops:
  0.0 1.4 %dft_far.2 = (bf16[128,256]{1,0:T(8,128)(2,1)S(1)}, bf16[4,128,128]{2,1,0:T(8,128)(2,1)S(1)}, bf16[4,128,128]{2,1,0:T(8,128)(2,1)S(1)}) custom-call(bf16[4,256,4096]{2,1,0:T(8,128)(2,1)} %snap_ref.1), custom_call_target="tpu_custom_call" | custom-call | tf_op jit(solution)/shard_map/dft_far/pallas_call | solution.py:113
  1.4 0.0 copy-start.1
  1.4 0.0 copy-start
  1.4 2.1 %dft_far.3 = (bf16[4,128,512]{2,1,0:T(8,128)(2,1)S(1)}, bf16[4,128,512]{2,1,0:T(8,128)(2,1)S(1)}) custom-call(bf16[4,256,4096]{2,1,0:T(8,128)(2,1)} %snap_ref.1, bf16[128,256]{1,0:T(8,128)(2,1)S(1)} %get-tuple-element.19.refs_1_.table_ref), custom_call_target="tpu_custom_call" | custom-call | tf_op jit(solution)/shard_map/dft_far/pallas_call | solution.py:113
  3.5 4.8 %dft_rest.1 = (bf16[4,128,256]{2,1,0:T(8,128)(2,1)S(1)}, bf16[4,128,256]{2,1,0:T(8,128)(2,1)S(1)}, bf16[4,128,128]{2,1,0:T(8,128)(2,1)S(1)}, bf16[4,128,128]{2,1...) custom-call(bf16[128,256]{1,0:T(8,128)(2,1)S(1)} %get-tuple-element.19.refs_1_.table_ref, ...), custom_call_target="tpu_custom_call" | custom-call | flops 1073741824 | bytes 12582912 | tf_op jit(solution)/shard_map/dft_rest/pallas_call | solution.py:141
  8.3 0.6 collective-permute-start
  8.9 2.6 %collective-permute-start.4 = (bf16[4,128,512]{2,1,0:T(8,128)(2,1)S(1)}, bf16[4,128,512]{2,1,0:T(8,128)(2,1)S(1)}, u32[]{:S(2)}, u32[]{:S(2)}) collective-permute-start(bf16[4,128,512]{2,1,0:T(8,128)(2,1)S(1)} %get-tuple-element.26), channel_id=1, source_target_pairs={{0,3},{1,2},{2,1},{3,0},{4,7},{5,6},{6,5},{7,4},{8,11},{9,10},{10,... | collective-permute-start | bytes 1572872 | tf_op jit(solution)/shard_map/ppermute | solution.py:370
  11.4 0.0 collective-permute-start.3
  11.5 2.0 %collective-permute-start.1 = (bf16[4,128,128]{2,1,0:T(8,128)(2,1)S(1)}, bf16[4,128,128]{2,1,0:T(8,128)(2,1)S(1)}, u32[]{:S(2)}, u32[]{:S(2)}) collective-permute-start(bf16[4,128,128]{2,1,0:T(8,128)(2,1)S(1)} %get-tuple-element.24), channel_id=1, source_target_pairs={{0,2},{1,3},{2,0},{3,1},{4,6},{5,7},{6,4},{7,5},{8,10},{9,11},{10,... | collective-permute-start | bytes 393224 | tf_op jit(solution)/shard_map/ppermute | solution.py:370
  13.5 0.0 collective-permute-start.2
  13.5 24.8 %collective-permute-done.1.refs_4_ = bf16[4,128,128]{2,1,0:T(8,128)(2,1)S(1)} collective-permute-done((bf16[4,128,128]{2,1,0:T(8,128)(2,1)S(1)}, bf16[4,128,128]{2,1,0:T(8,128)(2,1)S(1)}, u32[]{:S(2)}, u32[]{:S(2)}) %collective-permute-start.1) | collective-permute-done | bytes 131104 | tf_op jit(solution)/shard_map/ppermute | solution.py:370
  38.2 2.1 %collective-permute-start.5 = (bf16[4,128,256]{2,1,0:T(8,128)(2,1)S(1)}, bf16[4,128,256]{2,1,0:T(8,128)(2,1)S(1)}, u32[]{:S(2)}, u32[]{:S(2)}) collective-permute-start(bf16[4,128,256]{2,1,0:T(8,128)(2,1)S(1)} %get-tuple-element.27), channel_id=1, source_target_pairs={{0,2},{1,3},{2,0},{3,1},{4,6},{5,7},{6,4},{7,5},{8,10},{9,11},{10,... | collective-permute-start | bytes 786440 | tf_op jit(solution)/shard_map/ppermute | solution.py:370
  40.3 0.3 collective-permute-done.2.refs_5_
  40.6 1.9 %collective-permute-start.6 = (bf16[4,128,256]{2,1,0:T(8,128)(2,1)S(1)}, bf16[4,128,256]{2,1,0:T(8,128)(2,1)S(1)}, u32[]{:S(2)}, u32[]{:S(2)}) collective-permute-start(bf16[4,128,256]{2,1,0:T(8,128)(2,1)S(1)} %get-tuple-element.28), channel_id=1, source_target_pairs={{0,3},{1,2},{2,1},{3,0},{4,7},{5,6},{6,5},{7,4},{8,11},{9,10},{10,... | collective-permute-start | bytes 786440 | tf_op jit(solution)/shard_map/ppermute | solution.py:370
  42.5 0.0 collective-permute-done.4.refs_6_
  42.5 0.0 collective-permute-start.7
  42.5 0.0 collective-permute-done.refs_2_.refs_3_.refs_4_
  42.5 0.8 %collective-permute-start.8 = (bf16[4,128,128]{2,1,0:T(8,128)(2,1)S(1)}, bf16[4,128,128]{2,1,0:T(8,128)(2,1)S(1)}, u32[]{:S(2)}, u32[]{:S(2)}) collective-permute-start(bf16[4,128,128]{2,1,0:T(8,128)(2,1)S(1)} %get-tuple-element.31), channel_id=1, source_target_pairs={{0,3},{1,2},{2,1},{3,0},{4,7},{5,6},{6,5},{7,4},{8,11},{9,10},{10,... | collective-permute-start | bytes 393224 | tf_op jit(solution)/shard_map/ppermute | solution.py:370
  43.3 0.0 copy-done.1
  43.3 0.6 prepare.1
  43.9 0.0 copy-done
  43.9 1.2 %triads.4.refs_2_ = f32[16,16,128]{2,1,0:T(8,128)S(1)} custom-call(s32[2,64]{1,0:T(2,128)S(4)} %get-tuple-element.23.refs_0_, f32[1,4096]{1,0:T(1,128)S(1)} %bitcast.2, bf16[4,128,1024]{2,1,0:T(8,128)(2,1)S(1)} %get-tuple-element.21.refs_1_.refs_2_.refs_3_, bf16[4,128,1024]{2,1,0:T(8,128)(2,1)S(1)} %collective-permute-done.refs_2_.refs_3_.refs_4_, ...), custom_call_target="tpu_custom_call" | custom-call | flops 67108864 | bytes 524288 | tf_op jit(solution)/shard_map/triads/pallas_call | solution.py:299
  45.2 0.0 collective-permute-done.3.refs_5_
  45.2 3.6 %triads.5.refs_2_ = f32[16,16,128]{2,1,0:T(8,128)S(1)} custom-call(s32[2,64]{1,0:T(2,128)S(4)} %get-tuple-element.23.refs_0_, f32[1,4096]{1,0:T(1,128)S(1)} %bitcast.3, f32[16,16,128]{2,1,0:T(8,128)S(1)} %triads.4.refs_2_, bf16[4,128,1024]{2,1,0:T(8,128)(2,1)S(1)} %get-tuple-element.21.refs_1_.refs_2_.refs_3_, ...), custom_call_target="tpu_custom_call" | custom-call | flops 268435456 | bytes 2097152 | tf_op jit(solution)/shard_map/triads/pallas_call | solution.py:299
  48.8 0.0 collective-permute-done.5.refs_5_
  48.8 3.8 %collective-permute-done.6.refs_6_ = bf16[4,128,256]{2,1,0:T(8,128)(2,1)S(1)} collective-permute-done((bf16[4,128,256]{2,1,0:T(8,128)(2,1)S(1)}, bf16[4,128,256]{2,1,0:T(8,128)(2,1)S(1)}, u32[]{:S(2)}, u32[]{:S(2)}) %collective-permute-start.6) | collective-permute-done | bytes 262176 | tf_op jit(solution)/shard_map/ppermute | solution.py:370
  52.6 2.1 %triads.6.refs_1_.refs_2_ = f32[16,16,128]{2,1,0:T(8,128)S(1)} custom-call(s32[2,64]{1,0:T(2,128)S(4)} %get-tuple-element.23.refs_0_, f32[1,4096]{1,0:T(1,128)S(1)} %bitcast.4, f32[16,16,128]{2,1,0:T(8,128)S(1)} %triads.5.refs_2_, bf16[4,128,1024]{2,1,0:T(8,128)(2,1)S(1)} %get-tuple-element.21.refs_1_.refs_2_.refs_3_, ...), custom_call_target="tpu_custom_call" | custom-call | flops 134217728 | bytes 1048576 | tf_op jit(solution)/shard_map/triads/pallas_call | solution.py:299
  54.7 1.2 %collective-permute-done.7.refs_2_ = bf16[4,128,128]{2,1,0:T(8,128)(2,1)S(1)} collective-permute-done((bf16[4,128,128]{2,1,0:T(8,128)(2,1)S(1)}, bf16[4,128,128]{2,1,0:T(8,128)(2,1)S(1)}, u32[]{:S(2)}, u32[]{:S(2)}) %collective-permute-start.7) | collective-permute-done | bytes 131104 | tf_op jit(solution)/shard_map/ppermute | solution.py:370
  55.9 0.1 extend.1.refs_3_
  55.9 0.9 %collective-permute-done.8.refs_4_ = bf16[4,128,128]{2,1,0:T(8,128)(2,1)S(1)} collective-permute-done((bf16[4,128,128]{2,1,0:T(8,128)(2,1)S(1)}, bf16[4,128,128]{2,1,0:T(8,128)(2,1)S(1)}, u32[]{:S(2)}, u32[]{:S(2)}) %collective-permute-start.8) | collective-permute-done | bytes 131104 | tf_op jit(solution)/shard_map/ppermute | solution.py:370
  56.9 0.6 triads.7
  57.4 13.0 %all_to_all.5.part_ref = bf16[16,16,128]{2,1,0:T(8,128)(2,1)S(1)} all-to-all(bf16[16,16,128]{2,1,0:T(8,128)(2,1)S(1)} %get-tuple-element.32), channel_id=1, replica_groups=mesh['groups'=2,'space'=4,'freq'=2,'band'=2] {'space','freq','band'}, dimensions={0} | all-to-all | bytes 131072 | tf_op jit(solution)/shard_map/all_to_all | solution.py:410
  70.4 0.8 %finish.1 = f32[4,512]{1,0:T(4,128)} custom-call(bf16[16,16,128]{2,1,0:T(8,128)(2,1)S(1)} %all_to_all.5.part_ref), custom_call_target="tpu_custom_call" | custom-call | tf_op jit(solution)/shard_map/finish/pallas_call | solution.py:340
Async XLA Ops:
  1.4 41.9 %copy-start.1 = (s32[64,2]{0,1:T(2,128)S(1)}, s32[64,2]{0,1:T(2,128)}, u32[]{:S(2)}) copy-start(s32[64,2]{0,1:T(2,128)} %param.5) | copy-start | bytes 1540
  1.4 42.5 %copy-start = (f32[4096]{0:T(1024)S(1)}, f32[4096]{0:T(1024)}, u32[]{:S(2)}) copy-start(f32[4096]{0:T(1024)} %param.4) | copy-start | bytes 49156
  8.3 34.2 %collective-permute-start = (bf16[4,128,1024]{2,1,0:T(8,128)(2,1)S(1)}, bf16[4,128,1024]{2,1,0:T(8,128)(2,1)S(1)}, u32[]{:S(2)}, u32[]{:S(2)}) collective-permute-start(bf16[4,128,1024]{2,1,0:T(8,128)(2,1)S(1)} %get-tuple-element.22), channel_id=1, source_target_pairs={{0,1},{1,0},{2,3},{3,2},{4,5},{5,4},{6,7},{7,6},{8,9},{9,8},{10,11... | collective-permute-start | bytes 3145736 | tf_op jit(solution)/shard_map/ppermute | solution.py:370
  8.9 33.7 %collective-permute-start.4 = (bf16[4,128,512]{2,1,0:T(8,128)(2,1)S(1)}, bf16[4,128,512]{2,1,0:T(8,128)(2,1)S(1)}, u32[]{:S(2)}, u32[]{:S(2)}) collective-permute-start(bf16[4,128,512]{2,1,0:T(8,128)(2,1)S(1)} %get-tuple-element.26), channel_id=1, source_target_pairs={{0,3},{1,2},{2,1},{3,0},{4,7},{5,6},{6,5},{7,4},{8,11},{9,10},{10,... | collective-permute-start | bytes 1572872 | tf_op jit(solution)/shard_map/ppermute | solution.py:370
  11.4 33.7 %collective-permute-start.3 = (bf16[4,128,512]{2,1,0:T(8,128)(2,1)S(1)}, bf16[4,128,512]{2,1,0:T(8,128)(2,1)S(1)}, u32[]{:S(2)}, u32[]{:S(2)}) collective-permute-start(bf16[4,128,512]{2,1,0:T(8,128)(2,1)S(1)} %get-tuple-element.20.after_ref), channel_id=1, source_target_pairs={{0,2},{1,3},{2,0},{3,1},{4,6},{5,7},{6,4},{7,5},{8,10},{9,11},{10,... | collective-permute-start | bytes 1572872 | tf_op jit(solution)/shard_map/ppermute | solution.py:370
  11.5 26.7 %collective-permute-start.1 = (bf16[4,128,128]{2,1,0:T(8,128)(2,1)S(1)}, bf16[4,128,128]{2,1,0:T(8,128)(2,1)S(1)}, u32[]{:S(2)}, u32[]{:S(2)}) collective-permute-start(bf16[4,128,128]{2,1,0:T(8,128)(2,1)S(1)} %get-tuple-element.24), channel_id=1, source_target_pairs={{0,2},{1,3},{2,0},{3,1},{4,6},{5,7},{6,4},{7,5},{8,10},{9,11},{10,... | collective-permute-start | bytes 393224 | tf_op jit(solution)/shard_map/ppermute | solution.py:370
  13.5 27.1 %collective-permute-start.2 = (bf16[4,128,128]{2,1,0:T(8,128)(2,1)S(1)}, bf16[4,128,128]{2,1,0:T(8,128)(2,1)S(1)}, u32[]{:S(2)}, u32[]{:S(2)}) collective-permute-start(bf16[4,128,128]{2,1,0:T(8,128)(2,1)S(1)} %get-tuple-element.25), channel_id=1, source_target_pairs={{0,3},{1,2},{2,1},{3,0},{4,7},{5,6},{6,5},{7,4},{8,11},{9,10},{10,... | collective-permute-start | bytes 393224 | tf_op jit(solution)/shard_map/ppermute | solution.py:370
  38.2 10.5 %collective-permute-start.5 = (bf16[4,128,256]{2,1,0:T(8,128)(2,1)S(1)}, bf16[4,128,256]{2,1,0:T(8,128)(2,1)S(1)}, u32[]{:S(2)}, u32[]{:S(2)}) collective-permute-start(bf16[4,128,256]{2,1,0:T(8,128)(2,1)S(1)} %get-tuple-element.27), channel_id=1, source_target_pairs={{0,2},{1,3},{2,0},{3,1},{4,6},{5,7},{6,4},{7,5},{8,10},{9,11},{10,... | collective-permute-start | bytes 786440 | tf_op jit(solution)/shard_map/ppermute | solution.py:370
  40.6 12.0 %collective-permute-start.6 = (bf16[4,128,256]{2,1,0:T(8,128)(2,1)S(1)}, bf16[4,128,256]{2,1,0:T(8,128)(2,1)S(1)}, u32[]{:S(2)}, u32[]{:S(2)}) collective-permute-start(bf16[4,128,256]{2,1,0:T(8,128)(2,1)S(1)} %get-tuple-element.28), channel_id=1, source_target_pairs={{0,3},{1,2},{2,1},{3,0},{4,7},{5,6},{6,5},{7,4},{8,11},{9,10},{10,... | collective-permute-start | bytes 786440 | tf_op jit(solution)/shard_map/ppermute | solution.py:370
  42.5 13.3 %collective-permute-start.7 = (bf16[4,128,128]{2,1,0:T(8,128)(2,1)S(1)}, bf16[4,128,128]{2,1,0:T(8,128)(2,1)S(1)}, u32[]{:S(2)}, u32[]{:S(2)}) collective-permute-start(bf16[4,128,128]{2,1,0:T(8,128)(2,1)S(1)} %get-tuple-element.30), channel_id=1, source_target_pairs={{0,2},{1,3},{2,0},{3,1},{4,6},{5,7},{6,4},{7,5},{8,10},{9,11},{10,... | collective-permute-start | bytes 393224 | tf_op jit(solution)/shard_map/ppermute | solution.py:370
  42.5 14.3 %collective-permute-start.8 = (bf16[4,128,128]{2,1,0:T(8,128)(2,1)S(1)}, bf16[4,128,128]{2,1,0:T(8,128)(2,1)S(1)}, u32[]{:S(2)}, u32[]{:S(2)}) collective-permute-start(bf16[4,128,128]{2,1,0:T(8,128)(2,1)S(1)} %get-tuple-element.31), channel_id=1, source_target_pairs={{0,3},{1,2},{2,1},{3,0},{4,7},{5,6},{6,5},{7,4},{8,11},{9,10},{10,... | collective-permute-start | bytes 393224 | tf_op jit(solution)/shard_map/ppermute | solution.py:370
